TPU v7x, 32 devices: a whole 2x2x4 slice. The times are simulated.
32 devices in a mesh: mem: 4 (over x, core), tile: 8 (over z, y).
Axes of the slice: x: 2, y: 2, z: 4, core: 2. Of those that a mesh axis runs over, the one named last changes fastest.
Arguments:
- increment: float32 [70, 128, 256], P(None, 'tile')
- previous: float32 [70, 128, 256], P(None, 'tile'), may hold values from -6 to 6
- beta_prev: float32 [1], replicated, may hold values from 0.5 to 1.5
- members: bfloat16 [8, 70, 128, 256], P('mem', None, 'tile'), may hold values from -6 to 6
- band_widths: int32 [70], replicated, may hold values from 1 to 8, as said below
- diffusion_steps: int32 [8], replicated, may hold values from 1 to 4, as said below
Outputs:
- next_vector: float32 [70, 128, 256], P(None, 'tile')
- coefficients: float32 [2], replicated
Inputs may be any that keep to these rules, and one draw needn't show every extreme that they name: `band_widths`: every level's band width lies in the range and some level has exactly 8. `diffusion_steps`: every tile's iteration count lies in the range and some tile has exactly 4.
All inputs are finite; a program needn't handle non-finite values.
Results may differ from a plain program's by a relative error of at most 0.0003.
Values sent between devices are 32-bit elements; how exact they have to be, the bound alone decides.
No kernel may reach another device: no remote copies, remote signals or barrier semaphores. Data moves between devices by JAX's collectives and lax.ppermute only.
A program may use at most 64 MiB of HBM per device.

v0:
```python
import jax
import jax.numpy as jnp
from jax import lax
from jax.sharding import PartitionSpec as P

MEM_DEV = 2
DIFF = 4


def extended(value, sides, width):
    for axis, dim in sides:
        count, length = (lax.axis_size(axis), value.shape[dim])
        up = [(i, (i + 1) % count) for i in range(count - 1)]
        down = [(j, i) for i, j in up]
        last = lax.slice_in_dim(value, length - width, length, axis=dim)
        leading = lax.slice_in_dim(value, 0, width, axis=dim)
        before = lax.ppermute(last, axis, up)
        after = lax.ppermute(leading, axis, down)
        value = jnp.concatenate([before, value, after], axis=dim)
    return value


def vertical_matrix(band_widths):
    levels = jnp.arange(band_widths.shape[0], dtype=jnp.int32)
    apart = levels[:, None] - levels[None, :]
    band_float = band_widths.astype(jnp.float32)
    limit = jnp.minimum(band_widths[:, None], band_widths[None, :])
    weight = jnp.exp(-apart.astype(jnp.float32) ** 2 / (band_float[:, None] * band_float[None, :]))
    return jnp.where(jnp.abs(apart) <= limit, weight, jnp.float32(0.0))


def lanczos_sums(image_part, incr_part, prev_part, beta_value):
    inc_img, inc_inc = lax.psum(
        (jnp.sum(incr_part * image_part), jnp.sum(incr_part * incr_part)), ("mem", "tile")
    )
    alpha_value = inc_img / inc_inc
    residual = image_part - alpha_value * incr_part - beta_value * prev_part
    squares = lax.psum(jnp.sum(residual * residual), ("mem", "tile"))
    return (alpha_value, squares)


def row_owner_counts(diffusion_steps, first_row, row_total, tile_rows):
    global_rows = first_row + jnp.arange(row_total, dtype=jnp.int32)
    owner = jnp.floor_divide(global_rows, tile_rows)
    tile_ids = jnp.arange(diffusion_steps.shape[0], dtype=jnp.int32)
    matches = (owner[:, None] == tile_ids[None, :]).astype(jnp.int32)
    return jnp.sum(matches * diffusion_steps[None, :], axis=1)


def per_device(increment, previous, beta_prev, members, band_widths, diffusion_steps):
    vertical = vertical_matrix(band_widths)
    tile_rows = increment.shape[1]
    tile_here = lax.axis_index("tile")
    members_f = members.astype(jnp.float32)
    localized = jnp.einsum(
        "ij,mjyx->miyx", vertical, members_f * increment[None], precision=lax.Precision.HIGHEST
    )
    step_count = row_owner_counts(diffusion_steps, tile_here * tile_rows, tile_rows, tile_rows)[
        None, None, :, None
    ]
    for sweep_index in range(DIFF):
        padded = extended(localized, (("tile", 2),), 1)
        sideways = jnp.pad(localized, ((0, 0), (0, 0), (0, 0), (1, 1)))
        laplace = (
            padded[:, :, 2:, :]
            + padded[:, :, :-2, :]
            + sideways[:, :, :, 2:]
            + sideways[:, :, :, :-2]
            - 4.0 * localized
        )
        localized = jnp.where(sweep_index < step_count, localized + 0.24 * laplace, localized)
    partial_value = jnp.sum(members_f * localized, axis=0)
    inverse_count = 1.0 / (MEM_DEV * lax.axis_size("mem") - 1)
    beta_value = beta_prev[0]
    cells_all = increment.shape[0] * increment.shape[1] * lax.axis_size("tile") * increment.shape[2]
    share_width = increment.shape[2] // lax.axis_size("mem")
    offset = lax.axis_index("mem") * share_width
    incr_share = lax.dynamic_slice_in_dim(increment, offset, share_width, 2)
    prev_share = lax.dynamic_slice_in_dim(previous, offset, share_width, 2)
    summed = lax.psum(partial_value, "mem")
    image = increment + summed * inverse_count
    image_share = lax.dynamic_slice_in_dim(image, offset, share_width, 2)
    alpha_value, squares = lanczos_sums(image_share, incr_share, prev_share, beta_value)
    scale_value = jnp.sqrt(squares / cells_all + 1e-06)
    residual = image - alpha_value * increment - beta_value * previous
    next_vector = residual / scale_value
    coefficients = jnp.stack([alpha_value, scale_value])
    return (next_vector, coefficients)


def solution(mesh):
    in_specs = (
        P(None, "tile", None),
        P(None, "tile", None),
        P(),
        P("mem", None, "tile", None),
        P(),
        P(),
    )
    out_specs = (P(None, "tile", None), P())
    return jax.shard_map(
        per_device, mesh=mesh, in_specs=in_specs, out_specs=out_specs, check_vma=False
    )
```

profile of v0, /device:TPU:0, one launch (start us, length us, event | category | flops | bytes accessed | tf_op | source)
XLA Modules:
  0.0 210.4 jit_solution(6761432922234523690)
XLA Ops:
  7.2 2.0 copy.20
  9.9 3.4 %fusion.22 = f32[2,70,16,256]{3,1,2,0:T(8,128)S(1)} fusion(f32[70,16,256]{2,0,1:T(8,128)S(1)} %copy.20, bf16[2,70,16,256]{3,2,1,0:T(8,128)(2,1)S(1)} %copy-done.1, f32[70]{0:T(128)S(1)} %convert_element_type.17, s32[70]{0:T(128)} %param.10), kind=kOutput, calls=%fused_computation.44 | convolution fusion | flops 482885472 | bytes 4588080 | tf_op jit(solution)/shard_map/ij,mjyx->miyx/dot_general | solution.py:55
  13.3 0.7 fusion.45
  14.1 1.3 collective-permute-start
  15.4 6.2 %collective-permute-start.1 = (f32[2,70,1,256]{3,1,2,0:T(8,128)}, f32[2,70,1,256]{3,1,2,0:T(8,128)}, u32[]{:S(2)}, u32[]{:S(2)}) collective-permute-start(f32[2,70,1,256]{3,1,2,0:T(8,128)} %get-tuple-element.17), channel_id=1, source_target_pairs={{0,1},{1,2},{2,3},{3,4},{4,5},{5,6},{6,7},{8,9},{9,10},{10,11},{11... | collective-permute-start | bytes 430088 | tf_op jit(solution)/shard_map/ppermute | solution.py:17
  21.6 1.5 collective-permute-done
  23.1 3.3 %collective-permute-done.1 = f32[2,70,1,256]{3,1,2,0:T(8,128)} collective-permute-done((f32[2,70,1,256]{3,1,2,0:T(8,128)}, f32[2,70,1,256]{3,1,2,0:T(8,128)}, u32[]{:S(2)}, u32[]{:S(2)}) %collective-permute-start.1) | collective-permute-done | bytes 143392 | tf_op jit(solution)/shard_map/ppermute | solution.py:17
  26.4 2.6 %add_select_fusion.3 = f32[2,70,16,256]{3,1,2,0:T(8,128)S(1)} fusion(f32[2,70,16,256]{3,1,2,0:T(8,128)S(1)} %fusion.22, f32[2,70,1,256]{3,1,2,0:T(8,128)} %collective-permute-done.1, f32[2,70,1,256]{3,1,2,0:T(8,128)} %collective-permute-done, pred[16]{0:T(512)(128)(4,1)S(1)} %get-tuple-element.19), kind=kLoop, calls=%fused_computation.11 | loop fusion | flops 5734400 | bytes 4874256 | tf_op jit(solution)/shard_map/jit(_where)/select_n | solution.py:71
  29.1 1.3 collective-permute-start.2
  30.4 5.0 %collective-permute-start.3 = (f32[2,70,1,256]{3,1,2,0:T(8,128)S(1)}, f32[2,70,1,256]{3,1,2,0:T(8,128)S(1)}, u32[]{:S(2)}, u32[]{:S(2)}) collective-permute-start(f32[2,70,1,256]{3,1,2,0:T(8,128)S(1)} %get-tuple-element.15), channel_id=1, source_target_pairs={{0,1},{1,2},{2,3},{3,4},{4,5},{5,6},{6,7},{8,9},{9,10},{10,11},{11... | collective-permute-start | bytes 430088 | tf_op jit(solution)/shard_map/ppermute | solution.py:17
  35.4 2.1 collective-permute-done.2
  37.5 3.3 %collective-permute-done.3 = f32[2,70,1,256]{3,1,2,0:T(8,128)S(1)} collective-permute-done((f32[2,70,1,256]{3,1,2,0:T(8,128)S(1)}, f32[2,70,1,256]{3,1,2,0:T(8,128)S(1)}, u32[]{:S(2)}, u32[]{:S(2)}) %collective-permute-start.3) | collective-permute-done | bytes 143392 | tf_op jit(solution)/shard_map/ppermute | solution.py:17
  40.8 1.8 add_select_fusion.2
  42.6 1.3 collective-permute-start.4
  43.9 5.0 %collective-permute-start.5 = (f32[2,70,1,256]{3,1,2,0:T(8,128)S(1)}, f32[2,70,1,256]{3,1,2,0:T(8,128)S(1)}, u32[]{:S(2)}, u32[]{:S(2)}) collective-permute-start(f32[2,70,1,256]{3,1,2,0:T(8,128)S(1)} %get-tuple-element.13), channel_id=1, source_target_pairs={{0,1},{1,2},{2,3},{3,4},{4,5},{5,6},{6,7},{8,9},{9,10},{10,11},{11... | collective-permute-start | bytes 430088 | tf_op jit(solution)/shard_map/ppermute | solution.py:17
  48.9 2.1 collective-permute-done.4
  51.0 3.3 %collective-permute-done.5 = f32[2,70,1,256]{3,1,2,0:T(8,128)S(1)} collective-permute-done((f32[2,70,1,256]{3,1,2,0:T(8,128)S(1)}, f32[2,70,1,256]{3,1,2,0:T(8,128)S(1)}, u32[]{:S(2)}, u32[]{:S(2)}) %collective-permute-start.5) | collective-permute-done | bytes 143392 | tf_op jit(solution)/shard_map/ppermute | solution.py:17
  54.3 1.7 add_select_fusion.1
  56.1 1.3 collective-permute-start.6
  57.4 5.0 %collective-permute-start.7 = (f32[2,70,1,256]{3,1,2,0:T(8,128)S(1)}, f32[2,70,1,256]{3,1,2,0:T(8,128)S(1)}, u32[]{:S(2)}, u32[]{:S(2)}) collective-permute-start(f32[2,70,1,256]{3,1,2,0:T(8,128)S(1)} %get-tuple-element.11), channel_id=1, source_target_pairs={{0,1},{1,2},{2,3},{3,4},{4,5},{5,6},{6,7},{8,9},{9,10},{10,11},{11... | collective-permute-start | bytes 430088 | tf_op jit(solution)/shard_map/ppermute | solution.py:17
  62.4 2.1 collective-permute-done.6
  64.5 3.3 %collective-permute-done.7 = f32[2,70,1,256]{3,1,2,0:T(8,128)S(1)} collective-permute-done((f32[2,70,1,256]{3,1,2,0:T(8,128)S(1)}, f32[2,70,1,256]{3,1,2,0:T(8,128)S(1)}, u32[]{:S(2)}, u32[]{:S(2)}) %collective-permute-start.7) | collective-permute-done | bytes 143392 | tf_op jit(solution)/shard_map/ppermute | solution.py:17
  67.8 3.8 %fusion.1 = f32[70,16,256]{2,0,1:T(8,128)} fusion(f32[2,70,16,256]{3,1,2,0:T(8,128)S(1)} %add_select_fusion.1, f32[2,70,1,256]{3,1,2,0:T(8,128)S(1)} %collective-permute-done.7, f32[2,70,1,256]{3,1,2,0:T(8,128)S(1)} %collective-permute-done.6, pred[16]{0:T(512)(128)(4,1)S(1)} %get-tuple-element.18, bf16[2,70,16,256]{3,2,1,0:T(8,128)(2,1)S(1)} %copy-done.2), kind=kLoop, calls=%fused_computation.15 | loop fusion | flops 7168000 | bytes 4874256 | tf_op jit(solution)/shard_map/reduce_sum | solution.py:72
  72.4 1.7 copy.23
  74.1 36.2 %all-reduce.7.cloned.1.call-done = f32[70,16,256]{2,0,1:T(8,128)} async-done(((f32[70,16,256]{2,0,1:T(8,128)}), f32[70,16,256]{2,0,1:T(8,128)}) %all-reduce.7.cloned.1.call-update) | async-done | bytes 1146896 | tf_op jit(solution)/shard_map/psum | solution.py:80
  110.4 2.0 multiply_add_fusion
  112.4 1.0 multiply_reduce_fusion.1
  113.3 39.7 %all-reduce.4 = (f32[]{:T(128)}, f32[]{:T(128)}) all-reduce(f32[]{:T(128)} %get-tuple-element.7, f32[]{:T(128)} %get-tuple-element.6), channel_id=1, replica_groups=mesh['mem'=4,'tile'=8] {'mem','tile'}, use_global_device_ids=true, to_apply=%region_4.5 | all-reduce | flops 2 | bytes 16 | tf_op jit(solution)/shard_map/psum | solution.py:33
  154.4 2.2 %multiply_reduce_fusion = f32[]{:T(128)} fusion(f32[70,16,256]{2,0,1:T(8,128)} %copy.23, s32[]{:T(128)S(6)} %select_n.37, f32[70,16,256]{2,0,1:T(8,128)S(1)} %multiply_add_fusion, f32[70,16,256]{2,0,1:T(8,128)S(1)} %copy.20, f32[]{:T(128)} %bitcast.11, f32[]{:T(128)} %div.32), kind=kLoop, calls=%fused_computation.49 | loop fusion | flops 430079 | bytes 860176 | tf_op jit(solution)/shard_map/reduce_sum | solution.py:38
  156.6 41.4 %psum.31 = f32[]{:T(128)} all-reduce(f32[]{:T(128)} %multiply_reduce_fusion), channel_id=1, replica_groups=mesh['mem'=4,'tile'=8] {'mem','tile'}, use_global_device_ids=true, to_apply=%region_8.9 | all-reduce | flops 1 | bytes 8 | tf_op jit(solution)/shard_map/psum | solution.py:38
  198.6 3.0 %subtract_divide_fusion = f32[70,16,256]{2,0,1:T(8,128)S(1)} fusion(f32[]{:T(128)} %sqrt.3, f32[]{:T(128)} %bitcast.10, f32[]{:T(128)} %div.32, f32[70,16,256]{2,1,0:T(8,128)} %param.7, f32[70,16,256]{2,1,0:T(8,128)S(1)} %copy-done, f32[70,16,256]{2,0,1:T(8,128)} %all-reduce.7.cloned.1.call-done), kind=kLoop, calls=%fused_computation.45 | loop fusion | flops 2007040 | bytes 4587532 | tf_op jit(solution)/shard_map/div | solution.py:86
  201.6 1.4 copy.25
  (20 shorter events, 1.5 us)
Async XLA Ops:
  7.2 103.2 %all-reduce.7.cloned.1.call-start = ((), (), s32[]{:S(2)}) async-start(), calls=%async_computation | async-start | bytes 2359296 | tf_op jit(solution)/shard_map/psum | solution.py:80
  7.2 2.7 %copy-start.1 = (bf16[2,70,16,256]{3,2,1,0:T(8,128)(2,1)S(1)}, bf16[2,70,16,256]{3,2,1,0:T(8,128)(2,1)}, u32[]{:S(2)}) copy-start(bf16[2,70,16,256]{3,2,1,0:T(8,128)(2,1)} %param.9) | copy-start | bytes 3440644
  9.9 11.6 %copy-start.4 = (s32[8]{0:T(128)S(1)}, s32[8]{0:T(128)}, u32[]{:S(2)}) copy-start(s32[8]{0:T(128)} %param.11) | copy-start | bytes 100
  14.1 9.0 %collective-permute-start = (f32[2,70,1,256]{3,1,2,0:T(8,128)}, f32[2,70,1,256]{3,1,2,0:T(8,128)}, u32[]{:S(2)}, u32[]{:S(2)}) collective-permute-start(f32[2,70,1,256]{3,1,2,0:T(8,128)} %get-tuple-element.16), channel_id=1, source_target_pairs={{1,0},{2,1},{3,2},{4,3},{5,4},{6,5},{7,6},{9,8},{10,9},{11,10},{12... | collective-permute-start | bytes 430088 | tf_op jit(solution)/shard_map/ppermute | solution.py:18
  15.4 11.0 %collective-permute-start.1 = (f32[2,70,1,256]{3,1,2,0:T(8,128)}, f32[2,70,1,256]{3,1,2,0:T(8,128)}, u32[]{:S(2)}, u32[]{:S(2)}) collective-permute-start(f32[2,70,1,256]{3,1,2,0:T(8,128)} %get-tuple-element.17), channel_id=1, source_target_pairs={{0,1},{1,2},{2,3},{3,4},{4,5},{5,6},{6,7},{8,9},{9,10},{10,11},{11... | collective-permute-start | bytes 430088 | tf_op jit(solution)/shard_map/ppermute | solution.py:17
  29.1 8.4 %collective-permute-start.2 = (f32[2,70,1,256]{3,1,2,0:T(8,128)S(1)}, f32[2,70,1,256]{3,1,2,0:T(8,128)S(1)}, u32[]{:S(2)}, u32[]{:S(2)}) collective-permute-start(f32[2,70,1,256]{3,1,2,0:T(8,128)S(1)} %get-tuple-element.14), channel_id=1, source_target_pairs={{1,0},{2,1},{3,2},{4,3},{5,4},{6,5},{7,6},{9,8},{10,9},{11,10},{12... | collective-permute-start | bytes 430088 | tf_op jit(solution)/shard_map/ppermute | solution.py:18
  30.4 10.4 %collective-permute-start.3 = (f32[2,70,1,256]{3,1,2,0:T(8,128)S(1)}, f32[2,70,1,256]{3,1,2,0:T(8,128)S(1)}, u32[]{:S(2)}, u32[]{:S(2)}) collective-permute-start(f32[2,70,1,256]{3,1,2,0:T(8,128)S(1)} %get-tuple-element.15), channel_id=1, source_target_pairs={{0,1},{1,2},{2,3},{3,4},{4,5},{5,6},{6,7},{8,9},{9,10},{10,11},{11... | collective-permute-start | bytes 430088 | tf_op jit(solution)/shard_map/ppermute | solution.py:17
  42.6 8.4 %collective-permute-start.4 = (f32[2,70,1,256]{3,1,2,0:T(8,128)S(1)}, f32[2,70,1,256]{3,1,2,0:T(8,128)S(1)}, u32[]{:S(2)}, u32[]{:S(2)}) collective-permute-start(f32[2,70,1,256]{3,1,2,0:T(8,128)S(1)} %get-tuple-element.12), channel_id=1, source_target_pairs={{1,0},{2,1},{3,2},{4,3},{5,4},{6,5},{7,6},{9,8},{10,9},{11,10},{12... | collective-permute-start | bytes 430088 | tf_op jit(solution)/shard_map/ppermute | solution.py:18
  43.9 10.4 %collective-permute-start.5 = (f32[2,70,1,256]{3,1,2,0:T(8,128)S(1)}, f32[2,70,1,256]{3,1,2,0:T(8,128)S(1)}, u32[]{:S(2)}, u32[]{:S(2)}) collective-permute-start(f32[2,70,1,256]{3,1,2,0:T(8,128)S(1)} %get-tuple-element.13), channel_id=1, source_target_pairs={{0,1},{1,2},{2,3},{3,4},{4,5},{5,6},{6,7},{8,9},{9,10},{10,11},{11... | collective-permute-start | bytes 430088 | tf_op jit(solution)/shard_map/ppermute | solution.py:17
  54.3 13.5 %copy-start.2 = (bf16[2,70,16,256]{3,2,1,0:T(8,128)(2,1)S(1)}, bf16[2,70,16,256]{3,2,1,0:T(8,128)(2,1)}, u32[]{:S(2)}) copy-start(bf16[2,70,16,256]{3,2,1,0:T(8,128)(2,1)} %param.9) | copy-start | bytes 3440644
  56.1 8.4 %collective-permute-start.6 = (f32[2,70,1,256]{3,1,2,0:T(8,128)S(1)}, f32[2,70,1,256]{3,1,2,0:T(8,128)S(1)}, u32[]{:S(2)}, u32[]{:S(2)}) collective-permute-start(f32[2,70,1,256]{3,1,2,0:T(8,128)S(1)} %get-tuple-element.10), channel_id=1, source_target_pairs={{1,0},{2,1},{3,2},{4,3},{5,4},{6,5},{7,6},{9,8},{10,9},{11,10},{12... | collective-permute-start | bytes 430088 | tf_op jit(solution)/shard_map/ppermute | solution.py:18
  57.4 10.4 %collective-permute-start.7 = (f32[2,70,1,256]{3,1,2,0:T(8,128)S(1)}, f32[2,70,1,256]{3,1,2,0:T(8,128)S(1)}, u32[]{:S(2)}, u32[]{:S(2)}) collective-permute-start(f32[2,70,1,256]{3,1,2,0:T(8,128)S(1)} %get-tuple-element.11), channel_id=1, source_target_pairs={{0,1},{1,2},{2,3},{3,4},{4,5},{5,6},{6,7},{8,9},{9,10},{10,11},{11... | collective-permute-start | bytes 430088 | tf_op jit(solution)/shard_map/ppermute | solution.py:17
  67.8 4.6 %copy-start.3 = (f32[70,16,256]{2,1,0:T(8,128)S(1)}, f32[70,16,256]{2,1,0:T(8,128)}, u32[]{:S(2)}) copy-start(f32[70,16,256]{2,1,0:T(8,128)} %param.7) | copy-start | bytes 3440644
  71.6 38.7 %copy-start = (f32[70,16,256]{2,1,0:T(8,128)S(1)}, f32[70,16,256]{2,1,0:T(8,128)}, u32[]{:S(2)}) copy-start(f32[70,16,256]{2,1,0:T(8,128)} %param.6) | copy-start | bytes 3440644
Sparse Core Ops, SparseCore 0:
  71.8 38.5 all-reduce.6
where the time goes:
time: 211 us; the launch traced here: 210 us
  blocking collectives  81.1 us (38%)
  waiting for transfers between devices  57.2 us (27%)
  starting transfers between devices  26.4 us (13%)
  other arithmetic  19.4 us (9%)
  between operations  16.9 us (8%)
  local copies, waits for them, and re-layouts  5.91 us (3%)
  matrix products  3.43 us (2%)
    psum x1, blocking collectives, lanczos_sums(): squares = lax.psum(jnp.sum(residual * residual), ('mem', 'tile'))  41.4 us
    psum x1, blocking collectives, lanczos_sums(): lax.psum((jnp.sum(incr_part * image_part), jnp.sum(incr_part * incr_part)...  39.7 us
    psum x1, waiting for transfers between devices, per_device(): summed = lax.psum(partial_value, 'mem')  36.2 us
    ppermute x4, starting transfers between devices, extended(): before = lax.ppermute(last, axis, up)  21.2 us
    ppermute x4, waiting for transfers between devices, extended(): before = lax.ppermute(last, axis, up)  13.2 us
    ppermute x4, waiting for transfers between devices, extended(): after = lax.ppermute(leading, axis, down)  7.71 us
    select_n x3, other arithmetic, per_device(): jnp.where(sweep_index < step_count, localized + 0.24 * laplace, localized)  6.11 us
    ppermute x4, starting transfers between devices, extended(): after = lax.ppermute(leading, axis, down)  5.16 us
  transfers between devices with their start and end apart: 9, of which 9 were waited for; matrix products, arithmetic and copies ran while one was open for 1% of the time, Pallas kernels for 0%

commit v1 on v0

v1 whole, which is shorter than its diff:
```python
import functools

import jax
import jax.numpy as jnp
from jax import lax
from jax.experimental import pallas as pl
from jax.experimental.pallas import tpu as pltpu
from jax.sharding import PartitionSpec as P

DIFF = 4
RATE = 0.24
F32 = jnp.float32
VMEM_LIMIT = 48 * 1024 * 1024


def up_to(value, unit):
    return -(-value // unit) * unit


def vmem():
    return pl.BlockSpec(memory_space=pltpu.VMEM)


def smem():
    return pl.BlockSpec(memory_space=pltpu.SMEM)


def grid_row(tile, row, rows):
    return jnp.where(tile % 2 == 0, row, rows - 1 - row)


def put_flat(ref, value):
    for piece in range(ref.shape[0]):
        ref[piece, : value.shape[0], :] = value[:, piece * 128 : (piece + 1) * 128]


def strided(ref, start, count, stride):
    pieces = [ref[piece, pl.ds(start, count, stride=stride), :] for piece in range(ref.shape[0])]
    return jnp.concatenate(pieces, axis=1)


def sweep_counts(steps_ref, tile, tiles):
    even = tile % 2 == 0
    near = jnp.where(even, tile + 1, tile - 1)
    far = jnp.where(even, tile - 1, tile + 1)

    def count(index):
        inside = (index >= 0) & (index < tiles)
        return jnp.where(inside, steps_ref[jnp.clip(index, 0, tiles - 1)], 0)

    return count(tile), count(near), count(far)


def coefficient(sweep, count):
    return jnp.where(sweep < count, F32(RATE), F32(0.0))


def build_vertical(bands_ref, pad_ref, levels):
    pad_ref[...] = jnp.ones(pad_ref.shape, F32)
    pad_ref[0:1, 0:levels] = bands_ref[...].astype(F32)
    across = jnp.broadcast_to(pad_ref[0:1, :], (128, 128))
    down = across.T
    i = lax.broadcasted_iota(jnp.int32, (128, 128), 0)
    j = lax.broadcasted_iota(jnp.int32, (128, 128), 1)
    apart = (i - j).astype(F32)
    weight = jnp.exp(-(apart * apart) / (down * across))
    keep = (jnp.abs(apart) <= jnp.minimum(down, across)) & (i < levels) & (j < levels)
    full = jnp.where(keep, weight, F32(0.0))[: up_to(levels, 8), : up_to(levels, 16)]
    high = full.astype(jnp.bfloat16)
    return high, (full - high.astype(F32)).astype(jnp.bfloat16)


def apply_vertical(vertical, field):
    v_high, v_low = vertical
    high = field.astype(jnp.bfloat16)
    low = (field - high.astype(F32)).astype(jnp.bfloat16)
    dot = functools.partial(jnp.dot, preferred_element_type=F32)
    return dot(v_high, high) + dot(v_high, low) + dot(v_low, high)


def left_of(field):
    lane = lax.broadcasted_iota(jnp.int32, field.shape, field.ndim - 1)
    return jnp.where(lane == 0, F32(0.0), pltpu.roll(field, 1, field.ndim - 1))


def right_of(field):
    width = field.shape[-1]
    lane = lax.broadcasted_iota(jnp.int32, field.shape, field.ndim - 1)
    return jnp.where(lane == width - 1, F32(0.0), pltpu.roll(field, width - 1, field.ndim - 1))


def edge_kernel(rows, levels, bands_ref, members_ref, inc_ref, near_ref, far_ref, prod_ref, pad_ref):
    tile = lax.axis_index("tile")
    vertical = build_vertical(bands_ref, pad_ref, levels)
    deep = up_to(levels, 16)
    total = rows * levels
    width = inc_ref.shape[-1]
    for m in range(members_ref.shape[0]):
        put_flat(prod_ref.at[m], members_ref[m].astype(F32) * inc_ref[...])
        prod_ref[m, :, total:, :] = jnp.zeros((width // 128, prod_ref.shape[2] - total, 128), F32)
    for out_ref, base, sign in ((near_ref, rows - 1, -1), (far_ref, 0, 1)):
        for m in range(members_ref.shape[0]):
            for q in range(DIFF):
                row = grid_row(tile, base + sign * q, rows)
                field = strided(prod_ref.at[m], row, deep, rows)
                out_ref[m, q] = apply_vertical(vertical, field)


def own_kernel(
    rows, levels, tiles,
    bands_ref, steps_ref, members_ref, inc_ref, prev_ref,
    mine_ref, theirs_ref, cov_near_ref, cov_far_ref, mem_near_ref, mem_far_ref, inc_t_ref, prev_t_ref,
    prod_ref, memf_ref, one_ref, two_ref, pad_ref,
):
    tile = lax.axis_index("tile")
    half = lax.axis_index("mem") % 2
    counts = sweep_counts(steps_ref, tile, tiles)
    vertical = build_vertical(bands_ref, pad_ref, levels)
    deep, tall = up_to(levels, 16), up_to(levels, 8)
    total = rows * levels
    width = inc_ref.shape[-1]
    blank = jnp.zeros((width // 128, prod_ref.shape[1] - total, 128), F32)
    prod_ref[:, total:, :] = blank
    memf_ref[:, total:, :] = blank

    def transpose_to(ref):
        def body(row, _):
            ref[row] = strided(prod_ref, grid_row(tile, row, rows), tall, rows)
            return 0

        lax.fori_loop(0, rows, body, 0)

    put_flat(prod_ref, inc_ref[...])
    transpose_to(inc_t_ref)
    put_flat(prod_ref, prev_ref[...])
    transpose_to(prev_t_ref)
    zero = jnp.zeros((tall, width), F32)
    two_ref[0] = zero
    two_ref[rows + 5] = zero
    for m in range(members_ref.shape[0]):
        as_float = members_ref[m].astype(F32)
        put_flat(memf_ref, as_float)
        put_flat(prod_ref, as_float * inc_ref[...])
        for index in (0, 1, 2, rows + 3, rows + 4, rows + 5):
            one_ref[index] = zero

        def localize(row, _):
            field = strided(prod_ref, grid_row(tile, row, rows), deep, rows)
            one_ref[row + 3] = apply_vertical(vertical, field)
            return 0

        lax.fori_loop(0, rows, localize, 0)
        source, target = one_ref, two_ref
        for sweep in range(DIFF):
            own, near, far = (coefficient(sweep, count) for count in counts)

            def diffuse(index, _, source=source, target=target, own=own, near=near, far=far):
                rate = jnp.where(index < 3, far, jnp.where(index < rows + 3, own, near))
                here = source[index]
                around = source[index - 1] + source[index + 1] + left_of(here) + right_of(here)
                target[index] = here + rate * (around - 4.0 * here)
                return 0

            lax.fori_loop(1, rows + 5, diffuse, 0)
            source, target = target, source

        def member_row(row):
            return strided(memf_ref, grid_row(tile, row, rows), tall, rows)

        def add_to(ref, index, value):
            if m == 0:
                ref[index] = value
            else:
                ref[index] = ref[index] + value

        for q in range(DIFF):
            far_row, near_row = member_row(q), member_row(rows - 1 - q)
            mem_far_ref[m, q] = far_row
            mem_near_ref[m, q] = near_row
            add_to(cov_far_ref, q, far_row * source[q + 3])
            add_to(cov_near_ref, q, near_row * source[rows + 2 - q])
        part = (rows - 2 * DIFF) // 2
        for q in range(part):
            for ref, which in ((mine_ref, half), (theirs_ref, 1 - half)):
                row = DIFF + which * part + q
                add_to(ref, q, member_row(row) * source[row + 3])


def halo_kernel(near, tiles, steps_ref, halo_ref, mem_ref, cov_ref, out_ref):
    own_count, near_count, far_count = sweep_counts(steps_ref, lax.axis_index("tile"), tiles)
    own = [coefficient(k, own_count) for k in range(DIFF)]
    other = [coefficient(k, near_count if near else far_count) for k in range(DIFF)]

    def chunk(index, _):
        at = pl.ds(pl.multiple_of(index * 8, 8), 8)
        sums = [cov_ref[q, at, :] for q in range(DIFF)]
        for m in range(halo_ref.shape[0]):
            field = [None] * DIFF + [halo_ref[m, q, at, :] for q in range(DIFF)]
            for k in range(DIFF):
                new = list(field)
                for p in range(DIFF - 1 - k, 2 * DIFF - 1 - k):
                    rate = own[k] if p < DIFF else other[k]
                    around = field[p + 1]
                    if field[p] is not None:
                        here = field[p]
                        around = around + left_of(here) + right_of(here) - 4.0 * here
                        if p > 0 and field[p - 1] is not None:
                            around = around + field[p - 1]
                        new[p] = here + rate * around
                    else:
                        new[p] = rate * around
                field = new
            for q in range(DIFF):
                sums[q] = sums[q] + mem_ref[m, q, at, :] * field[DIFF - 1 - q]
        for q in range(DIFF):
            out_ref[q, at, :] = sums[q]
        return 0

    lax.fori_loop(0, halo_ref.shape[2] // 8, chunk, 0)


def reduced(value):
    return jnp.sum(value, axis=(0, 1), keepdims=True).reshape(1, 1)


def ratio(top, bottom):
    some = bottom != 0.0
    return jnp.where(some, top / jnp.where(some, bottom, F32(1.0)), F32(0.0))


def weighted(cov, inverse, prev, beta):
    return inverse * cov - beta * prev


def bulk_kernel(
    rows, inverse, halves,
    beta_ref, first_ref, second_ref, near_a_ref, near_b_ref, inc_ref, prev_ref, w_ref, sums_ref,
):
    beta = beta_ref[0]
    part = (rows - 2 * DIFF) // 2
    zero = jnp.zeros(inc_ref.shape[1:], F32)
    own_half = lax.axis_index("mem") % 2

    def rows_of():
        for q in range(part):
            yield DIFF + q, lambda q=q: jnp.where(own_half == 0, first_ref[q], second_ref[q])
        for q in range(part):
            yield DIFF + part + q, lambda q=q: jnp.where(own_half == 0, second_ref[q], first_ref[q])
        for q in range(DIFF):
            yield rows - 1 - q, lambda q=q: near_a_ref[q] + near_b_ref[q]

    square, cross = zero, zero
    for row, cov in rows_of():
        inc = inc_ref[row]
        scaled = inverse * cov()
        square = square + inc * inc
        cross = cross + inc * scaled
        w_ref[row - DIFF] = scaled - beta * prev_ref[row]
    square, cross = reduced(square), reduced(cross)
    pivot = ratio(cross, square)
    mixed, rest = zero, zero
    for row in range(DIFF, rows):
        inc = inc_ref[row]
        apart = w_ref[row - DIFF] - pivot * inc
        mixed = mixed + apart * inc
        rest = rest + apart * apart
    store_sums(sums_ref, square, cross, reduced(mixed), reduced(rest), pivot)


def store_sums(ref, *values):
    sub = lax.broadcasted_iota(jnp.int32, ref.shape, 0)
    out = jnp.zeros(ref.shape, F32)
    for index, value in enumerate(values):
        out = jnp.where(sub == index, value, out)
    ref[...] = out


def load_sums(ref):
    return [ref[index : index + 1, :] for index in range(5)]


def last_kernel(inverse, beta_ref, sums_ref, cov_a_ref, cov_b_ref, inc_ref, prev_ref, w_ref, out_ref):
    beta = beta_ref[0]
    square0, cross0, mixed0, rest0, pivot0 = [value[:, 0:1] for value in load_sums(sums_ref)]
    zero = jnp.zeros(inc_ref.shape[1:], F32)
    square, cross, mixed, rest = zero, zero, zero, zero
    for q in range(DIFF):
        inc = inc_ref[q]
        scaled = inverse * (cov_a_ref[q] + cov_b_ref[q])
        value = scaled - beta * prev_ref[q]
        w_ref[q] = value
        apart = value - pivot0 * inc
        square = square + inc * inc
        cross = cross + inc * scaled
        mixed = mixed + apart * inc
        rest = rest + apart * apart
    store_sums(
        out_ref,
        square0 + reduced(square), cross0 + reduced(cross), mixed0 + reduced(mixed), rest0 + reduced(rest), pivot0,
    )


def merged(parts):
    square = sum(part[0] for part in parts)
    cross = sum(part[1] for part in parts)
    pivot = ratio(cross, square)
    mixed, rest = F32(0.0), F32(0.0)
    for part in parts:
        shift = part[4] - pivot
        mixed = mixed + part[2] + shift * part[0]
        rest = rest + part[3] + 2.0 * shift * part[2] + shift * shift * part[0]
    return square, cross, mixed, rest, pivot


def merge_kernel(*refs):
    store_sums(refs[-1], *merged([load_sums(ref) for ref in refs[:-1]]))


def final_kernel(rows, levels, cells, count, *refs):
    sums_refs = refs[:count]
    w_far_ref, w_rest_ref, inc_ref, out_ref, coef_ref, flat_ref = refs[count:]
    tile = lax.axis_index("tile")
    _, _, _, rest, pivot = merged([load_sums(ref) for ref in sums_refs])
    scale = jnp.sqrt(rest / cells + 1e-6)
    coef_ref[...] = jnp.concatenate([1.0 + pivot, scale], axis=0)
    over = (1.0 / scale)[:, 0:1]
    pivot = pivot[:, 0:1]
    for row in range(rows):
        w = w_far_ref[row] if row < DIFF else w_rest_ref[row - DIFF]
        value = (w - pivot * inc_ref[row]) * over
        for piece in range(flat_ref.shape[0]):
            part = value[:levels, piece * 128 : (piece + 1) * 128]
            flat_ref[piece, pl.ds(grid_row(tile, row, rows), levels, stride=rows), :] = part
    for piece in range(flat_ref.shape[0]):
        out_ref[:, piece * 128 : (piece + 1) * 128] = flat_ref[piece]


def call(kernel, ins, outs, scratch=(), cost=None):
    specs = [smem() if kind == "s" else vmem() for kind, _ in ins]
    return pl.pallas_call(
        kernel,
        out_shape=tuple(jax.ShapeDtypeStruct(shape, F32) for shape in outs),
        in_specs=specs,
        out_specs=tuple(vmem() for _ in outs),
        scratch_shapes=scratch,
        compiler_params=pltpu.CompilerParams(vmem_limit_bytes=VMEM_LIMIT),
        cost_estimate=None
        if cost is None
        else pl.CostEstimate(flops=cost[0], bytes_accessed=cost[1], transcendentals=0),
    )(*(value for _, value in ins))


def flipped(axis, bit):
    count = lax.axis_size(axis)
    return [(i, i ^ bit) for i in range(count)]


def rotated(axis, digit, radix, by):
    count = lax.axis_size(axis)

    def target(i):
        value = i // digit % radix
        return i + ((value + by) % radix - value) * digit

    return [(i, target(i)) for i in range(count)]


def radices(count):
    out = [] if count % 2 else [2]
    rest = count // 2 if out else count
    factor = 4
    while rest > 1:
        while factor > 1 and rest % factor:
            factor -= 1
        if factor == 1:
            factor = rest
        out.append(factor)
        rest //= factor
        factor = min(factor, 4)
    return out


def per_device(increment, previous, beta_prev, members, band_widths, diffusion_steps):
    levels, rows, width = increment.shape
    tiles, mems = lax.axis_size("tile"), lax.axis_size("mem")
    owned = members.shape[0]
    tall, deep = up_to(levels, 8), up_to(levels, 16)
    inverse = 1.0 / (owned * mems - 1)
    cells = levels * rows * tiles * width
    inc = increment.reshape(levels * rows, width)
    prev = previous.reshape(levels * rows, width)
    mem = members.reshape(owned, levels * rows, width)
    bands = band_widths.reshape(1, levels)
    edge = (owned, DIFF, tall, width)
    part = (rows - 2 * DIFF) // 2
    near_pairs = [(i, i ^ 1) for i in range(tiles) if i ^ 1 < tiles]
    far_pairs = [pair for i in range(1, tiles - 1, 2) for pair in ((i, i + 1), (i + 1, i))]
    pad = pltpu.VMEM((8, 128), F32)

    near_edge, far_edge = call(
        functools.partial(edge_kernel, rows, levels),
        [("v", bands), ("v", mem), ("v", inc)],
        [edge, edge],
        [pltpu.VMEM((owned, width // 128, deep * rows, 128), F32), pad],
    )
    near_halo = lax.ppermute(near_edge, "tile", near_pairs)
    far_halo = lax.ppermute(far_edge, "tile", far_pairs)

    piece, four = (part, tall, width), (DIFF, tall, width)
    mine, theirs, cov_near, cov_far, mem_near, mem_far, inc_t, prev_t = call(
        functools.partial(own_kernel, rows, levels, tiles),
        [("v", bands), ("s", diffusion_steps), ("v", mem), ("v", inc), ("v", prev)],
        [piece, piece, four, four, edge, edge, (rows, tall, width), (rows, tall, width)],
        [pltpu.VMEM((width // 128, deep * rows, 128), F32)] * 2 + [pltpu.VMEM((rows + 6, tall, width), F32)] * 2 + [pad],
        (200_000_000, 10_000_000),
    )
    bits = [1 << k for k in range(1, mems.bit_length() - 1)]
    mine = mine + lax.ppermute(theirs, "mem", flipped("mem", 1))
    for bit in bits:
        mine = mine + lax.ppermute(mine, "mem", flipped("mem", bit))
    other = lax.ppermute(mine, "mem", flipped("mem", 1))

    def edge_sum(near, halo, mem_rows, cov):
        (value,) = call(
            functools.partial(halo_kernel, near, tiles),
            [("s", diffusion_steps), ("v", halo), ("v", mem_rows), ("v", cov)],
            [four],
        )
        for bit in [1] + bits[:-1]:
            value = value + lax.ppermute(value, "mem", flipped("mem", bit))
        return value, lax.ppermute(value, "mem", flipped("mem", bits[-1]))

    near_a, near_b = edge_sum(True, near_halo, mem_near, cov_near)
    w_rest, sums = call(
        functools.partial(bulk_kernel, rows, inverse, None),
        [("s", beta_prev), ("v", mine), ("v", other), ("v", near_a), ("v", near_b), ("v", inc_t), ("v", prev_t)],
        [(rows - DIFF, tall, width), (8, 128)],
    )
    far_a, far_b = edge_sum(False, far_halo, mem_far, cov_far)
    w_far, sums = call(
        functools.partial(last_kernel, inverse),
        [("s", beta_prev), ("v", sums), ("v", far_a), ("v", far_b), ("v", inc_t[:DIFF]), ("v", prev_t[:DIFF])],
        [four, (8, 128)],
    )
    digit = 1
    stages = radices(tiles)
    for index, radix in enumerate(stages):
        parts = [sums] + [lax.ppermute(sums, "tile", rotated("tile", digit, radix, by)) for by in range(1, radix)]
        if index < len(stages) - 1:
            (sums,) = call(merge_kernel, [("v", value) for value in parts], [(8, 128)])
        digit *= radix
    out, coefficients = call(
        functools.partial(final_kernel, rows, levels, cells, len(parts)),
        [("v", value) for value in parts] + [("v", w_far), ("v", w_rest), ("v", inc_t)],
        [(levels * rows, width), (2, 128)],
        [pltpu.VMEM((width // 128, levels * rows, 128), F32)],
    )
    return out.reshape(levels, rows, width), coefficients[:, 0]


def solution(mesh):
    in_specs = (
        P(None, "tile", None),
        P(None, "tile", None),
        P(),
        P("mem", None, "tile", None),
        P(),
        P(),
    )
    out_specs = (P(None, "tile", None), P())
    return jax.shard_map(
        per_device, mesh=mesh, in_specs=in_specs, out_specs=out_specs, check_vma=False
    )
```

time: 211 us -> 84.4 us (0.40)
  blocking collectives: 81.1 us -> 0 us
  Pallas kernels: 0 us -> 41.2 us
  waiting for transfers between devices: 57.2 us -> 20.5 us
  other arithmetic: 19.4 us -> 0.16 us
  between operations: 16.9 us -> 1.48 us
  starting transfers between devices: 26.4 us -> 17.1 us
  matrix products: 3.43 us -> 0 us
    psum x2 -> x0, blocking collectives: 81.1 us -> none  [the longest x1 41.4 us: lanczos_sums(): squares = lax.psum(jnp.sum(residual * residual), ('mem', 'tile'))]
    pallas_call x0 -> x8, Pallas kernels: none -> 41.2 us  [call(): pl.pallas_call(kernel, out_shape=tuple((jax.ShapeDtypeStruct(shape, F32)...]
    psum x1 -> x0, waiting for transfers between devices: 36.2 us -> none  [per_device(): summed = lax.psum(partial_value, 'mem')]
    ppermute x8 -> x13, starting transfers between devices: 26.4 us -> 17.1 us  [the longest x4 8.92 us: per_device(): lax.ppermute(sums, 'tile', rotated('tile', digit, radix, by))]
    reduce_sum x4 -> x0, other arithmetic: 7.08 us -> none  [the longest x1 3.81 us: per_device(): partial_value = jnp.sum(members_f * localized, axis=0)]
    select_n x4 -> x0, other arithmetic: 6.12 us -> none  [the longest x3 6.11 us: per_device(): jnp.where(sweep_index < step_count, localized + 0.24 * laplace, localized)]
    dot_general x1 -> x0, matrix products: 3.43 us -> none  [per_device(): jnp.einsum('ij,mjyx->miyx', vertical, members_f * increment[None], precis...]
    div x1 -> x0, other arithmetic: 2.96 us -> none  [per_device(): next_vector = residual / scale_value]
  transfers between devices with their start and end apart: 9 -> 13, of which waited for: 9 -> 7; matrix products, arithmetic and copies ran while one was open for 1% -> 0% of each run, Pallas kernels for 0% -> 45%
where the time goes in v1:
time: 84.4 us; the launch traced here: 84.2 us
  Pallas kernels  41.2 us (49%)
  waiting for transfers between devices  20.5 us (24%)
  starting transfers between devices  17.1 us (20%)
  local copies, waits for them, and re-layouts  3.85 us (5%)
  between operations  1.48 us (2%)
    pallas_call x8, Pallas kernels, call(): pl.pallas_call(kernel, out_shape=tuple((jax.ShapeDtypeStruct(shape, F32)...  41.2 us
    ppermute x2, waiting for transfers between devices, edge_sum(): return (value, lax.ppermute(value, 'mem', flipped('mem', bits[-1])))  12.1 us
    ppermute x4, starting transfers between devices, per_device(): lax.ppermute(sums, 'tile', rotated('tile', digit, radix, by))  8.92 us
    ppermute x4, waiting for transfers between devices, per_device(): lax.ppermute(sums, 'tile', rotated('tile', digit, radix, by))  5.41 us
    unnamed x16, local copies, waits for them, and re-layouts  3.18 us
    ppermute x1, starting transfers between devices, per_device(): near_halo = lax.ppermute(near_edge, 'tile', near_pairs)  3.05 us
    ppermute x2, starting transfers between devices, edge_sum(): return (value, lax.ppermute(value, 'mem', flipped('mem', bits[-1])))  2.16 us
  transfers between devices with their start and end apart: 13, of which 7 were waited for; matrix products, arithmetic and copies ran while one was open for 0% of the time, Pallas kernels for 45%

profile of v1, /device:TPU:0, one launch (start us, length us, event | category | flops | bytes accessed | tf_op | source)
XLA Modules:
  0.0 84.2 jit_solution(16149020808137073719)
XLA Ops:
  0.6 1.2 %copy-done.1 = bf16[2,70,16,256]{3,2,1,0:T(8,128)(2,1)S(1)} copy-done((bf16[2,70,16,256]{3,2,1,0:T(8,128)(2,1)S(1)}, bf16[2,70,16,256]{3,2,1,0:T(8,128)(2,1)}, u32[]{:S(2)}) %copy-start.1) | copy-done | bytes 1146904
  1.9 1.3 %copy-done.3 = f32[70,16,256]{2,1,0:T(8,128)S(1)} copy-done((f32[70,16,256]{2,1,0:T(8,128)S(1)}, f32[70,16,256]{2,1,0:T(8,128)}, u32[]{:S(2)}) %copy-start.3) | copy-done | bytes 1146904
  3.2 0.7 copy-done.7
  3.8 1.5 %shard_map.78 = (f32[2,4,72,256]{3,2,1,0:T(8,128)S(1)}, f32[2,4,72,256]{3,2,1,0:T(8,128)S(1)}) custom-call(s32[1,70]{1,0:T(1,128)S(1)} %bitcast.10, bf16[2,1120,256]{2,1,0:T(8,128)(2,1)S(1)} %bitcast.5, f32[1120,256]{1,0:T(8,128)S(1)} %bitcast.7), custom_call_target="tpu_custom_call" | custom-call | tf_op jit(solution)/shard_map/pallas_call | solution.py:340
  5.3 3.0 %collective-permute-start.3 = (f32[2,4,72,256]{3,2,1,0:T(8,128)S(1)}, f32[2,4,72,256]{3,2,1,0:T(8,128)S(1)}, u32[]{:S(2)}, u32[]{:S(2)}) collective-permute-start(f32[2,4,72,256]{3,2,1,0:T(8,128)S(1)} %get-tuple-element.20), channel_id=1, source_target_pairs={{0,1},{1,0},{2,3},{3,2},{4,5},{5,4},{6,7},{7,6},{8,9},{9,8},{10,11... | collective-permute-start | bytes 1769480 | tf_op jit(solution)/shard_map/ppermute | solution.py:406
  8.4 0.7 collective-permute-start.6
  9.1 31.2 %shard_map.77 = (f32[4,72,256]{2,1,0:T(8,128)S(1)}, f32[4,72,256]{2,1,0:T(8,128)S(1)}, f32[4,72,256]{2,1,0:T(8,128)S(1)}, f32[4,72,256]{2,1,0:T(8,128)S(1)}, f32...) custom-call(s32[1,70]{1,0:T(1,128)S(1)} %bitcast.11, ...), custom_call_target="tpu_custom_call" | custom-call | flops 200000000 | bytes 10000000 | tf_op jit(solution)/shard_map/pallas_call | solution.py:340
  40.3 0.0 collective-permute-start
  40.3 1.6 %collective-permute-done = f32[4,72,256]{2,1,0:T(8,128)S(1)} collective-permute-done((f32[4,72,256]{2,1,0:T(8,128)S(1)}, f32[4,72,256]{2,1,0:T(8,128)S(1)}, u32[]{:S(2)}, u32[]{:S(2)}) %collective-permute-start) | collective-permute-done | bytes 294944 | tf_op jit(solution)/shard_map/ppermute | solution.py:418
  41.9 1.6 %collective-permute-start.1 = (f32[4,72,256]{2,1,0:T(8,128)S(1)}, f32[4,72,256]{2,1,0:T(8,128)S(1)}, u32[]{:S(2)}, u32[]{:S(2)}) collective-permute-start(f32[4,72,256]{2,1,0:T(8,128)S(1)} %add.12), channel_id=1, source_target_pairs={{0,16},{8,24},{16,0},{24,8},{1,17},{9,25},{17,1},{25,9},{2,18},{10... | collective-permute-start | bytes 884744 | tf_op jit(solution)/shard_map/ppermute | solution.py:420
  43.5 0.0 collective-permute-done.3.halo_ref
  43.5 2.8 %shard_map.79 = f32[4,72,256]{2,1,0:T(8,128)S(1)} custom-call(s32[8]{0:T(128)S(1)} %copy-done.6, f32[2,4,72,256]{3,2,1,0:T(8,128)S(1)} %collective-permute-done.3.halo_ref, f32[2,4,72,256]{3,2,1,0:T(8,128)S(1)} %get-tuple-element.21.mem_ref, f32[4,72,256]{2,1,0:T(8,128)S(1)} %get-tuple-element.22.cov_ref), custom_call_target="tpu_custom_call" | custom-call | tf_op jit(solution)/shard_map/pallas_call | solution.py:340
  46.3 0.1 collective-permute-start.4
  46.4 2.8 %shard_map.81 = f32[4,72,256]{2,1,0:T(8,128)S(1)} custom-call(s32[8]{0:T(128)S(1)} %copy-done.6, f32[2,4,72,256]{3,2,1,0:T(8,128)S(1)} %collective-permute-done.6.halo_ref, f32[2,4,72,256]{3,2,1,0:T(8,128)S(1)} %get-tuple-element.27.mem_ref, f32[4,72,256]{2,1,0:T(8,128)S(1)} %get-tuple-element.28.cov_ref), custom_call_target="tpu_custom_call" | custom-call | tf_op jit(solution)/shard_map/pallas_call | solution.py:340
  49.2 0.6 collective-permute-start.7
  49.7 1.3 %collective-permute-done.1 = f32[4,72,256]{2,1,0:T(8,128)S(1)} collective-permute-done((f32[4,72,256]{2,1,0:T(8,128)S(1)}, f32[4,72,256]{2,1,0:T(8,128)S(1)}, u32[]{:S(2)}, u32[]{:S(2)}) %collective-permute-start.1) | collective-permute-done | bytes 294944 | tf_op jit(solution)/shard_map/ppermute | solution.py:420
  51.1 0.1 collective-permute-start.2
  51.2 1.6 %collective-permute-start.5 = (f32[4,72,256]{2,1,0:T(8,128)S(1)}, f32[4,72,256]{2,1,0:T(8,128)S(1)}, u32[]{:S(2)}, u32[]{:S(2)}) collective-permute-start(f32[4,72,256]{2,1,0:T(8,128)S(1)} %add.14.near_a_ref), channel_id=1, source_target_pairs={{0,16},{8,24},{16,0},{24,8},{1,17},{9,25},{17,1},{25,9},{2,18},{10... | collective-permute-start | bytes 884744 | tf_op jit(solution)/shard_map/ppermute | solution.py:431
  52.8 0.6 collective-permute-start.8
  54.2 6.9 %collective-permute-done.5.near_b_ref = f32[4,72,256]{2,1,0:T(8,128)S(1)} collective-permute-done((f32[4,72,256]{2,1,0:T(8,128)S(1)}, f32[4,72,256]{2,1,0:T(8,128)S(1)}, u32[]{:S(2)}, u32[]{:S(2)}) %collective-permute-start.5) | collective-permute-done | bytes 294944 | tf_op jit(solution)/shard_map/ppermute | solution.py:431
  61.1 0.7 shard_map.80
  61.8 5.2 %collective-permute-done.8.cov_b_ref = f32[4,72,256]{2,1,0:T(8,128)S(1)} collective-permute-done((f32[4,72,256]{2,1,0:T(8,128)S(1)}, f32[4,72,256]{2,1,0:T(8,128)S(1)}, u32[]{:S(2)}, u32[]{:S(2)}) %collective-permute-start.8) | collective-permute-done | bytes 294944 | tf_op jit(solution)/shard_map/ppermute | solution.py:431
  67.0 0.3 shard_map.82
  67.4 4.3 %collective-permute-start.9 = (f32[8,128]{1,0:T(8,128)S(1)}, f32[8,128]{1,0:T(8,128)S(1)}, u32[]{:S(2)}, u32[]{:S(2)}) collective-permute-start(f32[8,128]{1,0:T(8,128)S(1)} %get-tuple-element.29.refs_0_), channel_id=1, source_target_pairs={{0,1},{1,0},{2,3},{3,2},{4,5},{5,4},{6,7},{7,6},{8,9},{9,8},{10,11... | collective-permute-start | bytes 12296 | tf_op jit(solution)/shard_map/ppermute | solution.py:448
  71.6 1.6 %collective-permute-done.9.refs_1_ = f32[8,128]{1,0:T(8,128)S(1)} collective-permute-done((f32[8,128]{1,0:T(8,128)S(1)}, f32[8,128]{1,0:T(8,128)S(1)}, u32[]{:S(2)}, u32[]{:S(2)}) %collective-permute-start.9) | collective-permute-done | bytes 4128 | tf_op jit(solution)/shard_map/ppermute | solution.py:448
  73.2 3.1 %collective-permute-start.12 = (f32[8,128]{1,0:T(8,128)S(1)}, f32[8,128]{1,0:T(8,128)S(1)}, u32[]{:S(2)}, u32[]{:S(2)}) collective-permute-start(f32[8,128]{1,0:T(8,128)S(1)} %shard_map.83.refs_0_), channel_id=1, source_target_pairs={{0,6},{1,7},{2,0},{3,1},{4,2},{5,3},{6,4},{7,5},{8,14},{9,15},{10,... | collective-permute-start | bytes 12296 | tf_op jit(solution)/shard_map/ppermute | solution.py:448
  76.3 0.0 collective-permute-start.11
  76.3 1.6 %collective-permute-start.10 = (f32[8,128]{1,0:T(8,128)S(1)}, f32[8,128]{1,0:T(8,128)S(1)}, u32[]{:S(2)}, u32[]{:S(2)}) collective-permute-start(f32[8,128]{1,0:T(8,128)S(1)} %shard_map.83.refs_0_), channel_id=1, source_target_pairs={{0,2},{1,3},{2,4},{3,5},{4,6},{5,7},{6,0},{7,1},{8,10},{9,11},{10,... | collective-permute-start | bytes 12296 | tf_op jit(solution)/shard_map/ppermute | solution.py:448
  77.9 2.9 %collective-permute-done.11.refs_2_ = f32[8,128]{1,0:T(8,128)S(1)} collective-permute-done((f32[8,128]{1,0:T(8,128)S(1)}, f32[8,128]{1,0:T(8,128)S(1)}, u32[]{:S(2)}, u32[]{:S(2)}) %collective-permute-start.11) | collective-permute-done | bytes 4128 | tf_op jit(solution)/shard_map/ppermute | solution.py:448
  80.8 0.9 %collective-permute-done.10.refs_1_ = f32[8,128]{1,0:T(8,128)S(1)} collective-permute-done((f32[8,128]{1,0:T(8,128)S(1)}, f32[8,128]{1,0:T(8,128)S(1)}, u32[]{:S(2)}, u32[]{:S(2)}) %collective-permute-start.10) | collective-permute-done | bytes 4128 | tf_op jit(solution)/shard_map/ppermute | solution.py:448
  81.7 1.8 %shard_map.84 = (f32[1120,256]{1,0:T(8,128)}, f32[2,128]{1,0:T(2,128)S(1)}) custom-call(f32[8,128]{1,0:T(8,128)S(1)} %shard_map.83.refs_0_, f32[8,128]{1,0:T(8,128)S(1)} %collective-permute-done.10.refs_1_, f32[8,128]{1,0:T(8,128)S(1)} %collective-permute-done.11.refs_2_, f32[8,128]{1,0:T(8,128)S(1)} %collective-permute-done.12.refs_3_, ...), custom_call_target="tpu_custom_call" | custom-call | tf_op jit(solution)/shard_map/pallas_call | solution.py:340
  83.5 0.6 slice_reduce_fusion
  (25 shorter events, 0.3 us)
Async XLA Ops:
  0.6 1.3 %copy-start.1 = (bf16[2,70,16,256]{3,2,1,0:T(8,128)(2,1)S(1)}, bf16[2,70,16,256]{3,2,1,0:T(8,128)(2,1)}, u32[]{:S(2)}) copy-start(bf16[2,70,16,256]{3,2,1,0:T(8,128)(2,1)} %param.9) | copy-start | bytes 3440644
  1.9 1.3 %copy-start.3 = (f32[70,16,256]{2,1,0:T(8,128)S(1)}, f32[70,16,256]{2,1,0:T(8,128)}, u32[]{:S(2)}) copy-start(f32[70,16,256]{2,1,0:T(8,128)} %param.6) | copy-start | bytes 3440644
  3.2 0.7 copy-start.7
  3.8 5.3 %copy-start.2 = (bf16[2,70,16,256]{3,2,1,0:T(8,128)(2,1)S(1)}, bf16[2,70,16,256]{3,2,1,0:T(8,128)(2,1)}, u32[]{:S(2)}) copy-start(bf16[2,70,16,256]{3,2,1,0:T(8,128)(2,1)} %param.9) | copy-start | bytes 3440644
  3.8 5.3 %copy-start.5 = (f32[70,16,256]{2,1,0:T(8,128)S(1)}, f32[70,16,256]{2,1,0:T(8,128)}, u32[]{:S(2)}) copy-start(f32[70,16,256]{2,1,0:T(8,128)} %param.7) | copy-start | bytes 3440644
  3.8 5.3 %copy-start.6 = (s32[8]{0:T(128)S(1)}, s32[8]{0:T(128)}, u32[]{:S(2)}) copy-start(s32[8]{0:T(128)} %steps_ref.5) | copy-start | bytes 100
  5.3 38.2 %collective-permute-start.3 = (f32[2,4,72,256]{3,2,1,0:T(8,128)S(1)}, f32[2,4,72,256]{3,2,1,0:T(8,128)S(1)}, u32[]{:S(2)}, u32[]{:S(2)}) collective-permute-start(f32[2,4,72,256]{3,2,1,0:T(8,128)S(1)} %get-tuple-element.20), channel_id=1, source_target_pairs={{0,1},{1,0},{2,3},{3,2},{4,5},{5,4},{6,7},{7,6},{8,9},{9,8},{10,11... | collective-permute-start | bytes 1769480 | tf_op jit(solution)/shard_map/ppermute | solution.py:406
  8.4 38.0 %collective-permute-start.6 = (f32[2,4,72,256]{3,2,1,0:T(8,128)S(1)}, f32[2,4,72,256]{3,2,1,0:T(8,128)S(1)}, u32[]{:S(2)}, u32[]{:S(2)}) collective-permute-start(f32[2,4,72,256]{3,2,1,0:T(8,128)S(1)} %get-tuple-element.26), channel_id=1, source_target_pairs={{1,2},{2,1},{3,4},{4,3},{5,6},{6,5},{9,10},{10,9},{11,12},{12,11},... | collective-permute-start | bytes 1769480 | tf_op jit(solution)/shard_map/ppermute | solution.py:407
  40.3 1.6 %collective-permute-start = (f32[4,72,256]{2,1,0:T(8,128)S(1)}, f32[4,72,256]{2,1,0:T(8,128)S(1)}, u32[]{:S(2)}, u32[]{:S(2)}) collective-permute-start(f32[4,72,256]{2,1,0:T(8,128)S(1)} %get-tuple-element.19), channel_id=1, source_target_pairs={{0,8},{8,0},{16,24},{24,16},{1,9},{9,1},{17,25},{25,17},{2,10},{10... | collective-permute-start | bytes 884744 | tf_op jit(solution)/shard_map/ppermute | solution.py:418
  41.9 9.1 %collective-permute-start.1 = (f32[4,72,256]{2,1,0:T(8,128)S(1)}, f32[4,72,256]{2,1,0:T(8,128)S(1)}, u32[]{:S(2)}, u32[]{:S(2)}) collective-permute-start(f32[4,72,256]{2,1,0:T(8,128)S(1)} %add.12), channel_id=1, source_target_pairs={{0,16},{8,24},{16,0},{24,8},{1,17},{9,25},{17,1},{25,9},{2,18},{10... | collective-permute-start | bytes 884744 | tf_op jit(solution)/shard_map/ppermute | solution.py:420
  46.3 4.9 %collective-permute-start.4 = (f32[4,72,256]{2,1,0:T(8,128)S(1)}, f32[4,72,256]{2,1,0:T(8,128)S(1)}, u32[]{:S(2)}, u32[]{:S(2)}) collective-permute-start(f32[4,72,256]{2,1,0:T(8,128)S(1)} %shard_map.79), channel_id=1, source_target_pairs={{0,8},{8,0},{16,24},{24,16},{1,9},{9,1},{17,25},{25,17},{2,10},{10... | collective-permute-start | bytes 884744 | tf_op jit(solution)/shard_map/ppermute | solution.py:430
  49.2 4.9 %copy-start.4 = (f32[16,72,256]{2,1,0:T(8,128)S(1)}, f32[16,72,256]{2,1,0:T(8,128)}, u32[]{:S(2)}) copy-start(f32[16,72,256]{2,1,0:T(8,128)} %get-tuple-element.24.prev_ref) | copy-start | bytes 3538948
  49.2 3.6 %collective-permute-start.7 = (f32[4,72,256]{2,1,0:T(8,128)S(1)}, f32[4,72,256]{2,1,0:T(8,128)S(1)}, u32[]{:S(2)}, u32[]{:S(2)}) collective-permute-start(f32[4,72,256]{2,1,0:T(8,128)S(1)} %shard_map.81), channel_id=1, source_target_pairs={{0,8},{8,0},{16,24},{24,16},{1,9},{9,1},{17,25},{25,17},{2,10},{10... | collective-permute-start | bytes 884744 | tf_op jit(solution)/shard_map/ppermute | solution.py:430
  51.1 3.0 %copy-start = (f32[16,72,256]{2,1,0:T(8,128)S(1)}, f32[16,72,256]{2,1,0:T(8,128)}, u32[]{:S(2)}) copy-start(f32[16,72,256]{2,1,0:T(8,128)} %get-tuple-element.23.inc_ref.refs_6_) | copy-start | bytes 3538948
  51.1 3.1 %collective-permute-start.2 = (f32[4,72,256]{2,1,0:T(8,128)S(1)}, f32[4,72,256]{2,1,0:T(8,128)S(1)}, u32[]{:S(2)}, u32[]{:S(2)}) collective-permute-start(f32[4,72,256]{2,1,0:T(8,128)S(1)} %add.13.first_ref), channel_id=1, source_target_pairs={{0,8},{8,0},{16,24},{24,16},{1,9},{9,1},{17,25},{25,17},{2,10},{10... | collective-permute-start | bytes 884744 | tf_op jit(solution)/shard_map/ppermute | solution.py:421
  51.2 9.9 %collective-permute-start.5 = (f32[4,72,256]{2,1,0:T(8,128)S(1)}, f32[4,72,256]{2,1,0:T(8,128)S(1)}, u32[]{:S(2)}, u32[]{:S(2)}) collective-permute-start(f32[4,72,256]{2,1,0:T(8,128)S(1)} %add.14.near_a_ref), channel_id=1, source_target_pairs={{0,16},{8,24},{16,0},{24,8},{1,17},{9,25},{17,1},{25,9},{2,18},{10... | collective-permute-start | bytes 884744 | tf_op jit(solution)/shard_map/ppermute | solution.py:431
  52.8 14.2 %collective-permute-start.8 = (f32[4,72,256]{2,1,0:T(8,128)S(1)}, f32[4,72,256]{2,1,0:T(8,128)S(1)}, u32[]{:S(2)}, u32[]{:S(2)}) collective-permute-start(f32[4,72,256]{2,1,0:T(8,128)S(1)} %add.15.cov_a_ref), channel_id=1, source_target_pairs={{0,16},{8,24},{16,0},{24,8},{1,17},{9,25},{17,1},{25,9},{2,18},{10... | collective-permute-start | bytes 884744 | tf_op jit(solution)/shard_map/ppermute | solution.py:431
  67.4 5.8 %collective-permute-start.9 = (f32[8,128]{1,0:T(8,128)S(1)}, f32[8,128]{1,0:T(8,128)S(1)}, u32[]{:S(2)}, u32[]{:S(2)}) collective-permute-start(f32[8,128]{1,0:T(8,128)S(1)} %get-tuple-element.29.refs_0_), channel_id=1, source_target_pairs={{0,1},{1,0},{2,3},{3,2},{4,5},{5,4},{6,7},{7,6},{8,9},{9,8},{10,11... | collective-permute-start | bytes 12296 | tf_op jit(solution)/shard_map/ppermute | solution.py:448
  73.2 4.7 %collective-permute-start.12 = (f32[8,128]{1,0:T(8,128)S(1)}, f32[8,128]{1,0:T(8,128)S(1)}, u32[]{:S(2)}, u32[]{:S(2)}) collective-permute-start(f32[8,128]{1,0:T(8,128)S(1)} %shard_map.83.refs_0_), channel_id=1, source_target_pairs={{0,6},{1,7},{2,0},{3,1},{4,2},{5,3},{6,4},{7,5},{8,14},{9,15},{10,... | collective-permute-start | bytes 12296 | tf_op jit(solution)/shard_map/ppermute | solution.py:448
  76.3 4.5 %collective-permute-start.11 = (f32[8,128]{1,0:T(8,128)S(1)}, f32[8,128]{1,0:T(8,128)S(1)}, u32[]{:S(2)}, u32[]{:S(2)}) collective-permute-start(f32[8,128]{1,0:T(8,128)S(1)} %shard_map.83.refs_0_), channel_id=1, source_target_pairs={{0,4},{1,5},{2,6},{3,7},{4,0},{5,1},{6,2},{7,3},{8,12},{9,13},{10,... | collective-permute-start | bytes 12296 | tf_op jit(solution)/shard_map/ppermute | solution.py:448
  76.3 5.4 %collective-permute-start.10 = (f32[8,128]{1,0:T(8,128)S(1)}, f32[8,128]{1,0:T(8,128)S(1)}, u32[]{:S(2)}, u32[]{:S(2)}) collective-permute-start(f32[8,128]{1,0:T(8,128)S(1)} %shard_map.83.refs_0_), channel_id=1, source_target_pairs={{0,2},{1,3},{2,4},{3,5},{4,6},{5,7},{6,0},{7,1},{8,10},{9,11},{10,... | collective-permute-start | bytes 12296 | tf_op jit(solution)/shard_map/ppermute | solution.py:448

commit v2 on v1

v2 whole, which is shorter than its diff:
```python
import functools

import jax
import jax.numpy as jnp
import ml_dtypes
import numpy as np
from jax import lax
from jax.experimental import pallas as pl
from jax.experimental.pallas import tpu as pltpu
from jax.sharding import PartitionSpec as P

DIFF = 4
RATE = 0.24
F32 = jnp.float32
VMEM_LIMIT = 32 * 1024 * 1024
EDGE_LIMIT = 60 * 1024 * 1024


def up_to(value, unit):
    return -(-value // unit) * unit


def grid_row(tile, row, rows):
    return jnp.where(tile % 2 == 0, row, rows - 1 - row)


def put_flat(ref, value):
    for piece in range(ref.shape[0]):
        ref[piece, : value.shape[0], :] = value[:, piece * 128 : (piece + 1) * 128]


def strided(ref, start, count, stride):
    pieces = [ref[piece, pl.ds(start, count, stride=stride), :] for piece in range(ref.shape[0])]
    return jnp.concatenate(pieces, axis=1)


def sweep_counts(steps_ref, tile, tiles):
    even = tile % 2 == 0
    near = jnp.where(even, tile + 1, tile - 1)
    far = jnp.where(even, tile - 1, tile + 1)

    def count(index):
        inside = (index >= 0) & (index < tiles)
        return jnp.where(inside, steps_ref[jnp.clip(index, 0, tiles - 1)], 0)

    return count(tile), count(near), count(far)


def coefficient(sweep, count):
    return jnp.where(sweep < count, F32(RATE), F32(0.0))


def build_vertical(bands_ref, pad_ref, levels):
    pad_ref[...] = jnp.ones(pad_ref.shape, F32)
    pad_ref[0:1, 0:levels] = bands_ref[...].astype(F32)
    across = jnp.broadcast_to(pad_ref[0:1, :], (128, 128))
    down = across.T
    i = lax.broadcasted_iota(jnp.int32, (128, 128), 0)
    j = lax.broadcasted_iota(jnp.int32, (128, 128), 1)
    apart = (i - j).astype(F32)
    weight = jnp.exp(-(apart * apart) / (down * across))
    keep = (jnp.abs(apart) <= jnp.minimum(down, across)) & (i < levels) & (j < levels)
    full = jnp.where(keep, weight, F32(0.0))[: up_to(levels, 8), : up_to(levels, 16)]
    high = full.astype(jnp.bfloat16)
    return high, (full - high.astype(F32)).astype(jnp.bfloat16)


def apply_vertical(vertical, field):
    v_high, v_low = vertical
    high = field.astype(jnp.bfloat16)
    low = (field - high.astype(F32)).astype(jnp.bfloat16)
    dot = functools.partial(jnp.dot, preferred_element_type=F32)
    return dot(v_high, high) + dot(v_high, low) + dot(v_low, high)


def sine_matrix(width):
    mode = np.arange(1, width + 1)
    full = np.sqrt(2.0 / (width + 1)) * np.sin(np.pi * np.outer(mode, mode) / (width + 1))
    high = full.astype(ml_dtypes.bfloat16)
    low = (full - high.astype(np.float64)).astype(ml_dtypes.bfloat16)
    waves = np.broadcast_to(2.0 * np.cos(np.pi * mode / (width + 1)), (8, width)).astype(np.float32)
    return jnp.asarray(high), jnp.asarray(low), jnp.asarray(waves)


def transform(field, s_high, s_low):
    high = field.astype(jnp.bfloat16)
    low = (field - high.astype(F32)).astype(jnp.bfloat16)
    dot = functools.partial(jnp.dot, preferred_element_type=F32)
    return dot(high, s_high) + dot(low, s_high) + dot(high, s_low)


def advance(field, rates, bases):
    new = {}
    for p, rate in rates.items():
        near = [field[p + d] for d in (-1, 1) if p + d in field]
        value = None
        if near:
            value = rate * (near[0] + near[1] if len(near) == 2 else near[0])
        if p in field:
            here = bases[p] * field[p]
            value = here if value is None else here + value
        if value is not None:
            new[p] = value
    return new


def base_of(rate, waves):
    return (1.0 - 4.0 * rate) + rate * waves


def edge_kernel(
    near, rows, levels, cuts,
    bands_hbm, members_hbm, inc_hbm, s_high_hbm, s_low_hbm, *refs,
):
    out_refs = refs[: len(cuts)]
    bands_ref, mem_ref, inc_ref, s_high_ref, s_low_ref, prod_ref, pad_ref, sems = refs[len(cuts) :]
    tile = lax.axis_index("tile")
    high_end = (tile % 2 == 0) == near
    start = pl.multiple_of(jnp.where(high_end, rows - 8, 0), 8)
    owned = members_hbm.shape[0]
    pairs = [(bands_hbm, bands_ref), (inc_hbm.at[:, pl.ds(start, 8), :], inc_ref)]
    pairs += [(members_hbm.at[m, :, pl.ds(start, 8), :], mem_ref.at[m]) for m in range(owned)]
    pairs += [(s_high_hbm, s_high_ref), (s_low_hbm, s_low_ref)]
    copies = [pltpu.make_async_copy(source, target, sems.at[k]) for k, (source, target) in enumerate(pairs)]
    for copy in copies:
        copy.start()
    width = inc_ref.shape[-1]
    deep, tall = up_to(levels, 16), up_to(levels, 8)
    for piece in range(width // 128):
        prod_ref[piece, levels * 8 :, :] = jnp.zeros((prod_ref.shape[1] - levels * 8, 128), F32)
    copies[0].wait()
    vertical = build_vertical(bands_ref, pad_ref, levels)
    copies[1].wait()
    for m in range(owned):
        copies[2 + m].wait()
        product = mem_ref[m].astype(F32) * inc_ref[...]
        put_flat(prod_ref, product.reshape(levels * 8, width))
        local = []
        for q in range(DIFF):
            row = jnp.where(high_end, 7 - q, q)
            local.append(apply_vertical(vertical, strided(prod_ref, row, deep, 8)))
        if m == 0:
            copies[2 + owned].wait()
            copies[3 + owned].wait()
        waves = transform(jnp.concatenate(local, axis=0), s_high_ref[...], s_low_ref[...])
        for q in range(DIFF):
            for (low, high), out_ref in zip(cuts, out_refs):
                for piece in range(width // 128):
                    part = waves[q * tall + low : q * tall + high, piece * 128 : (piece + 1) * 128]
                    out_ref[m, piece, pl.ds(q, high - low, stride=DIFF), :] = part


def own_kernel(
    rows, levels, tiles,
    bands_ref, steps_ref, members_ref, inc_ref, prev_ref, s_high_ref, s_low_ref, waves_ref,
    mine_ref, theirs_ref, cov_near_ref, cov_far_ref, mem_near_ref, mem_far_ref, inc_t_ref, prev_t_ref,
    prod_ref, memf_ref, spec_ref, acc_ref, base_ref, pad_ref,
):
    tile = lax.axis_index("tile")
    half = lax.axis_index("mem") % 2
    counts = sweep_counts(steps_ref, tile, tiles)
    vertical = build_vertical(bands_ref, pad_ref, levels)
    deep, tall = up_to(levels, 16), up_to(levels, 8)
    total = rows * levels
    width = inc_ref.shape[-1]
    for ref in (prod_ref, memf_ref):
        for piece in range(width // 128):
            ref[piece, total:, :] = jnp.zeros((ref.shape[1] - total, 128), F32)

    def row_of(ref, row, count):
        return strided(ref, grid_row(tile, row, rows), count, rows)

    for source, target in ((inc_ref, inc_t_ref), (prev_ref, prev_t_ref)):
        put_flat(prod_ref, source[...])
        for row in range(rows):
            target[row] = row_of(prod_ref, row, tall)
    rate = [[coefficient(k, count) for count in counts] for k in range(DIFF)]
    for k in range(DIFF):
        for side in range(3):
            base_ref[k, side] = base_of(rate[k][side], waves_ref[...])

    def side_of(p):
        return 2 if p < 0 else 1 if p >= rows else 0

    for m in range(members_ref.shape[0]):
        as_float = members_ref[m].astype(F32)
        put_flat(memf_ref, as_float)
        put_flat(prod_ref, transform(as_float * inc_ref[...], s_high_ref[...], s_low_ref[...]))
        for row in range(rows):
            spec_ref[row] = apply_vertical(vertical, row_of(prod_ref, row, deep))

        def chunk(index, _):
            at = pl.ds(pl.multiple_of(index * 8, 8), 8)
            field = {p: spec_ref[p, at, :] for p in range(rows)}
            for k in range(DIFF):
                out = min(k + 1, DIFF - 1 - k)
                kept = range(-out, rows + out)
                bases = {p: base_ref[k, side_of(p)] for p in kept}
                field = advance(field, {p: rate[k][side_of(p)] for p in kept}, bases)
            for p in range(rows):
                spec_ref[p, at, :] = field[p]
            return 0

        lax.fori_loop(0, tall // 8, chunk, 0)
        group = 4
        for first in range(0, rows, group):
            block = spec_ref[first : first + group].reshape(group * tall, width)
            block = transform(block, s_high_ref[...], s_low_ref[...])
            for k in range(group):
                row = first + k
                member = row_of(memf_ref, row, tall)
                if row < DIFF:
                    mem_far_ref[m, row] = member
                if row >= rows - DIFF:
                    mem_near_ref[m, rows - 1 - row] = member
                value = member * block[k * tall : (k + 1) * tall]
                acc_ref[row] = value if m == 0 else acc_ref[row] + value
    part = (rows - 2 * DIFF) // 2
    for q in range(DIFF):
        cov_far_ref[q] = acc_ref[q]
        cov_near_ref[q] = acc_ref[rows - 1 - q]
    for q in range(part):
        mine_ref[q] = acc_ref[DIFF + half * part + q]
        theirs_ref[q] = acc_ref[DIFF + (1 - half) * part + q]


def halo_kernel(
    near, tiles, cut,
    steps_ref, halo_ref, mem_ref, cov_ref, s_high_ref, s_low_ref, waves_ref, out_ref, spec_ref, base_ref,
):
    counts = sweep_counts(steps_ref, lax.axis_index("tile"), tiles)
    owned, width = halo_ref.shape[0], cov_ref.shape[-1]
    low, high = cut
    count, tall = high - low, up_to(high - low, 8)
    rate = [[coefficient(k, counts[0]), coefficient(k, counts[1 if near else 2])] for k in range(DIFF)]
    for k in range(DIFF):
        for side in range(2):
            base_ref[k, side] = base_of(rate[k][side], waves_ref[...])
    for m in range(owned):
        for at in range(0, count, 8):
            size = min(8, count - at)
            field = {q: strided(halo_ref.at[m], q + DIFF * at, size, DIFF) for q in range(DIFF)}
            for k in range(DIFF):
                kept = range(-1 - k, DIFF - 1 - k)
                bases = {p: base_ref[k, 0 if p < 0 else 1][:size] for p in kept}
                field = advance(field, {p: rate[k][0 if p < 0 else 1] for p in kept}, bases)
            for q in range(DIFF):
                spec_ref[q, at : at + size, :] = field[-1 - q]
        if count < tall:
            for q in range(DIFF):
                spec_ref[q, count:, :] = jnp.zeros((tall - count, width), F32)
        block = spec_ref[...].reshape(DIFF * tall, width)
        block = transform(block, s_high_ref[...], s_low_ref[...])
        for q in range(DIFF):
            value = mem_ref[m, q, low : low + tall, :] * block[q * tall : (q + 1) * tall]
            out_ref[q] = value + (cov_ref[q, low : low + tall, :] if m == 0 else out_ref[q])


def reduced(value):
    return jnp.sum(value, axis=(0, 1), keepdims=True)


def folded(value):
    return jnp.sum(value.reshape(value.shape[0] // 8, 8, value.shape[1]), axis=0)


def ratio(top, bottom):
    some = bottom != 0.0
    return jnp.where(some, top / jnp.where(some, bottom, F32(1.0)), F32(0.0))


def put_row(ref, row, rows, low, value):
    for piece in range(ref.shape[0]):
        part = value[:, piece * 128 : (piece + 1) * 128]
        ref[piece, pl.ds(row + low * rows, value.shape[0], stride=rows), :] = part


def bulk_kernel(
    rows, levels, inverse, cut,
    beta_ref, mine_ref, other_ref, near_a_ref, near_b_ref, far_a_ref, far_b_ref, inc_ref, prev_ref,
    w_ref, sums_ref, keep_ref,
):
    beta = beta_ref[0]
    tile = lax.axis_index("tile")
    part = (rows - 2 * DIFF) // 2
    own_half = lax.axis_index("mem") % 2
    zero = jnp.zeros((8, inc_ref.shape[-1]), F32)

    def covariance(row):
        if row < DIFF:
            return far_a_ref[row] + far_b_ref[row]
        if row >= rows - DIFF:
            q = rows - 1 - row
            return near_a_ref[q] + near_b_ref[q]
        which, q = divmod(row - DIFF, part)
        return jnp.where(own_half == which, mine_ref[q], other_ref[q])

    square, cross = zero, zero
    for row in range(rows):
        high = cut if row < DIFF else inc_ref.shape[1]
        inc = inc_ref[row, :high]
        scaled = inverse * covariance(row)
        square = square + folded(inc * inc)
        cross = cross + folded(inc * scaled)
        value = scaled - beta * prev_ref[row, :high]
        keep_ref[row, :high] = value
        put_row(w_ref, grid_row(tile, row, rows), rows, 0, value[: min(high, levels)])
    square, cross = reduced(square), reduced(cross)
    pivot = ratio(cross, square)
    mixed, rest = zero, zero
    for row in range(rows):
        high = cut if row < DIFF else inc_ref.shape[1]
        inc = inc_ref[row, :high]
        apart = keep_ref[row, :high] - pivot * inc
        mixed = mixed + folded(apart * inc)
        rest = rest + folded(apart * apart)
    store_sums(sums_ref, square, cross, reduced(mixed), reduced(rest), pivot)


def store_sums(ref, *values):
    sub = lax.broadcasted_iota(jnp.int32, ref.shape, 0)
    out = jnp.zeros(ref.shape, F32)
    for index, value in enumerate(values):
        out = jnp.where(sub == index, value, out)
    ref[...] = out


def load_sums(ref):
    return [ref[index : index + 1, :] for index in range(5)]


def last_kernel(inverse, cut, beta_ref, sums_ref, cov_a_ref, cov_b_ref, inc_ref, prev_ref, w_ref, out_ref):
    beta = beta_ref[0]
    square0, cross0, mixed0, rest0, pivot0 = [value[:, 0:1] for value in load_sums(sums_ref)]
    zero = jnp.zeros((8, inc_ref.shape[-1]), F32)
    square, cross, mixed, rest = zero, zero, zero, zero
    for q in range(DIFF):
        inc = inc_ref[q, cut:]
        scaled = inverse * (cov_a_ref[q] + cov_b_ref[q])
        value = scaled - beta * prev_ref[q, cut:]
        w_ref[q] = value
        apart = value - pivot0 * inc
        square = square + folded(inc * inc)
        cross = cross + folded(inc * scaled)
        mixed = mixed + folded(apart * inc)
        rest = rest + folded(apart * apart)
    store_sums(
        out_ref,
        square0 + reduced(square), cross0 + reduced(cross), mixed0 + reduced(mixed), rest0 + reduced(rest), pivot0,
    )


def merged(parts):
    square = sum(part[0] for part in parts)
    cross = sum(part[1] for part in parts)
    pivot = ratio(cross, square)
    mixed, rest = F32(0.0), F32(0.0)
    for part in parts:
        shift = part[4] - pivot
        mixed = mixed + part[2] + shift * part[0]
        rest = rest + part[3] + 2.0 * shift * part[2] + shift * shift * part[0]
    return square, cross, mixed, rest, pivot


def merge_kernel(*refs):
    store_sums(refs[-1], *merged([load_sums(ref) for ref in refs[:-1]]))


def final_kernel(rows, levels, cells, cut, count, *refs):
    sums_refs = refs[:count]
    w_far_ref, w_ref, inc_ref, out_hbm, coef_ref, out_ref, end_ref, sems = refs[count:]
    tile = lax.axis_index("tile")
    _, _, _, rest, pivot = merged([load_sums(ref) for ref in sums_refs])
    scale = jnp.sqrt(rest / cells + 1e-6)
    lane = lax.broadcasted_iota(jnp.int32, scale.shape, 1)
    coef_ref[...] = jnp.where(lane == 0, 1.0 + pivot, scale)[:, :2]
    over = 1.0 / scale
    total, edge = rows * levels, rows * cut
    end_ref[...] = w_ref[:, edge:, :]
    for q in range(DIFF):
        put_row(end_ref, grid_row(tile, q, rows), rows, 0, w_far_ref[q, : levels - cut])
    bounds = [0, edge // 16 * 8, edge, total]
    copies = []
    for k in range(3):
        low, high = bounds[k], bounds[k + 1]
        for piece in range(w_ref.shape[0]):
            lanes = slice(piece * 128, (piece + 1) * 128)
            w = end_ref[piece] if k == 2 else w_ref[piece, low:high, :]
            out_ref[low:high, lanes] = (w - pivot * inc_ref[low:high, lanes]) * over
        copies.append(pltpu.make_async_copy(out_ref.at[low:high], out_hbm.at[low:high], sems.at[k]))
        copies[-1].start()
    for copy in copies:
        copy.wait()


def call(kernel, ins, outs, scratch=(), cost=None, limit=VMEM_LIMIT):
    spaces = {"s": pltpu.SMEM, "v": pltpu.VMEM, "h": pl.ANY}
    outs = [out if isinstance(out[0], str) else ("v", out) for out in outs]
    estimate = None
    if cost is not None:
        estimate = pl.CostEstimate(flops=cost[0], bytes_accessed=cost[1], transcendentals=0)
    return pl.pallas_call(
        kernel,
        out_shape=tuple(jax.ShapeDtypeStruct(shape, F32) for _, shape in outs),
        in_specs=[pl.BlockSpec(memory_space=spaces[kind]) for kind, _ in ins],
        out_specs=tuple(pl.BlockSpec(memory_space=spaces[kind]) for kind, _ in outs),
        scratch_shapes=scratch,
        compiler_params=pltpu.CompilerParams(vmem_limit_bytes=limit),
        cost_estimate=estimate,
    )(*(value for _, value in ins))


def flipped(axis, bit):
    count = lax.axis_size(axis)
    return [(i, i ^ bit) for i in range(count)]


def rotated(axis, digit, radix, by):
    count = lax.axis_size(axis)

    def target(i):
        value = i // digit % radix
        return i + ((value + by) % radix - value) * digit

    return [(i, target(i)) for i in range(count)]


def radices(count):
    out = [] if count % 2 else [2]
    rest = count // 2 if out else count
    factor = 4
    while rest > 1:
        while factor > 1 and rest % factor:
            factor -= 1
        if factor == 1:
            factor = rest
        out.append(factor)
        rest //= factor
        factor = min(factor, 4)
    return out


def per_device(increment, previous, beta_prev, members, band_widths, diffusion_steps):
    levels, rows, width = increment.shape
    tiles, mems = lax.axis_size("tile"), lax.axis_size("mem")
    owned = members.shape[0]
    tall, deep = up_to(levels, 8), up_to(levels, 16)
    cut = up_to(2 * levels // 3, 8)
    inverse = 1.0 / (owned * mems - 1)
    cells = levels * rows * tiles * width
    lanes = width // 128
    inc = increment.reshape(levels * rows, width)
    prev = previous.reshape(levels * rows, width)
    mem = members.reshape(owned, levels * rows, width)
    bands = band_widths.reshape(1, levels)
    s_high, s_low, waves = sine_matrix(width)
    edge = (owned, DIFF, tall, width)
    part = (rows - 2 * DIFF) // 2
    near_pairs = [(i, i ^ 1) for i in range(tiles) if i ^ 1 < tiles]
    far_pairs = [pair for i in range(1, tiles - 1, 2) for pair in ((i, i + 1), (i + 1, i))]
    pad = pltpu.VMEM((8, 128), F32)

    def edges(near, cuts):
        return call(
            functools.partial(edge_kernel, near, rows, levels, cuts),
            [("h", bands), ("h", members), ("h", increment), ("h", s_high), ("h", s_low)],
            [(owned, lanes, DIFF * (high - low), 128) for low, high in cuts],
            [
                pltpu.VMEM((1, levels), jnp.int32),
                pltpu.VMEM((owned, levels, 8, width), jnp.bfloat16),
                pltpu.VMEM((levels, 8, width), F32),
                pltpu.VMEM((width, width), jnp.bfloat16),
                pltpu.VMEM((width, width), jnp.bfloat16),
                pltpu.VMEM((lanes, deep * 8, 128), F32),
                pad,
                pltpu.SemaphoreType.DMA((owned + 4,)),
            ],
            limit=EDGE_LIMIT if near else VMEM_LIMIT,
        )

    near_cut, far_cuts = (0, levels), [(0, cut), (cut, levels)]
    (near_edge,) = edges(True, [near_cut])
    near_halo = lax.ppermute(near_edge, "tile", near_pairs)
    far_edges = edges(False, far_cuts)
    far_halos = [lax.ppermute(value, "tile", far_pairs) for value in far_edges]

    piece, four = (part, tall, width), (DIFF, tall, width)
    mine, theirs, cov_near, cov_far, mem_near, mem_far, inc_t, prev_t = call(
        functools.partial(own_kernel, rows, levels, tiles),
        [("v", bands), ("s", diffusion_steps), ("v", mem), ("v", inc), ("v", prev)]
        + [("v", s_high), ("v", s_low), ("v", waves)],
        [piece, piece, four, four, edge, edge, (rows, tall, width), (rows, tall, width)],
        [pltpu.VMEM((lanes, deep * rows, 128), F32)] * 2
        + [pltpu.VMEM((rows, tall, width), F32)] * 2
        + [pltpu.VMEM((DIFF, 3, 8, width), F32), pad],
        (200_000_000, 10_000_000),
    )
    bits = [1 << k for k in range(1, mems.bit_length() - 1)]
    mine = mine + lax.ppermute(theirs, "mem", flipped("mem", 1))
    for bit in bits:
        mine = mine + lax.ppermute(mine, "mem", flipped("mem", bit))
    other = lax.ppermute(mine, "mem", flipped("mem", 1))

    def edge_sum(near, span, halo, mem_rows, cov):
        size = up_to(span[1] - span[0], 8)
        (value,) = call(
            functools.partial(halo_kernel, near, tiles, span),
            [("s", diffusion_steps), ("v", halo), ("v", mem_rows), ("v", cov)]
            + [("v", s_high), ("v", s_low), ("v", waves)],
            [(DIFF, size, width)],
            [pltpu.VMEM((DIFF, size, width), F32), pltpu.VMEM((DIFF, 2, 8, width), F32)],
        )
        for bit in [1] + bits[:-1]:
            value = value + lax.ppermute(value, "mem", flipped("mem", bit))
        return value, lax.ppermute(value, "mem", flipped("mem", bits[-1]))

    near_sums = edge_sum(True, near_cut, near_halo, mem_near, cov_near)
    far_sums = edge_sum(False, far_cuts[0], far_halos[0], mem_far, cov_far)
    w_rest, sums = call(
        functools.partial(bulk_kernel, rows, levels, inverse, cut),
        [("s", beta_prev), ("v", mine), ("v", other)]
        + [("v", value) for value in near_sums + far_sums]
        + [("v", inc_t), ("v", prev_t)],
        [(lanes, levels * rows, 128), (8, 128)],
        [pltpu.VMEM((rows, tall, width), F32)],
    )
    last_sums = edge_sum(False, far_cuts[1], far_halos[1], mem_far, cov_far)
    w_far, sums = call(
        functools.partial(last_kernel, inverse, cut),
        [("s", beta_prev), ("v", sums)] + [("v", value) for value in last_sums] + [("v", inc_t), ("v", prev_t)],
        [(DIFF, tall - cut, width), (8, 128)],
    )
    digit = 1
    stages = radices(tiles)
    for index, radix in enumerate(stages):
        parts = [sums] + [lax.ppermute(sums, "tile", rotated("tile", digit, radix, by)) for by in range(1, radix)]
        if index < len(stages) - 1:
            (sums,) = call(merge_kernel, [("v", value) for value in parts], [(8, 128)])
        digit *= radix
    out, coefficients = call(
        functools.partial(final_kernel, rows, levels, cells, cut, len(parts)),
        [("v", value) for value in parts] + [("v", w_far), ("v", w_rest), ("v", inc)],
        [("h", (levels * rows, width)), (1, 2)],
        [
            pltpu.VMEM((levels * rows, width), F32),
            pltpu.VMEM((lanes, (levels - cut) * rows, 128), F32),
            pltpu.SemaphoreType.DMA((3,)),
        ],
    )
    return out.reshape(levels, rows, width), coefficients.reshape(2)


def solution(mesh):
    in_specs = (
        P(None, "tile", None),
        P(None, "tile", None),
        P(),
        P("mem", None, "tile", None),
        P(),
        P(),
    )
    out_specs = (P(None, "tile", None), P())
    return jax.shard_map(
        per_device, mesh=mesh, in_specs=in_specs, out_specs=out_specs, check_vma=False
    )
```

time: 84.4 us -> 69.5 us (0.82)
  Pallas kernels: 41.2 us -> 21.7 us
  starting transfers between devices: 17.1 us -> 25.7 us
  local copies, waits for them, and re-layouts: 3.85 us -> 1.29 us
  waiting for transfers between devices: 20.5 us -> 18.7 us
    pallas_call x8 -> x10, Pallas kernels: 41.2 us -> 21.7 us  [call(): pl.pallas_call(kernel, out_shape=tuple((jax.ShapeDtypeStruct(shape, F32)...]
    ppermute x4, starting transfers between devices: 8.92 us -> 15 us  [per_device(): lax.ppermute(sums, 'tile', rotated('tile', digit, radix, by))]
    ppermute x2 -> x3, waiting for transfers between devices: 12.1 us -> 7.79 us  [edge_sum(): return (value, lax.ppermute(value, 'mem', flipped('mem', bits[-1])))]
    ppermute x1, waiting for transfers between devices: 1.34 us -> 4.24 us  [per_device(): mine = mine + lax.ppermute(mine, 'mem', flipped('mem', bit))]
    unnamed x16, local copies, waits for them, and re-layouts: 3.18 us -> 1.29 us
    ppermute x1, waiting for transfers between devices: 1.58 us -> 0.01 us  [per_device(): mine = mine + lax.ppermute(theirs, 'mem', flipped('mem', 1))]
    ppermute x2 -> x3, starting transfers between devices: 2.16 us -> 3.72 us  [edge_sum(): return (value, lax.ppermute(value, 'mem', flipped('mem', bits[-1])))]
    ppermute x2 -> x3, waiting for transfers between devices: 0.01 us -> 1.29 us  [edge_sum(): value = value + lax.ppermute(value, 'mem', flipped('mem', bit))]
  transfers between devices with their start and end apart: 13 -> 16, of which waited for: 7 -> 7; matrix products, arithmetic and copies ran while one was open for 0% -> 0% of each run, Pallas kernels for 45% -> 23%
where the time goes in v2:
time: 69.5 us; the launch traced here: 69.3 us
  starting transfers between devices  25.7 us (37%)
  Pallas kernels  21.7 us (31%)
  waiting for transfers between devices  18.7 us (27%)
  between operations  1.68 us (2%)
  local copies, waits for them, and re-layouts  1.29 us (2%)
    pallas_call x10, Pallas kernels, call(): pl.pallas_call(kernel, out_shape=tuple((jax.ShapeDtypeStruct(shape, F32)...  21.7 us
    ppermute x4, starting transfers between devices, per_device(): lax.ppermute(sums, 'tile', rotated('tile', digit, radix, by))  15 us
    ppermute x3, waiting for transfers between devices, edge_sum(): return (value, lax.ppermute(value, 'mem', flipped('mem', bits[-1])))  7.79 us
    ppermute x4, waiting for transfers between devices, per_device(): lax.ppermute(sums, 'tile', rotated('tile', digit, radix, by))  5.41 us
    ppermute x1, waiting for transfers between devices, per_device(): mine = mine + lax.ppermute(mine, 'mem', flipped('mem', bit))  4.24 us
    ppermute x3, starting transfers between devices, edge_sum(): return (value, lax.ppermute(value, 'mem', flipped('mem', bits[-1])))  3.72 us
    ppermute x1, starting transfers between devices, per_device(): near_halo = lax.ppermute(near_edge, 'tile', near_pairs)  3.03 us
    ppermute x1, starting transfers between devices, per_device(): mine = mine + lax.ppermute(mine, 'mem', flipped('mem', bit))  1.56 us
  transfers between devices with their start and end apart: 16, of which 7 were waited for; matrix products, arithmetic and copies ran while one was open for 0% of the time, Pallas kernels for 23%

profile of v2, /device:TPU:0, one launch (start us, length us, event | category | flops | bytes accessed | tf_op | source)
XLA Modules:
  0.0 69.3 jit_solution(2489236956626355022)
XLA Ops:
  0.7 3.6 %shard_map.105 = f32[2,2,280,128]{3,2,1,0:T(8,128)} custom-call(s32[1,70]{1,0:T(1,128)} %bitcast.10, bf16[2,70,16,256]{3,2,1,0:T(8,128)(2,1)} %members_hbm.3, f32[70,16,256]{2,1,0:T(8,128)} %inc_hbm.3, bf16[256,256]{1,0:T(8,128)(2,1)} %constant.6.clone.s_high_ref.s_high_hbm, bf16[256,256]{1,0:T(8,128)(2,1)} %constant.7.clone.s_low_ref.s_low_hbm), custom_call_target="tpu_custom_call" | custom-call | tf_op jit(solution)/shard_map/pallas_call | solution.py:402
  4.3 3.0 %collective-permute-start.3 = (f32[2,2,280,128]{3,2,1,0:T(8,128)}, f32[2,2,280,128]{3,2,1,0:T(8,128)S(1)}, u32[]{:S(2)}, u32[]{:S(2)}) collective-permute-start(f32[2,2,280,128]{3,2,1,0:T(8,128)} %shard_map.105), channel_id=1, source_target_pairs={{0,1},{1,0},{2,3},{3,2},{4,5},{5,4},{6,7},{7,6},{8,9},{9,8},{10,11... | collective-permute-start | bytes 1720328 | tf_op jit(solution)/shard_map/ppermute | solution.py:483
  7.4 1.2 %copy-done.4 = f32[70,16,256]{2,1,0:T(8,128)S(1)} copy-done((f32[70,16,256]{2,1,0:T(8,128)S(1)}, f32[70,16,256]{2,1,0:T(8,128)}, u32[]{:S(2)}) %copy-start.4) | copy-done | bytes 1146904
  8.7 9.7 %shard_map.104 = (f32[4,72,256]{2,1,0:T(8,128)S(1)}, f32[4,72,256]{2,1,0:T(8,128)S(1)}, f32[4,72,256]{2,1,0:T(8,128)S(1)}, f32[4,72,256]{2,1,0:T(8,128)S(1)}, f3...) custom-call(s32[1,70]{1,0:T(1,128)S(1)} %bitcast.11, ...), custom_call_target="tpu_custom_call" | custom-call | flops 200000000 | bytes 10000000 | tf_op jit(solution)/shard_map/pallas_call | solution.py:402
  18.4 0.1 collective-permute-start
  18.5 2.1 %shard_map.107 = (f32[2,2,192,128]{3,2,1,0:T(8,128)S(1)}, f32[2,2,88,128]{3,2,1,0:T(8,128)S(1)}) custom-call(s32[1,70]{1,0:T(1,128)S(1)} %bitcast.12, bf16[2,70,16,256]{3,2,1,0:T(8,128)(2,1)S(1)} %copy-done.1, f32[70,16,256]{2,1,0:T(8,128)S(1)} %copy-done, bf16[256,256]{1,0:T(8,128)(2,1)S(1)} %copy-done.3, bf16[256,256]{1,0:T(8,128)(2,1)S(1)} %copy-done.2), custom_call_target="tpu_custom_call" | custom-call | tf_op jit(solution)/shard_map/pallas_call | solution.py:402
  20.6 0.7 collective-permute-start.6
  21.3 1.6 %collective-permute-start.1 = (f32[4,72,256]{2,1,0:T(8,128)S(1)}, f32[4,72,256]{2,1,0:T(8,128)S(1)}, u32[]{:S(2)}, u32[]{:S(2)}) collective-permute-start(f32[4,72,256]{2,1,0:T(8,128)S(1)} %add.15), channel_id=1, source_target_pairs={{0,16},{8,24},{16,0},{24,8},{1,17},{9,25},{17,1},{25,9},{2,18},{10... | collective-permute-start | bytes 884744 | tf_op jit(solution)/shard_map/ppermute | solution.py:501
  22.9 1.2 %shard_map.106 = f32[4,72,256]{2,1,0:T(8,128)S(1)} custom-call(s32[8]{0:T(128)S(1)} %copy-done.6, f32[2,2,280,128]{3,2,1,0:T(8,128)S(1)} %collective-permute-done.3.halo_ref, f32[2,4,72,256]{3,2,1,0:T(8,128)S(1)} %get-tuple-element.20.mem_ref, f32[4,72,256]{2,1,0:T(8,128)S(1)} %get-tuple-element.21.cov_ref, bf16[256,256]{1,0:T(8,128)(2,1)S(1)} %copy-done.3, ...), custom_call_target="tpu_custom_call" | custom-call | tf_op jit(solution)/shard_map/pallas_call | solution.py:402
  24.0 0.3 collective-permute-start.4
  24.3 1.0 %shard_map.108 = f32[4,48,256]{2,1,0:T(8,128)S(1)} custom-call(s32[8]{0:T(128)S(1)} %copy-done.6, f32[2,2,192,128]{3,2,1,0:T(8,128)S(1)} %collective-permute-done.6.halo_ref, f32[2,4,72,256]{3,2,1,0:T(8,128)S(1)} %get-tuple-element.23.mem_ref, f32[4,72,256]{2,1,0:T(8,128)S(1)} %get-tuple-element.24.cov_ref, bf16[256,256]{1,0:T(8,128)(2,1)S(1)} %copy-done.3, ...), custom_call_target="tpu_custom_call" | custom-call | tf_op jit(solution)/shard_map/pallas_call | solution.py:402
  25.3 0.4 collective-permute-start.7
  25.7 0.8 %collective-permute-start.9 = (f32[2,2,88,128]{3,2,1,0:T(8,128)S(1)}, f32[2,2,88,128]{3,2,1,0:T(8,128)S(1)}, u32[]{:S(2)}, u32[]{:S(2)}) collective-permute-start(f32[2,2,88,128]{3,2,1,0:T(8,128)S(1)} %get-tuple-element.28), channel_id=1, source_target_pairs={{1,2},{2,1},{3,4},{4,3},{5,6},{6,5},{9,10},{10,9},{11,12},{12,11},... | collective-permute-start | bytes 540680 | tf_op jit(solution)/shard_map/ppermute | solution.py:485
  26.5 4.2 %collective-permute-done.1 = f32[4,72,256]{2,1,0:T(8,128)S(1)} collective-permute-done((f32[4,72,256]{2,1,0:T(8,128)S(1)}, f32[4,72,256]{2,1,0:T(8,128)S(1)}, u32[]{:S(2)}, u32[]{:S(2)}) %collective-permute-start.1) | collective-permute-done | bytes 294944 | tf_op jit(solution)/shard_map/ppermute | solution.py:501
  31.0 1.6 %collective-permute-start.5 = (f32[4,72,256]{2,1,0:T(8,128)S(1)}, f32[4,72,256]{2,1,0:T(8,128)S(1)}, u32[]{:S(2)}, u32[]{:S(2)}) collective-permute-start(f32[4,72,256]{2,1,0:T(8,128)S(1)} %add.17.near_a_ref), channel_id=1, source_target_pairs={{0,16},{8,24},{16,0},{24,8},{1,17},{9,25},{17,1},{25,9},{2,18},{10... | collective-permute-start | bytes 884744 | tf_op jit(solution)/shard_map/ppermute | solution.py:515
  32.5 0.6 collective-permute-start.8
  33.1 0.9 %shard_map.110 = f32[4,24,256]{2,1,0:T(8,128)S(1)} custom-call(s32[8]{0:T(128)S(1)} %copy-done.6, f32[2,2,88,128]{3,2,1,0:T(8,128)S(1)} %collective-permute-done.9.halo_ref, f32[2,4,72,256]{3,2,1,0:T(8,128)S(1)} %get-tuple-element.23.mem_ref, f32[4,72,256]{2,1,0:T(8,128)S(1)} %get-tuple-element.24.cov_ref, bf16[256,256]{1,0:T(8,128)(2,1)S(1)} %copy-done.3, ...), custom_call_target="tpu_custom_call" | custom-call | tf_op jit(solution)/shard_map/pallas_call | solution.py:402
  34.0 0.1 collective-permute-start.10
  34.1 1.3 %collective-permute-done.10 = f32[4,24,256]{2,1,0:T(8,128)S(1)} collective-permute-done((f32[4,24,256]{2,1,0:T(8,128)S(1)}, f32[4,24,256]{2,1,0:T(8,128)S(1)}, u32[]{:S(2)}, u32[]{:S(2)}) %collective-permute-start.10) | collective-permute-done | bytes 98336 | tf_op jit(solution)/shard_map/ppermute | solution.py:514
  35.4 1.6 %collective-permute-start.11 = (f32[4,24,256]{2,1,0:T(8,128)S(1)}, f32[4,24,256]{2,1,0:T(8,128)S(1)}, u32[]{:S(2)}, u32[]{:S(2)}) collective-permute-start(f32[4,24,256]{2,1,0:T(8,128)S(1)} %add.19.cov_a_ref), channel_id=1, source_target_pairs={{0,16},{8,24},{16,0},{24,8},{1,17},{9,25},{17,1},{25,9},{2,18},{10... | collective-permute-start | bytes 294920 | tf_op jit(solution)/shard_map/ppermute | solution.py:515
  37.6 7.4 %collective-permute-done.8.far_b_ref = f32[4,48,256]{2,1,0:T(8,128)S(1)} collective-permute-done((f32[4,48,256]{2,1,0:T(8,128)S(1)}, f32[4,48,256]{2,1,0:T(8,128)S(1)}, u32[]{:S(2)}, u32[]{:S(2)}) %collective-permute-start.8) | collective-permute-done | bytes 196640 | tf_op jit(solution)/shard_map/ppermute | solution.py:515
  45.0 1.3 %shard_map.109 = (f32[2,1120,128]{2,1,0:T(8,128)S(1)}, f32[8,128]{1,0:T(8,128)S(1)}) custom-call(f32[1]{0:T(128)S(6)} %copy.11.beta_ref, f32[4,72,256]{2,1,0:T(8,128)S(1)} %add.16.mine_ref, f32[4,72,256]{2,1,0:T(8,128)S(1)} %collective-permute-done.2.other_ref, f32[4,72,256]{2,1,0:T(8,128)S(1)} %add.17.near_a_ref, ...), custom_call_target="tpu_custom_call" | custom-call | tf_op jit(solution)/shard_map/pallas_call | solution.py:402
  46.4 0.4 collective-permute-done.11.cov_b_ref
  46.7 0.2 shard_map.111
  47.0 10.4 %collective-permute-start.12 = (f32[8,128]{1,0:T(8,128)S(1)}, f32[8,128]{1,0:T(8,128)S(1)}, u32[]{:S(2)}, u32[]{:S(2)}) collective-permute-start(f32[8,128]{1,0:T(8,128)S(1)} %get-tuple-element.29.refs_0_), channel_id=1, source_target_pairs={{0,1},{1,0},{2,3},{3,2},{4,5},{5,4},{6,7},{7,6},{8,9},{9,8},{10,11... | collective-permute-start | bytes 12296 | tf_op jit(solution)/shard_map/ppermute | solution.py:536
  57.3 1.6 %collective-permute-done.12.refs_1_ = f32[8,128]{1,0:T(8,128)S(1)} collective-permute-done((f32[8,128]{1,0:T(8,128)S(1)}, f32[8,128]{1,0:T(8,128)S(1)}, u32[]{:S(2)}, u32[]{:S(2)}) %collective-permute-start.12) | collective-permute-done | bytes 4128 | tf_op jit(solution)/shard_map/ppermute | solution.py:536
  58.9 3.0 %collective-permute-start.15 = (f32[8,128]{1,0:T(8,128)S(1)}, f32[8,128]{1,0:T(8,128)S(1)}, u32[]{:S(2)}, u32[]{:S(2)}) collective-permute-start(f32[8,128]{1,0:T(8,128)S(1)} %shard_map.112.refs_0_), channel_id=1, source_target_pairs={{0,6},{1,7},{2,0},{3,1},{4,2},{5,3},{6,4},{7,5},{8,14},{9,15},{10,... | collective-permute-start | bytes 12296 | tf_op jit(solution)/shard_map/ppermute | solution.py:536
  61.9 0.1 collective-permute-start.14
  62.0 1.6 %collective-permute-start.13 = (f32[8,128]{1,0:T(8,128)S(1)}, f32[8,128]{1,0:T(8,128)S(1)}, u32[]{:S(2)}, u32[]{:S(2)}) collective-permute-start(f32[8,128]{1,0:T(8,128)S(1)} %shard_map.112.refs_0_), channel_id=1, source_target_pairs={{0,2},{1,3},{2,4},{3,5},{4,6},{5,7},{6,0},{7,1},{8,10},{9,11},{10,... | collective-permute-start | bytes 12296 | tf_op jit(solution)/shard_map/ppermute | solution.py:536
  63.6 2.8 %collective-permute-done.14.refs_2_ = f32[8,128]{1,0:T(8,128)S(1)} collective-permute-done((f32[8,128]{1,0:T(8,128)S(1)}, f32[8,128]{1,0:T(8,128)S(1)}, u32[]{:S(2)}, u32[]{:S(2)}) %collective-permute-start.14) | collective-permute-done | bytes 4128 | tf_op jit(solution)/shard_map/ppermute | solution.py:536
  66.4 1.0 %collective-permute-done.13.refs_1_ = f32[8,128]{1,0:T(8,128)S(1)} collective-permute-done((f32[8,128]{1,0:T(8,128)S(1)}, f32[8,128]{1,0:T(8,128)S(1)}, u32[]{:S(2)}, u32[]{:S(2)}) %collective-permute-start.13) | collective-permute-done | bytes 4128 | tf_op jit(solution)/shard_map/ppermute | solution.py:536
  67.4 1.7 %shard_map.113 = (f32[1120,256]{1,0:T(8,128)}, f32[1,2]{1,0:T(1,128)}) custom-call(f32[8,128]{1,0:T(8,128)S(1)} %shard_map.112.refs_0_, f32[8,128]{1,0:T(8,128)S(1)} %collective-permute-done.13.refs_1_, f32[8,128]{1,0:T(8,128)S(1)} %collective-permute-done.14.refs_2_, f32[8,128]{1,0:T(8,128)S(1)} %collective-permute-done.15.refs_3_, ...), custom_call_target="tpu_custom_call" | custom-call | tf_op jit(solution)/shard_map/pallas_call | solution.py:402
  (31 shorter events, 0.3 us)
Async XLA Ops:
  0.6 6.7 %copy-start = (f32[70,16,256]{2,1,0:T(8,128)S(1)}, f32[70,16,256]{2,1,0:T(8,128)}, u32[]{:S(2)}) copy-start(f32[70,16,256]{2,1,0:T(8,128)} %inc_hbm.3) | copy-start | bytes 3440644
  0.6 6.7 %copy-start.1 = (bf16[2,70,16,256]{3,2,1,0:T(8,128)(2,1)S(1)}, bf16[2,70,16,256]{3,2,1,0:T(8,128)(2,1)}, u32[]{:S(2)}) copy-start(bf16[2,70,16,256]{3,2,1,0:T(8,128)(2,1)} %members_hbm.3) | copy-start | bytes 3440644
  0.7 6.7 %copy-start.2 = (bf16[256,256]{1,0:T(8,128)(2,1)S(1)}, bf16[256,256]{1,0:T(8,128)(2,1)}, u32[]{:S(2)}) copy-start(bf16[256,256]{1,0:T(8,128)(2,1)} %constant.7.clone.s_low_ref.s_low_hbm) | copy-start | bytes 393220
  0.7 6.7 %copy-start.3 = (bf16[256,256]{1,0:T(8,128)(2,1)S(1)}, bf16[256,256]{1,0:T(8,128)(2,1)}, u32[]{:S(2)}) copy-start(bf16[256,256]{1,0:T(8,128)(2,1)} %constant.6.clone.s_high_ref.s_high_hbm) | copy-start | bytes 393220
  0.7 6.7 %copy-start.5 = (f32[8,256]{1,0:T(8,128)S(1)}, f32[8,256]{1,0:T(8,128)}, u32[]{:S(2)}) copy-start(f32[8,256]{1,0:T(8,128)} %constant.8.clone.waves_ref) | copy-start | bytes 24580
  0.7 6.7 %copy-start.6 = (s32[8]{0:T(128)S(1)}, s32[8]{0:T(128)}, u32[]{:S(2)}) copy-start(s32[8]{0:T(128)} %steps_ref.7) | copy-start | bytes 100
  0.7 6.7 %copy-start.7 = (s32[70]{0:T(128)S(1)}, s32[70]{0:T(128)}, u32[]{:S(2)}) copy-start(s32[70]{0:T(128)} %param.13) | copy-start | bytes 844
  4.3 18.6 %collective-permute-start.3 = (f32[2,2,280,128]{3,2,1,0:T(8,128)}, f32[2,2,280,128]{3,2,1,0:T(8,128)S(1)}, u32[]{:S(2)}, u32[]{:S(2)}) collective-permute-start(f32[2,2,280,128]{3,2,1,0:T(8,128)} %shard_map.105), channel_id=1, source_target_pairs={{0,1},{1,0},{2,3},{3,2},{4,5},{5,4},{6,7},{7,6},{8,9},{9,8},{10,11... | collective-permute-start | bytes 1720328 | tf_op jit(solution)/shard_map/ppermute | solution.py:483
  7.4 1.3 %copy-start.4 = (f32[70,16,256]{2,1,0:T(8,128)S(1)}, f32[70,16,256]{2,1,0:T(8,128)}, u32[]{:S(2)}) copy-start(f32[70,16,256]{2,1,0:T(8,128)} %param.10) | copy-start | bytes 3440644
  18.4 2.9 %collective-permute-start = (f32[4,72,256]{2,1,0:T(8,128)S(1)}, f32[4,72,256]{2,1,0:T(8,128)S(1)}, u32[]{:S(2)}, u32[]{:S(2)}) collective-permute-start(f32[4,72,256]{2,1,0:T(8,128)S(1)} %get-tuple-element.19), channel_id=1, source_target_pairs={{0,8},{8,0},{16,24},{24,16},{1,9},{9,1},{17,25},{25,17},{2,10},{10... | collective-permute-start | bytes 884744 | tf_op jit(solution)/shard_map/ppermute | solution.py:499
  20.6 3.8 %collective-permute-start.6 = (f32[2,2,192,128]{3,2,1,0:T(8,128)S(1)}, f32[2,2,192,128]{3,2,1,0:T(8,128)S(1)}, u32[]{:S(2)}, u32[]{:S(2)}) collective-permute-start(f32[2,2,192,128]{3,2,1,0:T(8,128)S(1)} %get-tuple-element.22), channel_id=1, source_target_pairs={{1,2},{2,1},{3,4},{4,3},{5,6},{6,5},{9,10},{10,9},{11,12},{12,11},... | collective-permute-start | bytes 1179656 | tf_op jit(solution)/shard_map/ppermute | solution.py:485
  21.3 9.5 %collective-permute-start.1 = (f32[4,72,256]{2,1,0:T(8,128)S(1)}, f32[4,72,256]{2,1,0:T(8,128)S(1)}, u32[]{:S(2)}, u32[]{:S(2)}) collective-permute-start(f32[4,72,256]{2,1,0:T(8,128)S(1)} %add.15), channel_id=1, source_target_pairs={{0,16},{8,24},{16,0},{24,8},{1,17},{9,25},{17,1},{25,9},{2,18},{10... | collective-permute-start | bytes 884744 | tf_op jit(solution)/shard_map/ppermute | solution.py:501
  24.0 6.8 %collective-permute-start.4 = (f32[4,72,256]{2,1,0:T(8,128)S(1)}, f32[4,72,256]{2,1,0:T(8,128)S(1)}, u32[]{:S(2)}, u32[]{:S(2)}) collective-permute-start(f32[4,72,256]{2,1,0:T(8,128)S(1)} %shard_map.106), channel_id=1, source_target_pairs={{0,8},{8,0},{16,24},{24,16},{1,9},{9,1},{17,25},{25,17},{2,10},{10... | collective-permute-start | bytes 884744 | tf_op jit(solution)/shard_map/ppermute | solution.py:514
  25.3 7.2 %collective-permute-start.7 = (f32[4,48,256]{2,1,0:T(8,128)S(1)}, f32[4,48,256]{2,1,0:T(8,128)S(1)}, u32[]{:S(2)}, u32[]{:S(2)}) collective-permute-start(f32[4,48,256]{2,1,0:T(8,128)S(1)} %shard_map.108), channel_id=1, source_target_pairs={{0,8},{8,0},{16,24},{24,16},{1,9},{9,1},{17,25},{25,17},{2,10},{10... | collective-permute-start | bytes 589832 | tf_op jit(solution)/shard_map/ppermute | solution.py:514
  25.7 7.5 %collective-permute-start.9 = (f32[2,2,88,128]{3,2,1,0:T(8,128)S(1)}, f32[2,2,88,128]{3,2,1,0:T(8,128)S(1)}, u32[]{:S(2)}, u32[]{:S(2)}) collective-permute-start(f32[2,2,88,128]{3,2,1,0:T(8,128)S(1)} %get-tuple-element.28), channel_id=1, source_target_pairs={{1,2},{2,1},{3,4},{4,3},{5,6},{6,5},{9,10},{10,9},{11,12},{12,11},... | collective-permute-start | bytes 540680 | tf_op jit(solution)/shard_map/ppermute | solution.py:485
  30.8 14.2 %collective-permute-start.2 = (f32[4,72,256]{2,1,0:T(8,128)S(1)}, f32[4,72,256]{2,1,0:T(8,128)S(1)}, u32[]{:S(2)}, u32[]{:S(2)}) collective-permute-start(f32[4,72,256]{2,1,0:T(8,128)S(1)} %add.16.mine_ref), channel_id=1, source_target_pairs={{0,8},{8,0},{16,24},{24,16},{1,9},{9,1},{17,25},{25,17},{2,10},{10... | collective-permute-start | bytes 884744 | tf_op jit(solution)/shard_map/ppermute | solution.py:502
  31.0 14.1 %collective-permute-start.5 = (f32[4,72,256]{2,1,0:T(8,128)S(1)}, f32[4,72,256]{2,1,0:T(8,128)S(1)}, u32[]{:S(2)}, u32[]{:S(2)}) collective-permute-start(f32[4,72,256]{2,1,0:T(8,128)S(1)} %add.17.near_a_ref), channel_id=1, source_target_pairs={{0,16},{8,24},{16,0},{24,8},{1,17},{9,25},{17,1},{25,9},{2,18},{10... | collective-permute-start | bytes 884744 | tf_op jit(solution)/shard_map/ppermute | solution.py:515
  32.5 12.5 %collective-permute-start.8 = (f32[4,48,256]{2,1,0:T(8,128)S(1)}, f32[4,48,256]{2,1,0:T(8,128)S(1)}, u32[]{:S(2)}, u32[]{:S(2)}) collective-permute-start(f32[4,48,256]{2,1,0:T(8,128)S(1)} %add.18.far_a_ref), channel_id=1, source_target_pairs={{0,16},{8,24},{16,0},{24,8},{1,17},{9,25},{17,1},{25,9},{2,18},{10... | collective-permute-start | bytes 589832 | tf_op jit(solution)/shard_map/ppermute | solution.py:515
  34.0 1.4 %collective-permute-start.10 = (f32[4,24,256]{2,1,0:T(8,128)S(1)}, f32[4,24,256]{2,1,0:T(8,128)S(1)}, u32[]{:S(2)}, u32[]{:S(2)}) collective-permute-start(f32[4,24,256]{2,1,0:T(8,128)S(1)} %shard_map.110), channel_id=1, source_target_pairs={{0,8},{8,0},{16,24},{24,16},{1,9},{9,1},{17,25},{25,17},{2,10},{10... | collective-permute-start | bytes 294920 | tf_op jit(solution)/shard_map/ppermute | solution.py:514
  35.4 11.3 %collective-permute-start.11 = (f32[4,24,256]{2,1,0:T(8,128)S(1)}, f32[4,24,256]{2,1,0:T(8,128)S(1)}, u32[]{:S(2)}, u32[]{:S(2)}) collective-permute-start(f32[4,24,256]{2,1,0:T(8,128)S(1)} %add.19.cov_a_ref), channel_id=1, source_target_pairs={{0,16},{8,24},{16,0},{24,8},{1,17},{9,25},{17,1},{25,9},{2,18},{10... | collective-permute-start | bytes 294920 | tf_op jit(solution)/shard_map/ppermute | solution.py:515
  47.0 12.0 %collective-permute-start.12 = (f32[8,128]{1,0:T(8,128)S(1)}, f32[8,128]{1,0:T(8,128)S(1)}, u32[]{:S(2)}, u32[]{:S(2)}) collective-permute-start(f32[8,128]{1,0:T(8,128)S(1)} %get-tuple-element.29.refs_0_), channel_id=1, source_target_pairs={{0,1},{1,0},{2,3},{3,2},{4,5},{5,4},{6,7},{7,6},{8,9},{9,8},{10,11... | collective-permute-start | bytes 12296 | tf_op jit(solution)/shard_map/ppermute | solution.py:536
  58.9 4.7 %collective-permute-start.15 = (f32[8,128]{1,0:T(8,128)S(1)}, f32[8,128]{1,0:T(8,128)S(1)}, u32[]{:S(2)}, u32[]{:S(2)}) collective-permute-start(f32[8,128]{1,0:T(8,128)S(1)} %shard_map.112.refs_0_), channel_id=1, source_target_pairs={{0,6},{1,7},{2,0},{3,1},{4,2},{5,3},{6,4},{7,5},{8,14},{9,15},{10,... | collective-permute-start | bytes 12296 | tf_op jit(solution)/shard_map/ppermute | solution.py:536
  61.9 4.5 %collective-permute-start.14 = (f32[8,128]{1,0:T(8,128)S(1)}, f32[8,128]{1,0:T(8,128)S(1)}, u32[]{:S(2)}, u32[]{:S(2)}) collective-permute-start(f32[8,128]{1,0:T(8,128)S(1)} %shard_map.112.refs_0_), channel_id=1, source_target_pairs={{0,4},{1,5},{2,6},{3,7},{4,0},{5,1},{6,2},{7,3},{8,12},{9,13},{10,... | collective-permute-start | bytes 12296 | tf_op jit(solution)/shard_map/ppermute | solution.py:536
  62.0 5.4 %collective-permute-start.13 = (f32[8,128]{1,0:T(8,128)S(1)}, f32[8,128]{1,0:T(8,128)S(1)}, u32[]{:S(2)}, u32[]{:S(2)}) collective-permute-start(f32[8,128]{1,0:T(8,128)S(1)} %shard_map.112.refs_0_), channel_id=1, source_target_pairs={{0,2},{1,3},{2,4},{3,5},{4,6},{5,7},{6,0},{7,1},{8,10},{9,11},{10,... | collective-permute-start | bytes 12296 | tf_op jit(solution)/shard_map/ppermute | solution.py:536

commit v3 on v2

--- a/solution.py
+++ b/solution.py
@@ -109,11 +109,10 @@
 
 
 def edge_kernel(
-    near, rows, levels, cuts,
-    bands_hbm, members_hbm, inc_hbm, s_high_hbm, s_low_hbm, *refs,
+    near, rows, levels,
+    bands_hbm, members_hbm, inc_hbm, s_high_hbm, s_low_hbm, out_ref,
+    bands_ref, mem_ref, inc_ref, s_high_ref, s_low_ref, prod_ref, pad_ref, sems,
 ):
-    out_refs = refs[: len(cuts)]
-    bands_ref, mem_ref, inc_ref, s_high_ref, s_low_ref, prod_ref, pad_ref, sems = refs[len(cuts) :]
     tile = lax.axis_index("tile")
     high_end = (tile % 2 == 0) == near
     start = pl.multiple_of(jnp.where(high_end, rows - 8, 0), 8)
@@ -144,10 +143,9 @@
             copies[3 + owned].wait()
         waves = transform(jnp.concatenate(local, axis=0), s_high_ref[...], s_low_ref[...])
         for q in range(DIFF):
-            for (low, high), out_ref in zip(cuts, out_refs):
-                for piece in range(width // 128):
-                    part = waves[q * tall + low : q * tall + high, piece * 128 : (piece + 1) * 128]
-                    out_ref[m, piece, pl.ds(q, high - low, stride=DIFF), :] = part
+            for piece in range(width // 128):
+                part = waves[q * tall : q * tall + levels, piece * 128 : (piece + 1) * 128]
+                out_ref[m, piece, pl.ds(q, levels, stride=DIFF), :] = part
 
 
 def own_kernel(
@@ -225,20 +223,20 @@
 
 
 def halo_kernel(
-    near, tiles, cut,
-    steps_ref, halo_ref, mem_ref, cov_ref, s_high_ref, s_low_ref, waves_ref, out_ref, spec_ref, base_ref,
+    near, levels, tiles,
+    steps_ref, halo_ref, mem_ref, cov_ref, s_high_ref, s_low_ref, waves_ref, *refs,
 ):
+    out_refs, (spec_ref, base_ref) = refs[:-2], refs[-2:]
     counts = sweep_counts(steps_ref, lax.axis_index("tile"), tiles)
-    owned, width = halo_ref.shape[0], cov_ref.shape[-1]
-    low, high = cut
-    count, tall = high - low, up_to(high - low, 8)
+    owned, tall, width = halo_ref.shape[0], cov_ref.shape[1], cov_ref.shape[2]
     rate = [[coefficient(k, counts[0]), coefficient(k, counts[1 if near else 2])] for k in range(DIFF)]
     for k in range(DIFF):
         for side in range(2):
             base_ref[k, side] = base_of(rate[k][side], waves_ref[...])
+    sums = [cov_ref[q] for q in range(DIFF)]
     for m in range(owned):
-        for at in range(0, count, 8):
-            size = min(8, count - at)
+        for at in range(0, levels, 8):
+            size = min(8, levels - at)
             field = {q: strided(halo_ref.at[m], q + DIFF * at, size, DIFF) for q in range(DIFF)}
             for k in range(DIFF):
                 kept = range(-1 - k, DIFF - 1 - k)
@@ -246,14 +244,28 @@
                 field = advance(field, {p: rate[k][0 if p < 0 else 1] for p in kept}, bases)
             for q in range(DIFF):
                 spec_ref[q, at : at + size, :] = field[-1 - q]
-        if count < tall:
+        if levels < tall:
             for q in range(DIFF):
-                spec_ref[q, count:, :] = jnp.zeros((tall - count, width), F32)
+                spec_ref[q, levels:, :] = jnp.zeros((tall - levels, width), F32)
         block = spec_ref[...].reshape(DIFF * tall, width)
         block = transform(block, s_high_ref[...], s_low_ref[...])
         for q in range(DIFF):
-            value = mem_ref[m, q, low : low + tall, :] * block[q * tall : (q + 1) * tall]
-            out_ref[q] = value + (cov_ref[q, low : low + tall, :] if m == 0 else out_ref[q])
+            sums[q] = sums[q] + mem_ref[m, q] * block[q * tall : (q + 1) * tall]
+    if len(out_refs) == 1:
+        for q in range(DIFF):
+            out_refs[0][q] = sums[q]
+        return
+    part = DIFF // 2
+    half = lax.axis_index("mem") % 2
+    for q in range(DIFF):
+
+        @pl.when(half == q // part)
+        def _(q=q):
+            out_refs[0][q % part] = sums[q]
+
+        @pl.when(half != q // part)
+        def _(q=q):
+            out_refs[1][q % part] = sums[q]
 
 
 def reduced(value):
@@ -269,15 +281,15 @@
     return jnp.where(some, top / jnp.where(some, bottom, F32(1.0)), F32(0.0))
 
 
-def put_row(ref, row, rows, low, value):
+def put_row(ref, row, rows, value):
     for piece in range(ref.shape[0]):
         part = value[:, piece * 128 : (piece + 1) * 128]
-        ref[piece, pl.ds(row + low * rows, value.shape[0], stride=rows), :] = part
+        ref[piece, pl.ds(row, value.shape[0], stride=rows), :] = part
 
 
 def bulk_kernel(
-    rows, levels, inverse, cut,
-    beta_ref, mine_ref, other_ref, near_a_ref, near_b_ref, far_a_ref, far_b_ref, inc_ref, prev_ref,
+    rows, levels, inverse,
+    beta_ref, mine_ref, other_ref, near_a_ref, near_b_ref, inc_ref, prev_ref,
     w_ref, sums_ref, keep_ref,
 ):
     beta = beta_ref[0]
@@ -287,8 +299,6 @@
     zero = jnp.zeros((8, inc_ref.shape[-1]), F32)
 
     def covariance(row):
-        if row < DIFF:
-            return far_a_ref[row] + far_b_ref[row]
         if row >= rows - DIFF:
             q = rows - 1 - row
             return near_a_ref[q] + near_b_ref[q]
@@ -296,22 +306,20 @@
         return jnp.where(own_half == which, mine_ref[q], other_ref[q])
 
     square, cross = zero, zero
-    for row in range(rows):
-        high = cut if row < DIFF else inc_ref.shape[1]
-        inc = inc_ref[row, :high]
+    for row in range(DIFF, rows):
+        inc = inc_ref[row]
         scaled = inverse * covariance(row)
         square = square + folded(inc * inc)
         cross = cross + folded(inc * scaled)
-        value = scaled - beta * prev_ref[row, :high]
-        keep_ref[row, :high] = value
-        put_row(w_ref, grid_row(tile, row, rows), rows, 0, value[: min(high, levels)])
+        value = scaled - beta * prev_ref[row]
+        keep_ref[row - DIFF] = value
+        put_row(w_ref, grid_row(tile, row, rows), rows, value[:levels])
     square, cross = reduced(square), reduced(cross)
     pivot = ratio(cross, square)
     mixed, rest = zero, zero
-    for row in range(rows):
-        high = cut if row < DIFF else inc_ref.shape[1]
-        inc = inc_ref[row, :high]
-        apart = keep_ref[row, :high] - pivot * inc
+    for row in range(DIFF, rows):
+        inc = inc_ref[row]
+        apart = keep_ref[row - DIFF] - pivot * inc
         mixed = mixed + folded(apart * inc)
         rest = rest + folded(apart * apart)
     store_sums(sums_ref, square, cross, reduced(mixed), reduced(rest), pivot)
@@ -329,15 +337,18 @@
     return [ref[index : index + 1, :] for index in range(5)]
 
 
-def last_kernel(inverse, cut, beta_ref, sums_ref, cov_a_ref, cov_b_ref, inc_ref, prev_ref, w_ref, out_ref):
+def last_kernel(inverse, beta_ref, sums_ref, mine_ref, other_ref, inc_ref, prev_ref, w_ref, out_ref):
+    own_half = lax.axis_index("mem") % 2
+    part = DIFF // 2
     beta = beta_ref[0]
     square0, cross0, mixed0, rest0, pivot0 = [value[:, 0:1] for value in load_sums(sums_ref)]
     zero = jnp.zeros((8, inc_ref.shape[-1]), F32)
     square, cross, mixed, rest = zero, zero, zero, zero
     for q in range(DIFF):
-        inc = inc_ref[q, cut:]
-        scaled = inverse * (cov_a_ref[q] + cov_b_ref[q])
-        value = scaled - beta * prev_ref[q, cut:]
+        inc = inc_ref[q]
+        which, index = divmod(q, part)
+        scaled = inverse * jnp.where(own_half == which, mine_ref[index], other_ref[index])
+        value = scaled - beta * prev_ref[q]
         w_ref[q] = value
         apart = value - pivot0 * inc
         square = square + folded(inc * inc)
@@ -366,35 +377,38 @@
     store_sums(refs[-1], *merged([load_sums(ref) for ref in refs[:-1]]))
 
 
-def final_kernel(rows, levels, cells, cut, count, *refs):
+def final_kernel(rows, levels, cells, count, *refs):
     sums_refs = refs[:count]
-    w_far_ref, w_ref, inc_ref, out_hbm, coef_ref, out_ref, end_ref, sems = refs[count:]
+    w_far_ref, w_ref, inc_t_ref, inc_ref, out_hbm, coef_ref, out_ref, sems = refs[count:]
     tile = lax.axis_index("tile")
     _, _, _, rest, pivot = merged([load_sums(ref) for ref in sums_refs])
     scale = jnp.sqrt(rest / cells + 1e-6)
     lane = lax.broadcasted_iota(jnp.int32, scale.shape, 1)
     coef_ref[...] = jnp.where(lane == 0, 1.0 + pivot, scale)[:, :2]
     over = 1.0 / scale
-    total, edge = rows * levels, rows * cut
-    end_ref[...] = w_ref[:, edge:, :]
-    for q in range(DIFF):
-        put_row(end_ref, grid_row(tile, q, rows), rows, 0, w_far_ref[q, : levels - cut])
-    bounds = [0, edge // 16 * 8, edge, total]
+    wide_pivot, wide_over = (jnp.concatenate([value] * w_ref.shape[0], axis=1) for value in (pivot, over))
+    step = up_to(up_to(levels, 8) // 4, 8)
     copies = []
-    for k in range(3):
-        low, high = bounds[k], bounds[k + 1]
+    for low in range(0, levels, step):
+        high = min(levels, low + step)
+        span = slice(low * rows, high * rows)
         for piece in range(w_ref.shape[0]):
             lanes = slice(piece * 128, (piece + 1) * 128)
-            w = end_ref[piece] if k == 2 else w_ref[piece, low:high, :]
-            out_ref[low:high, lanes] = (w - pivot * inc_ref[low:high, lanes]) * over
-        copies.append(pltpu.make_async_copy(out_ref.at[low:high], out_hbm.at[low:high], sems.at[k]))
-        copies[-1].start()
+            out_ref[piece, span, :] = (w_ref[piece, span, :] - pivot * inc_ref[span, lanes]) * over
+        for q in range(DIFF):
+            value = (w_far_ref[q, low:high] - wide_pivot * inc_t_ref[q, low:high]) * wide_over
+            put_row(out_ref, grid_row(tile, q, rows) + low * rows, rows, value)
+        for piece in range(w_ref.shape[0]):
+            lanes = slice(piece * 128, (piece + 1) * 128)
+            source, target = out_ref.at[piece, span, :], out_hbm.at[span, lanes]
+            copies.append(pltpu.make_async_copy(source, target, sems.at[len(copies)]))
+            copies[-1].start()
     for copy in copies:
         copy.wait()
 
 
 def call(kernel, ins, outs, scratch=(), cost=None, limit=VMEM_LIMIT):
-    spaces = {"s": pltpu.SMEM, "v": pltpu.VMEM, "h": pl.ANY}
+    spaces = {"s": pltpu.SMEM, "v": pltpu.VMEM, "h": pltpu.HBM}
     outs = [out if isinstance(out[0], str) else ("v", out) for out in outs]
     estimate = None
     if cost is not None:
@@ -445,13 +459,11 @@
     tiles, mems = lax.axis_size("tile"), lax.axis_size("mem")
     owned = members.shape[0]
     tall, deep = up_to(levels, 8), up_to(levels, 16)
-    cut = up_to(2 * levels // 3, 8)
     inverse = 1.0 / (owned * mems - 1)
     cells = levels * rows * tiles * width
     lanes = width // 128
     inc = increment.reshape(levels * rows, width)
     prev = previous.reshape(levels * rows, width)
-    mem = members.reshape(owned, levels * rows, width)
     bands = band_widths.reshape(1, levels)
     s_high, s_low, waves = sine_matrix(width)
     edge = (owned, DIFF, tall, width)
@@ -460,11 +472,11 @@
     far_pairs = [pair for i in range(1, tiles - 1, 2) for pair in ((i, i + 1), (i + 1, i))]
     pad = pltpu.VMEM((8, 128), F32)
 
-    def edges(near, cuts):
-        return call(
-            functools.partial(edge_kernel, near, rows, levels, cuts),
+    def edges(near):
+        (value,) = call(
+            functools.partial(edge_kernel, near, rows, levels),
             [("h", bands), ("h", members), ("h", increment), ("h", s_high), ("h", s_low)],
-            [(owned, lanes, DIFF * (high - low), 128) for low, high in cuts],
+            [(owned, lanes, DIFF * levels, 128)],
             [
                 pltpu.VMEM((1, levels), jnp.int32),
                 pltpu.VMEM((owned, levels, 8, width), jnp.bfloat16),
@@ -477,12 +489,14 @@
             ],
             limit=EDGE_LIMIT if near else VMEM_LIMIT,
         )
-
-    near_cut, far_cuts = (0, levels), [(0, cut), (cut, levels)]
-    (near_edge,) = edges(True, [near_cut])
+        return value
+
+    near_edge = edges(True)
     near_halo = lax.ppermute(near_edge, "tile", near_pairs)
-    far_edges = edges(False, far_cuts)
-    far_halos = [lax.ppermute(value, "tile", far_pairs) for value in far_edges]
+    far_edge = edges(False)
+    members, far_edge = lax.optimization_barrier((members, far_edge))
+    mem = members.reshape(owned, levels * rows, width)
+    far_halo = lax.ppermute(far_edge, "tile", far_pairs)
 
     piece, four = (part, tall, width), (DIFF, tall, width)
     mine, theirs, cov_near, cov_far, mem_near, mem_far, inc_t, prev_t = call(
@@ -501,34 +515,36 @@
         mine = mine + lax.ppermute(mine, "mem", flipped("mem", bit))
     other = lax.ppermute(mine, "mem", flipped("mem", 1))
 
-    def edge_sum(near, span, halo, mem_rows, cov):
-        size = up_to(span[1] - span[0], 8)
-        (value,) = call(
-            functools.partial(halo_kernel, near, tiles, span),
+    def edge_sum(near, halo, mem_rows, cov, outs):
+        return call(
+            functools.partial(halo_kernel, near, levels, tiles),
             [("s", diffusion_steps), ("v", halo), ("v", mem_rows), ("v", cov)]
             + [("v", s_high), ("v", s_low), ("v", waves)],
-            [(DIFF, size, width)],
-            [pltpu.VMEM((DIFF, size, width), F32), pltpu.VMEM((DIFF, 2, 8, width), F32)],
+            outs,
+            [pltpu.VMEM(four, F32), pltpu.VMEM((DIFF, 2, 8, width), F32)],
         )
-        for bit in [1] + bits[:-1]:
-            value = value + lax.ppermute(value, "mem", flipped("mem", bit))
-        return value, lax.ppermute(value, "mem", flipped("mem", bits[-1]))
-
-    near_sums = edge_sum(True, near_cut, near_halo, mem_near, cov_near)
-    far_sums = edge_sum(False, far_cuts[0], far_halos[0], mem_far, cov_far)
+
+    (near_sum,) = edge_sum(True, near_halo, mem_near, cov_near, [four])
+    for bit in [1] + bits[:-1]:
+        near_sum = near_sum + lax.ppermute(near_sum, "mem", flipped("mem", bit))
+    near_other = lax.ppermute(near_sum, "mem", flipped("mem", bits[-1]))
     w_rest, sums = call(
-        functools.partial(bulk_kernel, rows, levels, inverse, cut),
-        [("s", beta_prev), ("v", mine), ("v", other)]
-        + [("v", value) for value in near_sums + far_sums]
+        functools.partial(bulk_kernel, rows, levels, inverse),
+        [("s", beta_prev), ("v", mine), ("v", other), ("v", near_sum), ("v", near_other)]
         + [("v", inc_t), ("v", prev_t)],
         [(lanes, levels * rows, 128), (8, 128)],
-        [pltpu.VMEM((rows, tall, width), F32)],
-    )
-    last_sums = edge_sum(False, far_cuts[1], far_halos[1], mem_far, cov_far)
+        [pltpu.VMEM((rows - DIFF, tall, width), F32)],
+    )
+    two = (DIFF // 2, tall, width)
+    far_mine, far_theirs = edge_sum(False, far_halo, mem_far, cov_far, [two, two])
+    far_mine = far_mine + lax.ppermute(far_theirs, "mem", flipped("mem", 1))
+    for bit in bits:
+        far_mine = far_mine + lax.ppermute(far_mine, "mem", flipped("mem", bit))
+    far_other = lax.ppermute(far_mine, "mem", flipped("mem", 1))
     w_far, sums = call(
-        functools.partial(last_kernel, inverse, cut),
-        [("s", beta_prev), ("v", sums)] + [("v", value) for value in last_sums] + [("v", inc_t), ("v", prev_t)],
-        [(DIFF, tall - cut, width), (8, 128)],
+        functools.partial(last_kernel, inverse),
+        [("s", beta_prev), ("v", sums), ("v", far_mine), ("v", far_other), ("v", inc_t), ("v", prev_t)],
+        [four, (8, 128)],
     )
     digit = 1
     stages = radices(tiles)
@@ -538,14 +554,10 @@
             (sums,) = call(merge_kernel, [("v", value) for value in parts], [(8, 128)])
         digit *= radix
     out, coefficients = call(
-        functools.partial(final_kernel, rows, levels, cells, cut, len(parts)),
-        [("v", value) for value in parts] + [("v", w_far), ("v", w_rest), ("v", inc)],
+        functools.partial(final_kernel, rows, levels, cells, len(parts)),
+        [("v", value) for value in parts] + [("v", w_far), ("v", w_rest), ("v", inc_t), ("v", inc)],
         [("h", (levels * rows, width)), (1, 2)],
-        [
-            pltpu.VMEM((levels * rows, width), F32),
-            pltpu.VMEM((lanes, (levels - cut) * rows, 128), F32),
-            pltpu.SemaphoreType.DMA((3,)),
-        ],
+        [pltpu.VMEM((lanes, levels * rows, 128), F32), pltpu.SemaphoreType.DMA((4 * lanes,))],
     )
     return out.reshape(levels, rows, width), coefficients.reshape(2)
 

time: 69.5 us -> 64.5 us (0.928)
  starting transfers between devices: 25.7 us -> 17 us
  waiting for transfers between devices: 18.7 us -> 24.6 us
  local copies, waits for them, and re-layouts: 1.29 us -> 0.05 us
  Pallas kernels: 21.7 us -> 21 us
    ppermute x1, waiting for transfers between devices: 0.01 us -> 8.98 us  [per_device(): near_halo = lax.ppermute(near_edge, 'tile', near_pairs)]
    ppermute x4, starting transfers between devices: 15 us -> 8.51 us  [per_device(): lax.ppermute(sums, 'tile', rotated('tile', digit, radix, by))]
    ppermute x1, waiting for transfers between devices: 4.24 us -> 0.01 us  [per_device(): mine = mine + lax.ppermute(mine, 'mem', flipped('mem', bit))]
    ppermute x8 -> x6, starting transfers between devices: 5.96 us -> 3.77 us  [the longest x1 1.55 us: per_device(): near_other = lax.ppermute(near_sum, 'mem', flipped('mem', bits[-1]))]
    ppermute x4, waiting for transfers between devices: 5.41 us -> 3.84 us  [per_device(): lax.ppermute(sums, 'tile', rotated('tile', digit, radix, by))]
    ppermute x1, waiting for transfers between devices: 0.01 us -> 1.57 us  [per_device(): mine = mine + lax.ppermute(theirs, 'mem', flipped('mem', 1))]
    unnamed x16, local copies, waits for them, and re-layouts: 1.29 us -> 0.05 us
    ppermute x8 -> x6, waiting for transfers between devices: 9.08 us -> 10.2 us  [the longest x1 10.2 us: per_device(): far_mine = far_mine + lax.ppermute(far_mine, 'mem', flipped('mem', bit))]
  transfers between devices with their start and end apart: 16 -> 14, of which waited for: 7 -> 6; matrix products, arithmetic and copies ran while one was open for 0% -> 0% of each run, Pallas kernels for 23% -> 24%
where the time goes in v3:
time: 64.5 us; the launch traced here: 64.3 us
  waiting for transfers between devices  24.6 us (38%)
  Pallas kernels  21 us (33%)
  starting transfers between devices  17 us (26%)
  between operations  1.52 us (2%)
    pallas_call x9, Pallas kernels, call(): pl.pallas_call(kernel, out_shape=tuple((jax.ShapeDtypeStruct(shape, F32)...  21 us
    ppermute x1, waiting for transfers between devices, per_device(): far_mine = far_mine + lax.ppermute(far_mine, 'mem', flipped('mem', bit))  10.2 us
    ppermute x1, waiting for transfers between devices, per_device(): near_halo = lax.ppermute(near_edge, 'tile', near_pairs)  8.98 us
    ppermute x4, starting transfers between devices, per_device(): lax.ppermute(sums, 'tile', rotated('tile', digit, radix, by))  8.51 us
    ppermute x4, waiting for transfers between devices, per_device(): lax.ppermute(sums, 'tile', rotated('tile', digit, radix, by))  3.84 us
    ppermute x1, starting transfers between devices, per_device(): near_halo = lax.ppermute(near_edge, 'tile', near_pairs)  3.03 us
    ppermute x1, waiting for transfers between devices, per_device(): mine = mine + lax.ppermute(theirs, 'mem', flipped('mem', 1))  1.57 us
    ppermute x1, starting transfers between devices, per_device(): mine = mine + lax.ppermute(mine, 'mem', flipped('mem', bit))  1.56 us
  transfers between devices with their start and end apart: 14, of which 6 were waited for; matrix products, arithmetic and copies ran while one was open for 0% of the time, Pallas kernels for 24%

profile of v3, /device:TPU:0, one launch (start us, length us, event | category | flops | bytes accessed | tf_op | source)
XLA Modules:
  0.0 64.3 jit_solution(16999431374891949246)
XLA Ops:
  0.6 0.0 copy-start.2
  0.7 0.0 copy-start.3
  0.7 3.6 %shard_map.106 = f32[2,2,280,128]{3,2,1,0:T(8,128)} custom-call(s32[1,70]{1,0:T(1,128)} %bitcast.10, bf16[2,70,16,256]{3,2,1,0:T(8,128)(2,1)} %members_hbm.3, f32[70,16,256]{2,1,0:T(8,128)} %inc_hbm.3, bf16[256,256]{1,0:T(8,128)(2,1)} %constant.6.clone.s_high_hbm.s_high_ref, bf16[256,256]{1,0:T(8,128)(2,1)} %constant.7.clone.s_low_hbm.s_low_ref), custom_call_target="tpu_custom_call" | custom-call | tf_op jit(solution)/shard_map/pallas_call | solution.py:416
  4.3 0.0 copy-start.4
  4.3 0.0 copy-start.5
  4.3 3.0 %collective-permute-start.3 = (f32[2,2,280,128]{3,2,1,0:T(8,128)}, f32[2,2,280,128]{3,2,1,0:T(8,128)S(1)}, u32[]{:S(2)}, u32[]{:S(2)}) collective-permute-start(f32[2,2,280,128]{3,2,1,0:T(8,128)} %shard_map.106), channel_id=1, source_target_pairs={{0,1},{1,0},{2,3},{3,2},{4,5},{5,4},{6,7},{7,6},{8,9},{9,8},{10,11... | collective-permute-start | bytes 1720328 | tf_op jit(solution)/shard_map/ppermute | solution.py:495
  7.4 2.1 %shard_map.104 = f32[2,2,280,128]{3,2,1,0:T(8,128)S(1)} custom-call(s32[1,70]{1,0:T(1,128)S(1)} %bitcast.11, bf16[2,70,16,256]{3,2,1,0:T(8,128)(2,1)S(1)} %copy-done.1, f32[70,16,256]{2,1,0:T(8,128)S(1)} %copy-done, bf16[256,256]{1,0:T(8,128)(2,1)S(1)} %copy-done.2, bf16[256,256]{1,0:T(8,128)(2,1)S(1)} %copy-done.3), custom_call_target="tpu_custom_call" | custom-call | tf_op jit(solution)/shard_map/pallas_call | solution.py:416
  9.5 0.7 %collective-permute-start.6 = (f32[2,2,280,128]{3,2,1,0:T(8,128)S(1)}, f32[2,2,280,128]{3,2,1,0:T(8,128)S(1)}, u32[]{:S(2)}, u32[]{:S(2)}) collective-permute-start(f32[2,2,280,128]{3,2,1,0:T(8,128)S(1)} %shard_map.104), channel_id=1, source_target_pairs={{1,2},{2,1},{3,4},{4,3},{5,6},{6,5},{9,10},{10,9},{11,12},{12,11},... | collective-permute-start | bytes 1720328 | tf_op jit(solution)/shard_map/ppermute | solution.py:499
  10.2 9.8 %shard_map.105 = (f32[4,72,256]{2,1,0:T(8,128)S(1)}, f32[4,72,256]{2,1,0:T(8,128)S(1)}, f32[4,72,256]{2,1,0:T(8,128)S(1)}, f32[4,72,256]{2,1,0:T(8,128)S(1)}, f3...) custom-call(s32[1,70]{1,0:T(1,128)S(1)} %bitcast.12, ...), custom_call_target="tpu_custom_call" | custom-call | flops 200000000 | bytes 10000000 | tf_op jit(solution)/shard_map/pallas_call | solution.py:416
  20.0 0.1 collective-permute-start
  20.1 1.6 %collective-permute-done = f32[4,72,256]{2,1,0:T(8,128)S(1)} collective-permute-done((f32[4,72,256]{2,1,0:T(8,128)S(1)}, f32[4,72,256]{2,1,0:T(8,128)S(1)}, u32[]{:S(2)}, u32[]{:S(2)}) %collective-permute-start) | collective-permute-done | bytes 294944 | tf_op jit(solution)/shard_map/ppermute | solution.py:513
  21.7 1.6 %collective-permute-start.1 = (f32[4,72,256]{2,1,0:T(8,128)S(1)}, f32[4,72,256]{2,1,0:T(8,128)S(1)}, u32[]{:S(2)}, u32[]{:S(2)}) collective-permute-start(f32[4,72,256]{2,1,0:T(8,128)S(1)} %add.15), channel_id=1, source_target_pairs={{0,16},{8,24},{16,0},{24,8},{1,17},{9,25},{17,1},{25,9},{2,18},{10... | collective-permute-start | bytes 884744 | tf_op jit(solution)/shard_map/ppermute | solution.py:515
  23.2 9.0 %collective-permute-done.3.halo_ref = f32[2,2,280,128]{3,2,1,0:T(8,128)S(1)} collective-permute-done((f32[2,2,280,128]{3,2,1,0:T(8,128)}, f32[2,2,280,128]{3,2,1,0:T(8,128)S(1)}, u32[]{:S(2)}, u32[]{:S(2)}) %collective-permute-start.3) | collective-permute-done | bytes 573472 | tf_op jit(solution)/shard_map/ppermute | solution.py:495
  32.2 1.2 %shard_map.107 = f32[4,72,256]{2,1,0:T(8,128)S(1)} custom-call(s32[8]{0:T(128)S(1)} %copy-done.6, f32[2,2,280,128]{3,2,1,0:T(8,128)S(1)} %collective-permute-done.3.halo_ref, f32[2,4,72,256]{3,2,1,0:T(8,128)S(1)} %get-tuple-element.23.mem_ref, f32[4,72,256]{2,1,0:T(8,128)S(1)} %get-tuple-element.24.cov_ref, bf16[256,256]{1,0:T(8,128)(2,1)S(1)} %copy-done.2, ...), custom_call_target="tpu_custom_call" | custom-call | tf_op jit(solution)/shard_map/pallas_call | solution.py:416
  33.4 0.1 collective-permute-start.4
  33.5 1.2 %shard_map.109 = (f32[2,72,256]{2,1,0:T(8,128)S(1)}, f32[2,72,256]{2,1,0:T(8,128)S(1)}) custom-call(s32[8]{0:T(128)S(1)} %copy-done.6, f32[2,2,280,128]{3,2,1,0:T(8,128)S(1)} %collective-permute-done.6.halo_ref, f32[2,4,72,256]{3,2,1,0:T(8,128)S(1)} %get-tuple-element.29.mem_ref, f32[4,72,256]{2,1,0:T(8,128)S(1)} %get-tuple-element.30.cov_ref, ...), custom_call_target="tpu_custom_call" | custom-call | tf_op jit(solution)/shard_map/pallas_call | solution.py:416
  34.7 0.5 collective-permute-start.7
  35.3 0.1 collective-permute-start.2
  35.4 1.6 %collective-permute-start.5 = (f32[4,72,256]{2,1,0:T(8,128)S(1)}, f32[4,72,256]{2,1,0:T(8,128)S(1)}, u32[]{:S(2)}, u32[]{:S(2)}) collective-permute-start(f32[4,72,256]{2,1,0:T(8,128)S(1)} %add.17.near_a_ref), channel_id=1, source_target_pairs={{0,16},{8,24},{16,0},{24,8},{1,17},{9,25},{17,1},{25,9},{2,18},{10... | collective-permute-start | bytes 884744 | tf_op jit(solution)/shard_map/ppermute | solution.py:530
  37.0 0.8 %collective-permute-start.8 = (f32[2,72,256]{2,1,0:T(8,128)S(1)}, f32[2,72,256]{2,1,0:T(8,128)S(1)}, u32[]{:S(2)}, u32[]{:S(2)}) collective-permute-start(f32[2,72,256]{2,1,0:T(8,128)S(1)} %add.18), channel_id=1, source_target_pairs={{0,16},{8,24},{16,0},{24,8},{1,17},{9,25},{17,1},{25,9},{2,18},{10... | collective-permute-start | bytes 442376 | tf_op jit(solution)/shard_map/ppermute | solution.py:542
  37.8 10.2 %collective-permute-done.8 = f32[2,72,256]{2,1,0:T(8,128)S(1)} collective-permute-done((f32[2,72,256]{2,1,0:T(8,128)S(1)}, f32[2,72,256]{2,1,0:T(8,128)S(1)}, u32[]{:S(2)}, u32[]{:S(2)}) %collective-permute-start.8) | collective-permute-done | bytes 147488 | tf_op jit(solution)/shard_map/ppermute | solution.py:542
  48.0 0.1 collective-permute-start.9
  48.8 1.1 %shard_map.108 = (f32[2,1120,128]{2,1,0:T(8,128)S(1)}, f32[8,128]{1,0:T(8,128)S(1)}) custom-call(f32[1]{0:T(128)S(6)} %copy.11.beta_ref, f32[4,72,256]{2,1,0:T(8,128)S(1)} %add.16.mine_ref, f32[4,72,256]{2,1,0:T(8,128)S(1)} %collective-permute-done.2.other_ref, f32[4,72,256]{2,1,0:T(8,128)S(1)} %add.17.near_a_ref, ...), custom_call_target="tpu_custom_call" | custom-call | tf_op jit(solution)/shard_map/pallas_call | solution.py:416
  49.9 0.3 shard_map.110
  50.2 2.4 %collective-permute-start.10 = (f32[8,128]{1,0:T(8,128)S(1)}, f32[8,128]{1,0:T(8,128)S(1)}, u32[]{:S(2)}, u32[]{:S(2)}) collective-permute-start(f32[8,128]{1,0:T(8,128)S(1)} %get-tuple-element.33.refs_0_), channel_id=1, source_target_pairs={{0,1},{1,0},{2,3},{3,2},{4,5},{5,4},{6,7},{7,6},{8,9},{9,8},{10,11... | collective-permute-start | bytes 12296 | tf_op jit(solution)/shard_map/ppermute | solution.py:552
  52.7 1.6 %collective-permute-done.10.refs_1_ = f32[8,128]{1,0:T(8,128)S(1)} collective-permute-done((f32[8,128]{1,0:T(8,128)S(1)}, f32[8,128]{1,0:T(8,128)S(1)}, u32[]{:S(2)}, u32[]{:S(2)}) %collective-permute-start.10) | collective-permute-done | bytes 4128 | tf_op jit(solution)/shard_map/ppermute | solution.py:552
  54.3 2.1 %collective-permute-start.11 = (f32[8,128]{1,0:T(8,128)S(1)}, f32[8,128]{1,0:T(8,128)S(1)}, u32[]{:S(2)}, u32[]{:S(2)}) collective-permute-start(f32[8,128]{1,0:T(8,128)S(1)} %shard_map.111.refs_0_), channel_id=1, source_target_pairs={{0,2},{1,3},{2,4},{3,5},{4,6},{5,7},{6,0},{7,1},{8,10},{9,11},{10,... | collective-permute-start | bytes 12296 | tf_op jit(solution)/shard_map/ppermute | solution.py:552
  56.4 2.6 %collective-permute-start.12 = (f32[8,128]{1,0:T(8,128)S(1)}, f32[8,128]{1,0:T(8,128)S(1)}, u32[]{:S(2)}, u32[]{:S(2)}) collective-permute-start(f32[8,128]{1,0:T(8,128)S(1)} %shard_map.111.refs_0_), channel_id=1, source_target_pairs={{0,4},{1,5},{2,6},{3,7},{4,0},{5,1},{6,2},{7,3},{8,12},{9,13},{10,... | collective-permute-start | bytes 12296 | tf_op jit(solution)/shard_map/ppermute | solution.py:552
  59.0 1.3 %collective-permute-start.13 = (f32[8,128]{1,0:T(8,128)S(1)}, f32[8,128]{1,0:T(8,128)S(1)}, u32[]{:S(2)}, u32[]{:S(2)}) collective-permute-start(f32[8,128]{1,0:T(8,128)S(1)} %shard_map.111.refs_0_), channel_id=1, source_target_pairs={{0,6},{1,7},{2,0},{3,1},{4,2},{5,3},{6,4},{7,5},{8,14},{9,15},{10,... | collective-permute-start | bytes 12296 | tf_op jit(solution)/shard_map/ppermute | solution.py:552
  60.4 0.6 collective-permute-done.12.refs_2_
  60.9 1.7 %collective-permute-done.13.refs_3_ = f32[8,128]{1,0:T(8,128)S(1)} collective-permute-done((f32[8,128]{1,0:T(8,128)S(1)}, f32[8,128]{1,0:T(8,128)S(1)}, u32[]{:S(2)}, u32[]{:S(2)}) %collective-permute-start.13) | collective-permute-done | bytes 4128 | tf_op jit(solution)/shard_map/ppermute | solution.py:552
  62.6 1.7 %shard_map.112 = (f32[1120,256]{1,0:T(8,128)}, f32[1,2]{1,0:T(1,128)}) custom-call(f32[8,128]{1,0:T(8,128)S(1)} %shard_map.111.refs_0_, f32[8,128]{1,0:T(8,128)S(1)} %collective-permute-done.11.refs_1_, f32[8,128]{1,0:T(8,128)S(1)} %collective-permute-done.12.refs_2_, f32[8,128]{1,0:T(8,128)S(1)} %collective-permute-done.13.refs_3_, ...), custom_call_target="tpu_custom_call" | custom-call | tf_op jit(solution)/shard_map/pallas_call | solution.py:416
  (26 shorter events, 0.2 us)
Async XLA Ops:
  0.6 6.7 %copy-start = (f32[70,16,256]{2,1,0:T(8,128)S(1)}, f32[70,16,256]{2,1,0:T(8,128)}, u32[]{:S(2)}) copy-start(f32[70,16,256]{2,1,0:T(8,128)} %inc_hbm.3) | copy-start | bytes 3440644
  0.6 6.7 %copy-start.1 = (bf16[2,70,16,256]{3,2,1,0:T(8,128)(2,1)S(1)}, bf16[2,70,16,256]{3,2,1,0:T(8,128)(2,1)}, u32[]{:S(2)}) copy-start(bf16[2,70,16,256]{3,2,1,0:T(8,128)(2,1)} %members_hbm.3) | copy-start | bytes 3440644
  0.6 6.7 %copy-start.2 = (bf16[256,256]{1,0:T(8,128)(2,1)S(1)}, bf16[256,256]{1,0:T(8,128)(2,1)}, u32[]{:S(2)}) copy-start(bf16[256,256]{1,0:T(8,128)(2,1)} %constant.6.clone.s_high_hbm.s_high_ref) | copy-start | bytes 393220
  0.7 6.7 %copy-start.3 = (bf16[256,256]{1,0:T(8,128)(2,1)S(1)}, bf16[256,256]{1,0:T(8,128)(2,1)}, u32[]{:S(2)}) copy-start(bf16[256,256]{1,0:T(8,128)(2,1)} %constant.7.clone.s_low_hbm.s_low_ref) | copy-start | bytes 393220
  0.7 6.7 %copy-start.7 = (s32[70]{0:T(128)S(1)}, s32[70]{0:T(128)}, u32[]{:S(2)}) copy-start(s32[70]{0:T(128)} %param.13) | copy-start | bytes 844
  4.3 5.9 %copy-start.4 = (f32[70,16,256]{2,1,0:T(8,128)S(1)}, f32[70,16,256]{2,1,0:T(8,128)}, u32[]{:S(2)}) copy-start(f32[70,16,256]{2,1,0:T(8,128)} %param.10) | copy-start | bytes 3440644
  4.3 5.9 %copy-start.5 = (f32[8,256]{1,0:T(8,128)S(1)}, f32[8,256]{1,0:T(8,128)}, u32[]{:S(2)}) copy-start(f32[8,256]{1,0:T(8,128)} %constant.8.clone.waves_ref) | copy-start | bytes 24580
  4.3 5.9 %copy-start.6 = (s32[8]{0:T(128)S(1)}, s32[8]{0:T(128)}, u32[]{:S(2)}) copy-start(s32[8]{0:T(128)} %steps_ref.5) | copy-start | bytes 100
  4.3 27.9 %collective-permute-start.3 = (f32[2,2,280,128]{3,2,1,0:T(8,128)}, f32[2,2,280,128]{3,2,1,0:T(8,128)S(1)}, u32[]{:S(2)}, u32[]{:S(2)}) collective-permute-start(f32[2,2,280,128]{3,2,1,0:T(8,128)} %shard_map.106), channel_id=1, source_target_pairs={{0,1},{1,0},{2,3},{3,2},{4,5},{5,4},{6,7},{7,6},{8,9},{9,8},{10,11... | collective-permute-start | bytes 1720328 | tf_op jit(solution)/shard_map/ppermute | solution.py:495
  9.5 24.0 %collective-permute-start.6 = (f32[2,2,280,128]{3,2,1,0:T(8,128)S(1)}, f32[2,2,280,128]{3,2,1,0:T(8,128)S(1)}, u32[]{:S(2)}, u32[]{:S(2)}) collective-permute-start(f32[2,2,280,128]{3,2,1,0:T(8,128)S(1)} %shard_map.104), channel_id=1, source_target_pairs={{1,2},{2,1},{3,4},{4,3},{5,6},{6,5},{9,10},{10,9},{11,12},{12,11},... | collective-permute-start | bytes 1720328 | tf_op jit(solution)/shard_map/ppermute | solution.py:499
  20.0 1.6 %collective-permute-start = (f32[4,72,256]{2,1,0:T(8,128)S(1)}, f32[4,72,256]{2,1,0:T(8,128)S(1)}, u32[]{:S(2)}, u32[]{:S(2)}) collective-permute-start(f32[4,72,256]{2,1,0:T(8,128)S(1)} %get-tuple-element.22), channel_id=1, source_target_pairs={{0,8},{8,0},{16,24},{24,16},{1,9},{9,1},{17,25},{25,17},{2,10},{10... | collective-permute-start | bytes 884744 | tf_op jit(solution)/shard_map/ppermute | solution.py:513
  21.7 13.5 %collective-permute-start.1 = (f32[4,72,256]{2,1,0:T(8,128)S(1)}, f32[4,72,256]{2,1,0:T(8,128)S(1)}, u32[]{:S(2)}, u32[]{:S(2)}) collective-permute-start(f32[4,72,256]{2,1,0:T(8,128)S(1)} %add.15), channel_id=1, source_target_pairs={{0,16},{8,24},{16,0},{24,8},{1,17},{9,25},{17,1},{25,9},{2,18},{10... | collective-permute-start | bytes 884744 | tf_op jit(solution)/shard_map/ppermute | solution.py:515
  33.4 2.0 %collective-permute-start.4 = (f32[4,72,256]{2,1,0:T(8,128)S(1)}, f32[4,72,256]{2,1,0:T(8,128)S(1)}, u32[]{:S(2)}, u32[]{:S(2)}) collective-permute-start(f32[4,72,256]{2,1,0:T(8,128)S(1)} %shard_map.107), channel_id=1, source_target_pairs={{0,8},{8,0},{16,24},{24,16},{1,9},{9,1},{17,25},{25,17},{2,10},{10... | collective-permute-start | bytes 884744 | tf_op jit(solution)/shard_map/ppermute | solution.py:529
  34.7 2.3 %collective-permute-start.7 = (f32[2,72,256]{2,1,0:T(8,128)S(1)}, f32[2,72,256]{2,1,0:T(8,128)S(1)}, u32[]{:S(2)}, u32[]{:S(2)}) collective-permute-start(f32[2,72,256]{2,1,0:T(8,128)S(1)} %get-tuple-element.32), channel_id=1, source_target_pairs={{0,8},{8,0},{16,24},{24,16},{1,9},{9,1},{17,25},{25,17},{2,10},{10... | collective-permute-start | bytes 442376 | tf_op jit(solution)/shard_map/ppermute | solution.py:540
  35.3 13.5 %collective-permute-start.2 = (f32[4,72,256]{2,1,0:T(8,128)S(1)}, f32[4,72,256]{2,1,0:T(8,128)S(1)}, u32[]{:S(2)}, u32[]{:S(2)}) collective-permute-start(f32[4,72,256]{2,1,0:T(8,128)S(1)} %add.16.mine_ref), channel_id=1, source_target_pairs={{0,8},{8,0},{16,24},{24,16},{1,9},{9,1},{17,25},{25,17},{2,10},{10... | collective-permute-start | bytes 884744 | tf_op jit(solution)/shard_map/ppermute | solution.py:516
  35.4 13.4 %collective-permute-start.5 = (f32[4,72,256]{2,1,0:T(8,128)S(1)}, f32[4,72,256]{2,1,0:T(8,128)S(1)}, u32[]{:S(2)}, u32[]{:S(2)}) collective-permute-start(f32[4,72,256]{2,1,0:T(8,128)S(1)} %add.17.near_a_ref), channel_id=1, source_target_pairs={{0,16},{8,24},{16,0},{24,8},{1,17},{9,25},{17,1},{25,9},{2,18},{10... | collective-permute-start | bytes 884744 | tf_op jit(solution)/shard_map/ppermute | solution.py:530
  37.0 11.0 %collective-permute-start.8 = (f32[2,72,256]{2,1,0:T(8,128)S(1)}, f32[2,72,256]{2,1,0:T(8,128)S(1)}, u32[]{:S(2)}, u32[]{:S(2)}) collective-permute-start(f32[2,72,256]{2,1,0:T(8,128)S(1)} %add.18), channel_id=1, source_target_pairs={{0,16},{8,24},{16,0},{24,8},{1,17},{9,25},{17,1},{25,9},{2,18},{10... | collective-permute-start | bytes 442376 | tf_op jit(solution)/shard_map/ppermute | solution.py:542
  48.0 1.9 %collective-permute-start.9 = (f32[2,72,256]{2,1,0:T(8,128)S(1)}, f32[2,72,256]{2,1,0:T(8,128)S(1)}, u32[]{:S(2)}, u32[]{:S(2)}) collective-permute-start(f32[2,72,256]{2,1,0:T(8,128)S(1)} %add.19.mine_ref), channel_id=1, source_target_pairs={{0,8},{8,0},{16,24},{24,16},{1,9},{9,1},{17,25},{25,17},{2,10},{10... | collective-permute-start | bytes 442376 | tf_op jit(solution)/shard_map/ppermute | solution.py:543
  50.2 4.0 %collective-permute-start.10 = (f32[8,128]{1,0:T(8,128)S(1)}, f32[8,128]{1,0:T(8,128)S(1)}, u32[]{:S(2)}, u32[]{:S(2)}) collective-permute-start(f32[8,128]{1,0:T(8,128)S(1)} %get-tuple-element.33.refs_0_), channel_id=1, source_target_pairs={{0,1},{1,0},{2,3},{3,2},{4,5},{5,4},{6,7},{7,6},{8,9},{9,8},{10,11... | collective-permute-start | bytes 12296 | tf_op jit(solution)/shard_map/ppermute | solution.py:552
  54.3 6.1 %collective-permute-start.11 = (f32[8,128]{1,0:T(8,128)S(1)}, f32[8,128]{1,0:T(8,128)S(1)}, u32[]{:S(2)}, u32[]{:S(2)}) collective-permute-start(f32[8,128]{1,0:T(8,128)S(1)} %shard_map.111.refs_0_), channel_id=1, source_target_pairs={{0,2},{1,3},{2,4},{3,5},{4,6},{5,7},{6,0},{7,1},{8,10},{9,11},{10,... | collective-permute-start | bytes 12296 | tf_op jit(solution)/shard_map/ppermute | solution.py:552
  56.4 4.5 %collective-permute-start.12 = (f32[8,128]{1,0:T(8,128)S(1)}, f32[8,128]{1,0:T(8,128)S(1)}, u32[]{:S(2)}, u32[]{:S(2)}) collective-permute-start(f32[8,128]{1,0:T(8,128)S(1)} %shard_map.111.refs_0_), channel_id=1, source_target_pairs={{0,4},{1,5},{2,6},{3,7},{4,0},{5,1},{6,2},{7,3},{8,12},{9,13},{10,... | collective-permute-start | bytes 12296 | tf_op jit(solution)/shard_map/ppermute | solution.py:552
  59.0 3.6 %collective-permute-start.13 = (f32[8,128]{1,0:T(8,128)S(1)}, f32[8,128]{1,0:T(8,128)S(1)}, u32[]{:S(2)}, u32[]{:S(2)}) collective-permute-start(f32[8,128]{1,0:T(8,128)S(1)} %shard_map.111.refs_0_), channel_id=1, source_target_pairs={{0,6},{1,7},{2,0},{3,1},{4,2},{5,3},{6,4},{7,5},{8,14},{9,15},{10,... | collective-permute-start | bytes 12296 | tf_op jit(solution)/shard_map/ppermute | solution.py:552

commit v4 on v3

--- a/solution.py
+++ b/solution.py
@@ -148,10 +148,20 @@
                 out_ref[m, piece, pl.ds(q, levels, stride=DIFF), :] = part
 
 
+def turn_kernel(rows, levels, inc_ref, prev_ref, inc_t_ref, prev_t_ref, flat_ref):
+    tile = lax.axis_index("tile")
+    for piece in range(flat_ref.shape[0]):
+        flat_ref[piece, rows * levels :, :] = jnp.zeros((flat_ref.shape[1] - rows * levels, 128), F32)
+    for source, target in ((inc_ref, inc_t_ref), (prev_ref, prev_t_ref)):
+        put_flat(flat_ref, source[...])
+        for row in range(rows):
+            target[row] = strided(flat_ref, grid_row(tile, row, rows), target.shape[1], rows)
+
+
 def own_kernel(
     rows, levels, tiles,
-    bands_ref, steps_ref, members_ref, inc_ref, prev_ref, s_high_ref, s_low_ref, waves_ref,
-    mine_ref, theirs_ref, cov_near_ref, cov_far_ref, mem_near_ref, mem_far_ref, inc_t_ref, prev_t_ref,
+    bands_ref, steps_ref, members_ref, inc_ref, s_high_ref, s_low_ref, waves_ref,
+    mine_ref, theirs_ref, cov_near_ref, cov_far_ref, mem_near_ref, mem_far_ref,
     prod_ref, memf_ref, spec_ref, acc_ref, base_ref, pad_ref,
 ):
     tile = lax.axis_index("tile")
@@ -168,10 +178,6 @@
     def row_of(ref, row, count):
         return strided(ref, grid_row(tile, row, rows), count, rows)
 
-    for source, target in ((inc_ref, inc_t_ref), (prev_ref, prev_t_ref)):
-        put_flat(prod_ref, source[...])
-        for row in range(rows):
-            target[row] = row_of(prod_ref, row, tall)
     rate = [[coefficient(k, count) for count in counts] for k in range(DIFF)]
     for k in range(DIFF):
         for side in range(3):
@@ -251,10 +257,6 @@
         block = transform(block, s_high_ref[...], s_low_ref[...])
         for q in range(DIFF):
             sums[q] = sums[q] + mem_ref[m, q] * block[q * tall : (q + 1) * tall]
-    if len(out_refs) == 1:
-        for q in range(DIFF):
-            out_refs[0][q] = sums[q]
-        return
     part = DIFF // 2
     half = lax.axis_index("mem") % 2
     for q in range(DIFF):
@@ -289,7 +291,7 @@
 
 def bulk_kernel(
     rows, levels, inverse,
-    beta_ref, mine_ref, other_ref, near_a_ref, near_b_ref, inc_ref, prev_ref,
+    beta_ref, mine_ref, other_ref, near_mine_ref, near_other_ref, inc_ref, prev_ref,
     w_ref, sums_ref, keep_ref,
 ):
     beta = beta_ref[0]
@@ -300,8 +302,8 @@
 
     def covariance(row):
         if row >= rows - DIFF:
-            q = rows - 1 - row
-            return near_a_ref[q] + near_b_ref[q]
+            which, q = divmod(rows - 1 - row, DIFF // 2)
+            return jnp.where(own_half == which, near_mine_ref[q], near_other_ref[q])
         which, q = divmod(row - DIFF, part)
         return jnp.where(own_half == which, mine_ref[q], other_ref[q])
 
@@ -496,19 +498,27 @@
     far_edge = edges(False)
     members, far_edge = lax.optimization_barrier((members, far_edge))
     mem = members.reshape(owned, levels * rows, width)
-    far_halo = lax.ppermute(far_edge, "tile", far_pairs)
 
     piece, four = (part, tall, width), (DIFF, tall, width)
-    mine, theirs, cov_near, cov_far, mem_near, mem_far, inc_t, prev_t = call(
+    mine, theirs, cov_near, cov_far, mem_near, mem_far = call(
         functools.partial(own_kernel, rows, levels, tiles),
-        [("v", bands), ("s", diffusion_steps), ("v", mem), ("v", inc), ("v", prev)]
+        [("v", bands), ("s", diffusion_steps), ("v", mem), ("v", inc)]
         + [("v", s_high), ("v", s_low), ("v", waves)],
-        [piece, piece, four, four, edge, edge, (rows, tall, width), (rows, tall, width)],
+        [piece, piece, four, four, edge, edge],
         [pltpu.VMEM((lanes, deep * rows, 128), F32)] * 2
         + [pltpu.VMEM((rows, tall, width), F32)] * 2
         + [pltpu.VMEM((DIFF, 3, 8, width), F32), pad],
         (200_000_000, 10_000_000),
     )
+    prev, _ = lax.optimization_barrier((prev, theirs))
+    inc_t, prev_t = call(
+        functools.partial(turn_kernel, rows, levels),
+        [("v", inc), ("v", prev)],
+        [(rows, tall, width), (rows, tall, width)],
+        [pltpu.VMEM((lanes, tall * rows, 128), F32)],
+    )
+    theirs, far_edge = lax.optimization_barrier((theirs, far_edge))
+    far_halo = lax.ppermute(far_edge, "tile", far_pairs)
     bits = [1 << k for k in range(1, mems.bit_length() - 1)]
     mine = mine + lax.ppermute(theirs, "mem", flipped("mem", 1))
     for bit in bits:
@@ -524,18 +534,20 @@
             [pltpu.VMEM(four, F32), pltpu.VMEM((DIFF, 2, 8, width), F32)],
         )
 
-    (near_sum,) = edge_sum(True, near_halo, mem_near, cov_near, [four])
-    for bit in [1] + bits[:-1]:
-        near_sum = near_sum + lax.ppermute(near_sum, "mem", flipped("mem", bit))
-    near_other = lax.ppermute(near_sum, "mem", flipped("mem", bits[-1]))
+    two = (DIFF // 2, tall, width)
+    near_mine, near_theirs = edge_sum(True, near_halo, mem_near, cov_near, [two, two])
+    near_mine = near_mine + lax.ppermute(near_theirs, "mem", flipped("mem", 1))
+    for bit in bits:
+        near_mine = near_mine + lax.ppermute(near_mine, "mem", flipped("mem", bit))
+    near_other = lax.ppermute(near_mine, "mem", flipped("mem", 1))
+    cov_far, near_mine, inc_t = lax.optimization_barrier((cov_far, near_mine, inc_t))
     w_rest, sums = call(
         functools.partial(bulk_kernel, rows, levels, inverse),
-        [("s", beta_prev), ("v", mine), ("v", other), ("v", near_sum), ("v", near_other)]
+        [("s", beta_prev), ("v", mine), ("v", other), ("v", near_mine), ("v", near_other)]
         + [("v", inc_t), ("v", prev_t)],
         [(lanes, levels * rows, 128), (8, 128)],
         [pltpu.VMEM((rows - DIFF, tall, width), F32)],
     )
-    two = (DIFF // 2, tall, width)
     far_mine, far_theirs = edge_sum(False, far_halo, mem_far, cov_far, [two, two])
     far_mine = far_mine + lax.ppermute(far_theirs, "mem", flipped("mem", 1))
     for bit in bits:

time: 64.5 us -> 60.5 us (0.938)
  waiting for transfers between devices: 24.6 us -> 21 us
    ppermute x1, waiting for transfers between devices: 8.98 us -> 1.89 us  [per_device(): near_halo = lax.ppermute(near_edge, 'tile', near_pairs)]
    ppermute x1, waiting for transfers between devices: 10.2 us -> 4.33 us  [per_device(): far_mine = far_mine + lax.ppermute(far_mine, 'mem', flipped('mem', bit))]
    ppermute x2 -> x3, waiting for transfers between devices: 0.01 us -> 4.54 us  [the longest x1 3.18 us: per_device(): near_mine = near_mine + lax.ppermute(near_mine, 'mem', flipped('mem', bit))]
    ppermute x1, waiting for transfers between devices: 0.01 us -> 4.22 us  [per_device(): mine = mine + lax.ppermute(mine, 'mem', flipped('mem', bit))]
    ppermute x4, waiting for transfers between devices: 3.84 us -> 5.98 us  [per_device(): lax.ppermute(sums, 'tile', rotated('tile', digit, radix, by))]
    ppermute x1, waiting for transfers between devices: 1.57 us -> 0.01 us  [per_device(): mine = mine + lax.ppermute(theirs, 'mem', flipped('mem', 1))]
    ppermute x1, starting transfers between devices: 1.56 us -> 0.38 us  [per_device(): mine = mine + lax.ppermute(mine, 'mem', flipped('mem', bit))]
    ppermute x1, starting transfers between devices: 0.83 us -> 1.77 us  [per_device(): far_mine = far_mine + lax.ppermute(far_mine, 'mem', flipped('mem', bit))]
  transfers between devices with their start and end apart: 14 -> 15, of which waited for: 6 -> 9; matrix products, arithmetic and copies ran while one was open for 0% -> 0% of each run, Pallas kernels for 24% -> 25%
where the time goes in v4:
time: 60.5 us; the launch traced here: 60.4 us
  Pallas kernels  21 us (35%)
  waiting for transfers between devices  21 us (35%)
  starting transfers between devices  16.7 us (28%)
  between operations  1.54 us (3%)
    pallas_call x10, Pallas kernels, call(): pl.pallas_call(kernel, out_shape=tuple((jax.ShapeDtypeStruct(shape, F32)...  21 us
    ppermute x4, starting transfers between devices, per_device(): lax.ppermute(sums, 'tile', rotated('tile', digit, radix, by))  8.51 us
    ppermute x4, waiting for transfers between devices, per_device(): lax.ppermute(sums, 'tile', rotated('tile', digit, radix, by))  5.98 us
    ppermute x1, waiting for transfers between devices, per_device(): far_mine = far_mine + lax.ppermute(far_mine, 'mem', flipped('mem', bit))  4.33 us
    ppermute x1, waiting for transfers between devices, per_device(): mine = mine + lax.ppermute(mine, 'mem', flipped('mem', bit))  4.22 us
    ppermute x1, waiting for transfers between devices, per_device(): near_mine = near_mine + lax.ppermute(near_mine, 'mem', flipped('mem', bit))  3.18 us
    ppermute x1, starting transfers between devices, per_device(): near_halo = lax.ppermute(near_edge, 'tile', near_pairs)  3.03 us
    ppermute x1, waiting for transfers between devices, per_device(): near_halo = lax.ppermute(near_edge, 'tile', near_pairs)  1.89 us
  transfers between devices with their start and end apart: 15, of which 9 were waited for; matrix products, arithmetic and copies ran while one was open for 0% of the time, Pallas kernels for 25%

profile of v4, /device:TPU:0, one launch (start us, length us, event | category | flops | bytes accessed | tf_op | source)
XLA Modules:
  0.0 60.4 jit_solution(7497516398334419448)
XLA Ops:
  0.7 3.6 %shard_map.106 = f32[2,2,280,128]{3,2,1,0:T(8,128)} custom-call(s32[1,70]{1,0:T(1,128)} %bitcast.11, bf16[2,70,16,256]{3,2,1,0:T(8,128)(2,1)} %members_hbm.3, f32[70,16,256]{2,1,0:T(8,128)} %inc_hbm.3, bf16[256,256]{1,0:T(8,128)(2,1)} %constant.6.clone.s_high_hbm.s_high_ref, bf16[256,256]{1,0:T(8,128)(2,1)} %constant.7.clone.s_low_hbm.s_low_ref), custom_call_target="tpu_custom_call" | custom-call | tf_op jit(solution)/shard_map/pallas_call | solution.py:418
  4.3 3.0 %collective-permute-start.3 = (f32[2,2,280,128]{3,2,1,0:T(8,128)}, f32[2,2,280,128]{3,2,1,0:T(8,128)S(1)}, u32[]{:S(2)}, u32[]{:S(2)}) collective-permute-start(f32[2,2,280,128]{3,2,1,0:T(8,128)} %shard_map.106), channel_id=1, source_target_pairs={{0,1},{1,0},{2,3},{3,2},{4,5},{5,4},{6,7},{7,6},{8,9},{9,8},{10,11... | collective-permute-start | bytes 1720328 | tf_op jit(solution)/shard_map/ppermute | solution.py:497
  7.4 2.1 %shard_map.104 = f32[2,2,280,128]{3,2,1,0:T(8,128)S(1)} custom-call(s32[1,70]{1,0:T(1,128)S(1)} %bitcast.12, bf16[2,70,16,256]{3,2,1,0:T(8,128)(2,1)S(1)} %copy-done.1, f32[70,16,256]{2,1,0:T(8,128)S(1)} %copy-done, bf16[256,256]{1,0:T(8,128)(2,1)S(1)} %copy-done.3, bf16[256,256]{1,0:T(8,128)(2,1)S(1)} %copy-done.2), custom_call_target="tpu_custom_call" | custom-call | tf_op jit(solution)/shard_map/pallas_call | solution.py:418
  9.5 8.4 %shard_map.105 = (f32[4,72,256]{2,1,0:T(8,128)S(1)}, f32[4,72,256]{2,1,0:T(8,128)S(1)}, f32[4,72,256]{2,1,0:T(8,128)S(1)}, f32[4,72,256]{2,1,0:T(8,128)S(1)}, f3...) custom-call(s32[1,70]{1,0:T(1,128)S(1)} %bitcast.13, s32[8]{0:T(128)S(1)} %copy-done.6, ...), custom_call_target="tpu_custom_call" | custom-call | flops 200000000 | bytes 10000000 | tf_op jit(solution)/shard_map/pallas_call | solution.py:418
  17.9 0.7 %collective-permute-start.7 = (f32[2,2,280,128]{3,2,1,0:T(8,128)S(1)}, f32[2,2,280,128]{3,2,1,0:T(8,128)S(1)}, u32[]{:S(2)}, u32[]{:S(2)}) collective-permute-start(f32[2,2,280,128]{3,2,1,0:T(8,128)S(1)} %shard_map.104), channel_id=1, source_target_pairs={{1,2},{2,1},{3,4},{4,3},{5,6},{6,5},{9,10},{10,9},{11,12},{12,11},... | collective-permute-start | bytes 1720328 | tf_op jit(solution)/shard_map/ppermute | solution.py:521
  18.6 0.1 collective-permute-start
  18.6 1.9 %collective-permute-done.3.halo_ref = f32[2,2,280,128]{3,2,1,0:T(8,128)S(1)} collective-permute-done((f32[2,2,280,128]{3,2,1,0:T(8,128)}, f32[2,2,280,128]{3,2,1,0:T(8,128)S(1)}, u32[]{:S(2)}, u32[]{:S(2)}) %collective-permute-start.3) | collective-permute-done | bytes 573472 | tf_op jit(solution)/shard_map/ppermute | solution.py:497
  20.5 1.2 %shard_map.107 = (f32[2,72,256]{2,1,0:T(8,128)S(1)}, f32[2,72,256]{2,1,0:T(8,128)S(1)}) custom-call(s32[8]{0:T(128)S(1)} %copy-done.6, f32[2,2,280,128]{3,2,1,0:T(8,128)S(1)} %collective-permute-done.3.halo_ref, f32[2,4,72,256]{3,2,1,0:T(8,128)S(1)} %get-tuple-element.34.mem_ref, f32[4,72,256]{2,1,0:T(8,128)S(1)} %get-tuple-element.35.cov_ref, ...), custom_call_target="tpu_custom_call" | custom-call | tf_op jit(solution)/shard_map/pallas_call | solution.py:418
  21.7 0.1 collective-permute-start.4
  21.8 1.4 %collective-permute-done.4 = f32[2,72,256]{2,1,0:T(8,128)S(1)} collective-permute-done((f32[2,72,256]{2,1,0:T(8,128)S(1)}, f32[2,72,256]{2,1,0:T(8,128)S(1)}, u32[]{:S(2)}, u32[]{:S(2)}) %collective-permute-start.4) | collective-permute-done | bytes 147488 | tf_op jit(solution)/shard_map/ppermute | solution.py:539
  23.2 1.8 %collective-permute-start.5 = (f32[2,72,256]{2,1,0:T(8,128)S(1)}, f32[2,72,256]{2,1,0:T(8,128)S(1)}, u32[]{:S(2)}, u32[]{:S(2)}) collective-permute-start(f32[2,72,256]{2,1,0:T(8,128)S(1)} %add.20), channel_id=1, source_target_pairs={{0,16},{8,24},{16,0},{24,8},{1,17},{9,25},{17,1},{25,9},{2,18},{10... | collective-permute-start | bytes 442376 | tf_op jit(solution)/shard_map/ppermute | solution.py:541
  25.0 0.4 collective-permute-start.1
  25.4 1.4 %shard_map.108 = (f32[16,72,256]{2,1,0:T(8,128)S(1)}, f32[16,72,256]{2,1,0:T(8,128)S(1)}) custom-call(f32[1120,256]{1,0:T(8,128)S(1)} %bitcast.7, f32[1120,256]{1,0:T(8,128)S(1)} %bitcast.10), custom_call_target="tpu_custom_call" | custom-call | tf_op jit(solution)/shard_map/pallas_call | solution.py:418
  26.8 3.2 %collective-permute-done.5 = f32[2,72,256]{2,1,0:T(8,128)S(1)} collective-permute-done((f32[2,72,256]{2,1,0:T(8,128)S(1)}, f32[2,72,256]{2,1,0:T(8,128)S(1)}, u32[]{:S(2)}, u32[]{:S(2)}) %collective-permute-start.5) | collective-permute-done | bytes 147488 | tf_op jit(solution)/shard_map/ppermute | solution.py:541
  30.0 1.2 %shard_map.110 = (f32[2,72,256]{2,1,0:T(8,128)S(1)}, f32[2,72,256]{2,1,0:T(8,128)S(1)}) custom-call(s32[8]{0:T(128)S(1)} %copy-done.6, f32[2,2,280,128]{3,2,1,0:T(8,128)S(1)} %collective-permute-done.7.halo_ref, f32[2,4,72,256]{3,2,1,0:T(8,128)S(1)} %get-tuple-element.45.mem_ref, f32[4,72,256]{2,1,0:T(8,128)S(1)} %get-tuple-element.46.cov_ref, ...), custom_call_target="tpu_custom_call" | custom-call | tf_op jit(solution)/shard_map/pallas_call | solution.py:418
  31.2 0.1 collective-permute-start.8
  31.3 4.2 %collective-permute-done.1 = f32[4,72,256]{2,1,0:T(8,128)S(1)} collective-permute-done((f32[4,72,256]{2,1,0:T(8,128)S(1)}, f32[4,72,256]{2,1,0:T(8,128)S(1)}, u32[]{:S(2)}, u32[]{:S(2)}) %collective-permute-start.1) | collective-permute-done | bytes 294944 | tf_op jit(solution)/shard_map/ppermute | solution.py:525
  35.5 0.1 collective-permute-start.2
  35.6 1.8 %collective-permute-start.9 = (f32[2,72,256]{2,1,0:T(8,128)S(1)}, f32[2,72,256]{2,1,0:T(8,128)S(1)}, u32[]{:S(2)}, u32[]{:S(2)}) collective-permute-start(f32[2,72,256]{2,1,0:T(8,128)S(1)} %add.22), channel_id=1, source_target_pairs={{0,16},{8,24},{16,0},{24,8},{1,17},{9,25},{17,1},{25,9},{2,18},{10... | collective-permute-start | bytes 442376 | tf_op jit(solution)/shard_map/ppermute | solution.py:554
  37.4 0.2 collective-permute-start.6
  37.6 4.3 %collective-permute-done.9 = f32[2,72,256]{2,1,0:T(8,128)S(1)} collective-permute-done((f32[2,72,256]{2,1,0:T(8,128)S(1)}, f32[2,72,256]{2,1,0:T(8,128)S(1)}, u32[]{:S(2)}, u32[]{:S(2)}) %collective-permute-start.9) | collective-permute-done | bytes 147488 | tf_op jit(solution)/shard_map/ppermute | solution.py:554
  42.0 0.1 collective-permute-start.10
  42.7 1.1 %shard_map.109 = (f32[2,1120,128]{2,1,0:T(8,128)S(1)}, f32[8,128]{1,0:T(8,128)S(1)}) custom-call(f32[1]{0:T(128)S(6)} %copy.11.beta_ref, f32[4,72,256]{2,1,0:T(8,128)S(1)} %add.19.mine_ref, f32[4,72,256]{2,1,0:T(8,128)S(1)} %collective-permute-done.2.other_ref, f32[2,72,256]{2,1,0:T(8,128)S(1)} %add.21.near_mine_ref, ...), custom_call_target="tpu_custom_call" | custom-call | tf_op jit(solution)/shard_map/pallas_call | solution.py:418
  43.8 0.3 shard_map.111
  44.2 2.8 %collective-permute-start.11 = (f32[8,128]{1,0:T(8,128)S(1)}, f32[8,128]{1,0:T(8,128)S(1)}, u32[]{:S(2)}, u32[]{:S(2)}) collective-permute-start(f32[8,128]{1,0:T(8,128)S(1)} %get-tuple-element.49.refs_0_), channel_id=1, source_target_pairs={{0,1},{1,0},{2,3},{3,2},{4,5},{5,4},{6,7},{7,6},{8,9},{9,8},{10,11... | collective-permute-start | bytes 12296 | tf_op jit(solution)/shard_map/ppermute | solution.py:564
  46.9 1.6 %collective-permute-done.11.refs_1_ = f32[8,128]{1,0:T(8,128)S(1)} collective-permute-done((f32[8,128]{1,0:T(8,128)S(1)}, f32[8,128]{1,0:T(8,128)S(1)}, u32[]{:S(2)}, u32[]{:S(2)}) %collective-permute-start.11) | collective-permute-done | bytes 4128 | tf_op jit(solution)/shard_map/ppermute | solution.py:564
  48.5 4.7 %collective-permute-start.14 = (f32[8,128]{1,0:T(8,128)S(1)}, f32[8,128]{1,0:T(8,128)S(1)}, u32[]{:S(2)}, u32[]{:S(2)}) collective-permute-start(f32[8,128]{1,0:T(8,128)S(1)} %shard_map.112.refs_0_), channel_id=1, source_target_pairs={{0,6},{1,7},{2,0},{3,1},{4,2},{5,3},{6,4},{7,5},{8,14},{9,15},{10,... | collective-permute-start | bytes 12296 | tf_op jit(solution)/shard_map/ppermute | solution.py:564
  53.3 1.0 %collective-permute-start.12 = (f32[8,128]{1,0:T(8,128)S(1)}, f32[8,128]{1,0:T(8,128)S(1)}, u32[]{:S(2)}, u32[]{:S(2)}) collective-permute-start(f32[8,128]{1,0:T(8,128)S(1)} %shard_map.112.refs_0_), channel_id=1, source_target_pairs={{0,2},{1,3},{2,4},{3,5},{4,6},{5,7},{6,0},{7,1},{8,10},{9,11},{10,... | collective-permute-start | bytes 12296 | tf_op jit(solution)/shard_map/ppermute | solution.py:564
  54.3 0.3 collective-permute-done.14.refs_3_
  54.6 3.2 %collective-permute-done.13.refs_2_ = f32[8,128]{1,0:T(8,128)S(1)} collective-permute-done((f32[8,128]{1,0:T(8,128)S(1)}, f32[8,128]{1,0:T(8,128)S(1)}, u32[]{:S(2)}, u32[]{:S(2)}) %collective-permute-start.13) | collective-permute-done | bytes 4128 | tf_op jit(solution)/shard_map/ppermute | solution.py:564
  57.8 0.9 %collective-permute-done.12.refs_1_ = f32[8,128]{1,0:T(8,128)S(1)} collective-permute-done((f32[8,128]{1,0:T(8,128)S(1)}, f32[8,128]{1,0:T(8,128)S(1)}, u32[]{:S(2)}, u32[]{:S(2)}) %collective-permute-start.12) | collective-permute-done | bytes 4128 | tf_op jit(solution)/shard_map/ppermute | solution.py:564
  58.7 1.7 %shard_map.113 = (f32[1120,256]{1,0:T(8,128)}, f32[1,2]{1,0:T(1,128)}) custom-call(f32[8,128]{1,0:T(8,128)S(1)} %shard_map.112.refs_0_, f32[8,128]{1,0:T(8,128)S(1)} %collective-permute-done.12.refs_1_, f32[8,128]{1,0:T(8,128)S(1)} %collective-permute-done.13.refs_2_, f32[8,128]{1,0:T(8,128)S(1)} %collective-permute-done.14.refs_3_, ...), custom_call_target="tpu_custom_call" | custom-call | tf_op jit(solution)/shard_map/pallas_call | solution.py:418
  (30 shorter events, 0.2 us)
Async XLA Ops:
  0.6 6.7 %copy-start = (f32[70,16,256]{2,1,0:T(8,128)S(1)}, f32[70,16,256]{2,1,0:T(8,128)}, u32[]{:S(2)}) copy-start(f32[70,16,256]{2,1,0:T(8,128)} %inc_hbm.3) | copy-start | bytes 3440644
  0.6 6.7 %copy-start.1 = (bf16[2,70,16,256]{3,2,1,0:T(8,128)(2,1)S(1)}, bf16[2,70,16,256]{3,2,1,0:T(8,128)(2,1)}, u32[]{:S(2)}) copy-start(bf16[2,70,16,256]{3,2,1,0:T(8,128)(2,1)} %members_hbm.3) | copy-start | bytes 3440644
  0.6 6.7 %copy-start.2 = (bf16[256,256]{1,0:T(8,128)(2,1)S(1)}, bf16[256,256]{1,0:T(8,128)(2,1)}, u32[]{:S(2)}) copy-start(bf16[256,256]{1,0:T(8,128)(2,1)} %constant.7.clone.s_low_hbm.s_low_ref) | copy-start | bytes 393220
  0.7 6.7 %copy-start.3 = (bf16[256,256]{1,0:T(8,128)(2,1)S(1)}, bf16[256,256]{1,0:T(8,128)(2,1)}, u32[]{:S(2)}) copy-start(bf16[256,256]{1,0:T(8,128)(2,1)} %constant.6.clone.s_high_hbm.s_high_ref) | copy-start | bytes 393220
  0.7 6.7 %copy-start.7 = (s32[70]{0:T(128)S(1)}, s32[70]{0:T(128)}, u32[]{:S(2)}) copy-start(s32[70]{0:T(128)} %param.13) | copy-start | bytes 844
  4.3 5.2 %copy-start.5 = (f32[8,256]{1,0:T(8,128)S(1)}, f32[8,256]{1,0:T(8,128)}, u32[]{:S(2)}) copy-start(f32[8,256]{1,0:T(8,128)} %constant.8.clone.waves_ref) | copy-start | bytes 24580
  4.3 5.2 %copy-start.6 = (s32[8]{0:T(128)S(1)}, s32[8]{0:T(128)}, u32[]{:S(2)}) copy-start(s32[8]{0:T(128)} %steps_ref.5) | copy-start | bytes 100
  4.3 16.2 %collective-permute-start.3 = (f32[2,2,280,128]{3,2,1,0:T(8,128)}, f32[2,2,280,128]{3,2,1,0:T(8,128)S(1)}, u32[]{:S(2)}, u32[]{:S(2)}) collective-permute-start(f32[2,2,280,128]{3,2,1,0:T(8,128)} %shard_map.106), channel_id=1, source_target_pairs={{0,1},{1,0},{2,3},{3,2},{4,5},{5,4},{6,7},{7,6},{8,9},{9,8},{10,11... | collective-permute-start | bytes 1720328 | tf_op jit(solution)/shard_map/ppermute | solution.py:497
  17.9 12.1 %collective-permute-start.7 = (f32[2,2,280,128]{3,2,1,0:T(8,128)S(1)}, f32[2,2,280,128]{3,2,1,0:T(8,128)S(1)}, u32[]{:S(2)}, u32[]{:S(2)}) collective-permute-start(f32[2,2,280,128]{3,2,1,0:T(8,128)S(1)} %shard_map.104), channel_id=1, source_target_pairs={{1,2},{2,1},{3,4},{4,3},{5,6},{6,5},{9,10},{10,9},{11,12},{12,11},... | collective-permute-start | bytes 1720328 | tf_op jit(solution)/shard_map/ppermute | solution.py:521
  18.6 6.4 %collective-permute-start = (f32[4,72,256]{2,1,0:T(8,128)S(1)}, f32[4,72,256]{2,1,0:T(8,128)S(1)}, u32[]{:S(2)}, u32[]{:S(2)}) collective-permute-start(f32[4,72,256]{2,1,0:T(8,128)S(1)} %get-tuple-element.32), channel_id=1, source_target_pairs={{0,8},{8,0},{16,24},{24,16},{1,9},{9,1},{17,25},{25,17},{2,10},{10... | collective-permute-start | bytes 884744 | tf_op jit(solution)/shard_map/ppermute | solution.py:523
  20.5 4.9 %copy-start.4 = (f32[70,16,256]{2,1,0:T(8,128)S(1)}, f32[70,16,256]{2,1,0:T(8,128)}, u32[]{:S(2)}) copy-start(f32[70,16,256]{2,1,0:T(8,128)} %param.10) | copy-start | bytes 3440644
  21.7 1.4 %collective-permute-start.4 = (f32[2,72,256]{2,1,0:T(8,128)S(1)}, f32[2,72,256]{2,1,0:T(8,128)S(1)}, u32[]{:S(2)}, u32[]{:S(2)}) collective-permute-start(f32[2,72,256]{2,1,0:T(8,128)S(1)} %get-tuple-element.37), channel_id=1, source_target_pairs={{0,8},{8,0},{16,24},{24,16},{1,9},{9,1},{17,25},{25,17},{2,10},{10... | collective-permute-start | bytes 442376 | tf_op jit(solution)/shard_map/ppermute | solution.py:539
  23.2 6.8 %collective-permute-start.5 = (f32[2,72,256]{2,1,0:T(8,128)S(1)}, f32[2,72,256]{2,1,0:T(8,128)S(1)}, u32[]{:S(2)}, u32[]{:S(2)}) collective-permute-start(f32[2,72,256]{2,1,0:T(8,128)S(1)} %add.20), channel_id=1, source_target_pairs={{0,16},{8,24},{16,0},{24,8},{1,17},{9,25},{17,1},{25,9},{2,18},{10... | collective-permute-start | bytes 442376 | tf_op jit(solution)/shard_map/ppermute | solution.py:541
  25.0 10.5 %collective-permute-start.1 = (f32[4,72,256]{2,1,0:T(8,128)S(1)}, f32[4,72,256]{2,1,0:T(8,128)S(1)}, u32[]{:S(2)}, u32[]{:S(2)}) collective-permute-start(f32[4,72,256]{2,1,0:T(8,128)S(1)} %add.18), channel_id=1, source_target_pairs={{0,16},{8,24},{16,0},{24,8},{1,17},{9,25},{17,1},{25,9},{2,18},{10... | collective-permute-start | bytes 884744 | tf_op jit(solution)/shard_map/ppermute | solution.py:525
  31.2 4.4 %collective-permute-start.8 = (f32[2,72,256]{2,1,0:T(8,128)S(1)}, f32[2,72,256]{2,1,0:T(8,128)S(1)}, u32[]{:S(2)}, u32[]{:S(2)}) collective-permute-start(f32[2,72,256]{2,1,0:T(8,128)S(1)} %get-tuple-element.48), channel_id=1, source_target_pairs={{0,8},{8,0},{16,24},{24,16},{1,9},{9,1},{17,25},{25,17},{2,10},{10... | collective-permute-start | bytes 442376 | tf_op jit(solution)/shard_map/ppermute | solution.py:552
  35.5 7.2 %collective-permute-start.2 = (f32[4,72,256]{2,1,0:T(8,128)S(1)}, f32[4,72,256]{2,1,0:T(8,128)S(1)}, u32[]{:S(2)}, u32[]{:S(2)}) collective-permute-start(f32[4,72,256]{2,1,0:T(8,128)S(1)} %add.19.mine_ref), channel_id=1, source_target_pairs={{0,8},{8,0},{16,24},{24,16},{1,9},{9,1},{17,25},{25,17},{2,10},{10... | collective-permute-start | bytes 884744 | tf_op jit(solution)/shard_map/ppermute | solution.py:526
  35.6 6.3 %collective-permute-start.9 = (f32[2,72,256]{2,1,0:T(8,128)S(1)}, f32[2,72,256]{2,1,0:T(8,128)S(1)}, u32[]{:S(2)}, u32[]{:S(2)}) collective-permute-start(f32[2,72,256]{2,1,0:T(8,128)S(1)} %add.22), channel_id=1, source_target_pairs={{0,16},{8,24},{16,0},{24,8},{1,17},{9,25},{17,1},{25,9},{2,18},{10... | collective-permute-start | bytes 442376 | tf_op jit(solution)/shard_map/ppermute | solution.py:554
  37.4 5.3 %collective-permute-start.6 = (f32[2,72,256]{2,1,0:T(8,128)S(1)}, f32[2,72,256]{2,1,0:T(8,128)S(1)}, u32[]{:S(2)}, u32[]{:S(2)}) collective-permute-start(f32[2,72,256]{2,1,0:T(8,128)S(1)} %add.21.near_mine_ref), channel_id=1, source_target_pairs={{0,8},{8,0},{16,24},{24,16},{1,9},{9,1},{17,25},{25,17},{2,10},{10... | collective-permute-start | bytes 442376 | tf_op jit(solution)/shard_map/ppermute | solution.py:542
  42.0 1.9 %collective-permute-start.10 = (f32[2,72,256]{2,1,0:T(8,128)S(1)}, f32[2,72,256]{2,1,0:T(8,128)S(1)}, u32[]{:S(2)}, u32[]{:S(2)}) collective-permute-start(f32[2,72,256]{2,1,0:T(8,128)S(1)} %add.23.mine_ref), channel_id=1, source_target_pairs={{0,8},{8,0},{16,24},{24,16},{1,9},{9,1},{17,25},{25,17},{2,10},{10... | collective-permute-start | bytes 442376 | tf_op jit(solution)/shard_map/ppermute | solution.py:555
  44.2 4.4 %collective-permute-start.11 = (f32[8,128]{1,0:T(8,128)S(1)}, f32[8,128]{1,0:T(8,128)S(1)}, u32[]{:S(2)}, u32[]{:S(2)}) collective-permute-start(f32[8,128]{1,0:T(8,128)S(1)} %get-tuple-element.49.refs_0_), channel_id=1, source_target_pairs={{0,1},{1,0},{2,3},{3,2},{4,5},{5,4},{6,7},{7,6},{8,9},{9,8},{10,11... | collective-permute-start | bytes 12296 | tf_op jit(solution)/shard_map/ppermute | solution.py:564
  48.5 6.1 %collective-permute-start.14 = (f32[8,128]{1,0:T(8,128)S(1)}, f32[8,128]{1,0:T(8,128)S(1)}, u32[]{:S(2)}, u32[]{:S(2)}) collective-permute-start(f32[8,128]{1,0:T(8,128)S(1)} %shard_map.112.refs_0_), channel_id=1, source_target_pairs={{0,6},{1,7},{2,0},{3,1},{4,2},{5,3},{6,4},{7,5},{8,14},{9,15},{10,... | collective-permute-start | bytes 12296 | tf_op jit(solution)/shard_map/ppermute | solution.py:564
  53.3 4.5 %collective-permute-start.13 = (f32[8,128]{1,0:T(8,128)S(1)}, f32[8,128]{1,0:T(8,128)S(1)}, u32[]{:S(2)}, u32[]{:S(2)}) collective-permute-start(f32[8,128]{1,0:T(8,128)S(1)} %shard_map.112.refs_0_), channel_id=1, source_target_pairs={{0,4},{1,5},{2,6},{3,7},{4,0},{5,1},{6,2},{7,3},{8,12},{9,13},{10,... | collective-permute-start | bytes 12296 | tf_op jit(solution)/shard_map/ppermute | solution.py:564
  53.3 5.4 %collective-permute-start.12 = (f32[8,128]{1,0:T(8,128)S(1)}, f32[8,128]{1,0:T(8,128)S(1)}, u32[]{:S(2)}, u32[]{:S(2)}) collective-permute-start(f32[8,128]{1,0:T(8,128)S(1)} %shard_map.112.refs_0_), channel_id=1, source_target_pairs={{0,2},{1,3},{2,4},{3,5},{4,6},{5,7},{6,0},{7,1},{8,10},{9,11},{10,... | collective-permute-start | bytes 12296 | tf_op jit(solution)/shard_map/ppermute | solution.py:564

commit v5 on v4

--- a/solution.py
+++ b/solution.py
@@ -60,17 +60,21 @@
     apart = (i - j).astype(F32)
     weight = jnp.exp(-(apart * apart) / (down * across))
     keep = (jnp.abs(apart) <= jnp.minimum(down, across)) & (i < levels) & (j < levels)
-    full = jnp.where(keep, weight, F32(0.0))[: up_to(levels, 8), : up_to(levels, 16)]
-    high = full.astype(jnp.bfloat16)
-    return high, (full - high.astype(F32)).astype(jnp.bfloat16)
+    full = jnp.where(keep, weight, F32(0.0))[: up_to(levels, 8)]
+    high = full.astype(jnp.bfloat16).astype(F32)
+    blank = jnp.zeros(full.shape, F32)
+    deep = up_to(levels, 16)
+    high, low = jnp.concatenate([high, blank], axis=1), jnp.concatenate([full - high, blank], axis=1)
+    stacked = high + pltpu.roll(high, deep, 1) + pltpu.roll(low, 2 * deep, 1)
+    return stacked.astype(jnp.bfloat16)
 
 
 def apply_vertical(vertical, field):
-    v_high, v_low = vertical
     high = field.astype(jnp.bfloat16)
     low = (field - high.astype(F32)).astype(jnp.bfloat16)
-    dot = functools.partial(jnp.dot, preferred_element_type=F32)
-    return dot(v_high, high) + dot(v_high, low) + dot(v_low, high)
+    blank = jnp.zeros((vertical.shape[1] - 3 * field.shape[0], field.shape[1]), jnp.bfloat16)
+    stacked = jnp.concatenate([high, low, high, blank], axis=0)
+    return jnp.dot(vertical, stacked, preferred_element_type=F32)
 
 
 def sine_matrix(width):

time: 60.5 us -> 59.7 us (0.987)
  Pallas kernels: 21 us -> 20.1 us
    pallas_call x10, Pallas kernels: 21 us -> 20.1 us  [call(): pl.pallas_call(kernel, out_shape=tuple((jax.ShapeDtypeStruct(shape, F32)...]
    ppermute x1, waiting for transfers between devices: 1.89 us -> 2.54 us  [per_device(): near_halo = lax.ppermute(near_edge, 'tile', near_pairs)]
    ppermute x4, starting transfers between devices: 8.51 us -> 7.87 us  [per_device(): lax.ppermute(sums, 'tile', rotated('tile', digit, radix, by))]
where the time goes in v5:
time: 59.7 us; the launch traced here: 59.6 us
  waiting for transfers between devices  21.6 us (36%)
  Pallas kernels  20.1 us (34%)
  starting transfers between devices  16.1 us (27%)
  between operations  1.55 us (3%)
    pallas_call x10, Pallas kernels, call(): pl.pallas_call(kernel, out_shape=tuple((jax.ShapeDtypeStruct(shape, F32)...  20.1 us
    ppermute x4, starting transfers between devices, per_device(): lax.ppermute(sums, 'tile', rotated('tile', digit, radix, by))  7.87 us
    ppermute x4, waiting for transfers between devices, per_device(): lax.ppermute(sums, 'tile', rotated('tile', digit, radix, by))  5.98 us
    ppermute x1, waiting for transfers between devices, per_device(): far_mine = far_mine + lax.ppermute(far_mine, 'mem', flipped('mem', bit))  4.33 us
    ppermute x1, waiting for transfers between devices, per_device(): mine = mine + lax.ppermute(mine, 'mem', flipped('mem', bit))  4.22 us
    ppermute x1, waiting for transfers between devices, per_device(): near_mine = near_mine + lax.ppermute(near_mine, 'mem', flipped('mem', bit))  3.18 us
    ppermute x1, starting transfers between devices, per_device(): near_halo = lax.ppermute(near_edge, 'tile', near_pairs)  3.03 us
    ppermute x1, waiting for transfers between devices, per_device(): near_halo = lax.ppermute(near_edge, 'tile', near_pairs)  2.54 us
  transfers between devices with their start and end apart: 15, of which 9 were waited for; matrix products, arithmetic and copies ran while one was open for 0% of the time, Pallas kernels for 25%

profile of v5, /device:TPU:0, one launch (start us, length us, event | category | flops | bytes accessed | tf_op | source)
XLA Modules:
  0.0 59.6 jit_solution(9853804108985418863)
XLA Ops:
  0.7 3.4 %shard_map.106 = f32[2,2,280,128]{3,2,1,0:T(8,128)} custom-call(s32[1,70]{1,0:T(1,128)} %bitcast.11, bf16[2,70,16,256]{3,2,1,0:T(8,128)(2,1)} %members_hbm.3, f32[70,16,256]{2,1,0:T(8,128)} %inc_hbm.3, bf16[256,256]{1,0:T(8,128)(2,1)} %constant.6.clone.s_high_hbm.s_high_ref, bf16[256,256]{1,0:T(8,128)(2,1)} %constant.7.clone.s_low_hbm.s_low_ref), custom_call_target="tpu_custom_call" | custom-call | tf_op jit(solution)/shard_map/pallas_call | solution.py:422
  4.1 3.0 %collective-permute-start.3 = (f32[2,2,280,128]{3,2,1,0:T(8,128)}, f32[2,2,280,128]{3,2,1,0:T(8,128)S(1)}, u32[]{:S(2)}, u32[]{:S(2)}) collective-permute-start(f32[2,2,280,128]{3,2,1,0:T(8,128)} %shard_map.106), channel_id=1, source_target_pairs={{0,1},{1,0},{2,3},{3,2},{4,5},{5,4},{6,7},{7,6},{8,9},{9,8},{10,11... | collective-permute-start | bytes 1720328 | tf_op jit(solution)/shard_map/ppermute | solution.py:501
  7.2 2.0 %shard_map.104 = f32[2,2,280,128]{3,2,1,0:T(8,128)S(1)} custom-call(s32[1,70]{1,0:T(1,128)S(1)} %bitcast.12, bf16[2,70,16,256]{3,2,1,0:T(8,128)(2,1)S(1)} %copy-done.1, f32[70,16,256]{2,1,0:T(8,128)S(1)} %copy-done, bf16[256,256]{1,0:T(8,128)(2,1)S(1)} %copy-done.3, bf16[256,256]{1,0:T(8,128)(2,1)S(1)} %copy-done.2), custom_call_target="tpu_custom_call" | custom-call | tf_op jit(solution)/shard_map/pallas_call | solution.py:422
  9.2 7.8 %shard_map.105 = (f32[4,72,256]{2,1,0:T(8,128)S(1)}, f32[4,72,256]{2,1,0:T(8,128)S(1)}, f32[4,72,256]{2,1,0:T(8,128)S(1)}, f32[4,72,256]{2,1,0:T(8,128)S(1)}, f3...) custom-call(s32[1,70]{1,0:T(1,128)S(1)} %bitcast.13, s32[8]{0:T(128)S(1)} %copy-done.6, ...), custom_call_target="tpu_custom_call" | custom-call | flops 200000000 | bytes 10000000 | tf_op jit(solution)/shard_map/pallas_call | solution.py:422
  17.0 0.7 %collective-permute-start.7 = (f32[2,2,280,128]{3,2,1,0:T(8,128)S(1)}, f32[2,2,280,128]{3,2,1,0:T(8,128)S(1)}, u32[]{:S(2)}, u32[]{:S(2)}) collective-permute-start(f32[2,2,280,128]{3,2,1,0:T(8,128)S(1)} %shard_map.104), channel_id=1, source_target_pairs={{1,2},{2,1},{3,4},{4,3},{5,6},{6,5},{9,10},{10,9},{11,12},{12,11},... | collective-permute-start | bytes 1720328 | tf_op jit(solution)/shard_map/ppermute | solution.py:525
  17.7 0.1 collective-permute-start
  17.8 2.5 %collective-permute-done.3.halo_ref = f32[2,2,280,128]{3,2,1,0:T(8,128)S(1)} collective-permute-done((f32[2,2,280,128]{3,2,1,0:T(8,128)}, f32[2,2,280,128]{3,2,1,0:T(8,128)S(1)}, u32[]{:S(2)}, u32[]{:S(2)}) %collective-permute-start.3) | collective-permute-done | bytes 573472 | tf_op jit(solution)/shard_map/ppermute | solution.py:501
  20.4 1.2 %shard_map.107 = (f32[2,72,256]{2,1,0:T(8,128)S(1)}, f32[2,72,256]{2,1,0:T(8,128)S(1)}) custom-call(s32[8]{0:T(128)S(1)} %copy-done.6, f32[2,2,280,128]{3,2,1,0:T(8,128)S(1)} %collective-permute-done.3.halo_ref, f32[2,4,72,256]{3,2,1,0:T(8,128)S(1)} %get-tuple-element.34.mem_ref, f32[4,72,256]{2,1,0:T(8,128)S(1)} %get-tuple-element.35.cov_ref, ...), custom_call_target="tpu_custom_call" | custom-call | tf_op jit(solution)/shard_map/pallas_call | solution.py:422
  21.6 0.1 collective-permute-start.4
  21.6 1.4 %collective-permute-done.4 = f32[2,72,256]{2,1,0:T(8,128)S(1)} collective-permute-done((f32[2,72,256]{2,1,0:T(8,128)S(1)}, f32[2,72,256]{2,1,0:T(8,128)S(1)}, u32[]{:S(2)}, u32[]{:S(2)}) %collective-permute-start.4) | collective-permute-done | bytes 147488 | tf_op jit(solution)/shard_map/ppermute | solution.py:543
  23.0 1.8 %collective-permute-start.5 = (f32[2,72,256]{2,1,0:T(8,128)S(1)}, f32[2,72,256]{2,1,0:T(8,128)S(1)}, u32[]{:S(2)}, u32[]{:S(2)}) collective-permute-start(f32[2,72,256]{2,1,0:T(8,128)S(1)} %add.20), channel_id=1, source_target_pairs={{0,16},{8,24},{16,0},{24,8},{1,17},{9,25},{17,1},{25,9},{2,18},{10... | collective-permute-start | bytes 442376 | tf_op jit(solution)/shard_map/ppermute | solution.py:545
  24.8 0.4 collective-permute-start.1
  25.2 1.4 %shard_map.108 = (f32[16,72,256]{2,1,0:T(8,128)S(1)}, f32[16,72,256]{2,1,0:T(8,128)S(1)}) custom-call(f32[1120,256]{1,0:T(8,128)S(1)} %bitcast.7, f32[1120,256]{1,0:T(8,128)S(1)} %bitcast.10), custom_call_target="tpu_custom_call" | custom-call | tf_op jit(solution)/shard_map/pallas_call | solution.py:422
  26.6 3.2 %collective-permute-done.5 = f32[2,72,256]{2,1,0:T(8,128)S(1)} collective-permute-done((f32[2,72,256]{2,1,0:T(8,128)S(1)}, f32[2,72,256]{2,1,0:T(8,128)S(1)}, u32[]{:S(2)}, u32[]{:S(2)}) %collective-permute-start.5) | collective-permute-done | bytes 147488 | tf_op jit(solution)/shard_map/ppermute | solution.py:545
  29.8 1.2 %shard_map.110 = (f32[2,72,256]{2,1,0:T(8,128)S(1)}, f32[2,72,256]{2,1,0:T(8,128)S(1)}) custom-call(s32[8]{0:T(128)S(1)} %copy-done.6, f32[2,2,280,128]{3,2,1,0:T(8,128)S(1)} %collective-permute-done.7.halo_ref, f32[2,4,72,256]{3,2,1,0:T(8,128)S(1)} %get-tuple-element.45.mem_ref, f32[4,72,256]{2,1,0:T(8,128)S(1)} %get-tuple-element.46.cov_ref, ...), custom_call_target="tpu_custom_call" | custom-call | tf_op jit(solution)/shard_map/pallas_call | solution.py:422
  31.0 0.1 collective-permute-start.8
  31.1 4.2 %collective-permute-done.1 = f32[4,72,256]{2,1,0:T(8,128)S(1)} collective-permute-done((f32[4,72,256]{2,1,0:T(8,128)S(1)}, f32[4,72,256]{2,1,0:T(8,128)S(1)}, u32[]{:S(2)}, u32[]{:S(2)}) %collective-permute-start.1) | collective-permute-done | bytes 294944 | tf_op jit(solution)/shard_map/ppermute | solution.py:529
  35.3 0.1 collective-permute-start.2
  35.5 1.8 %collective-permute-start.9 = (f32[2,72,256]{2,1,0:T(8,128)S(1)}, f32[2,72,256]{2,1,0:T(8,128)S(1)}, u32[]{:S(2)}, u32[]{:S(2)}) collective-permute-start(f32[2,72,256]{2,1,0:T(8,128)S(1)} %add.22), channel_id=1, source_target_pairs={{0,16},{8,24},{16,0},{24,8},{1,17},{9,25},{17,1},{25,9},{2,18},{10... | collective-permute-start | bytes 442376 | tf_op jit(solution)/shard_map/ppermute | solution.py:558
  37.2 0.2 collective-permute-start.6
  37.4 4.3 %collective-permute-done.9 = f32[2,72,256]{2,1,0:T(8,128)S(1)} collective-permute-done((f32[2,72,256]{2,1,0:T(8,128)S(1)}, f32[2,72,256]{2,1,0:T(8,128)S(1)}, u32[]{:S(2)}, u32[]{:S(2)}) %collective-permute-start.9) | collective-permute-done | bytes 147488 | tf_op jit(solution)/shard_map/ppermute | solution.py:558
  41.8 0.1 collective-permute-start.10
  42.5 1.1 %shard_map.109 = (f32[2,1120,128]{2,1,0:T(8,128)S(1)}, f32[8,128]{1,0:T(8,128)S(1)}) custom-call(f32[1]{0:T(128)S(6)} %copy.11.beta_ref, f32[4,72,256]{2,1,0:T(8,128)S(1)} %add.19.mine_ref, f32[4,72,256]{2,1,0:T(8,128)S(1)} %collective-permute-done.2.other_ref, f32[2,72,256]{2,1,0:T(8,128)S(1)} %add.21.near_mine_ref, ...), custom_call_target="tpu_custom_call" | custom-call | tf_op jit(solution)/shard_map/pallas_call | solution.py:422
  43.6 0.3 shard_map.111
  44.0 2.1 %collective-permute-start.11 = (f32[8,128]{1,0:T(8,128)S(1)}, f32[8,128]{1,0:T(8,128)S(1)}, u32[]{:S(2)}, u32[]{:S(2)}) collective-permute-start(f32[8,128]{1,0:T(8,128)S(1)} %get-tuple-element.49.refs_0_), channel_id=1, source_target_pairs={{0,1},{1,0},{2,3},{3,2},{4,5},{5,4},{6,7},{7,6},{8,9},{9,8},{10,11... | collective-permute-start | bytes 12296 | tf_op jit(solution)/shard_map/ppermute | solution.py:568
  46.1 1.6 %collective-permute-done.11.refs_1_ = f32[8,128]{1,0:T(8,128)S(1)} collective-permute-done((f32[8,128]{1,0:T(8,128)S(1)}, f32[8,128]{1,0:T(8,128)S(1)}, u32[]{:S(2)}, u32[]{:S(2)}) %collective-permute-start.11) | collective-permute-done | bytes 4128 | tf_op jit(solution)/shard_map/ppermute | solution.py:568
  47.7 4.7 %collective-permute-start.14 = (f32[8,128]{1,0:T(8,128)S(1)}, f32[8,128]{1,0:T(8,128)S(1)}, u32[]{:S(2)}, u32[]{:S(2)}) collective-permute-start(f32[8,128]{1,0:T(8,128)S(1)} %shard_map.112.refs_0_), channel_id=1, source_target_pairs={{0,6},{1,7},{2,0},{3,1},{4,2},{5,3},{6,4},{7,5},{8,14},{9,15},{10,... | collective-permute-start | bytes 12296 | tf_op jit(solution)/shard_map/ppermute | solution.py:568
  52.4 1.0 %collective-permute-start.12 = (f32[8,128]{1,0:T(8,128)S(1)}, f32[8,128]{1,0:T(8,128)S(1)}, u32[]{:S(2)}, u32[]{:S(2)}) collective-permute-start(f32[8,128]{1,0:T(8,128)S(1)} %shard_map.112.refs_0_), channel_id=1, source_target_pairs={{0,2},{1,3},{2,4},{3,5},{4,6},{5,7},{6,0},{7,1},{8,10},{9,11},{10,... | collective-permute-start | bytes 12296 | tf_op jit(solution)/shard_map/ppermute | solution.py:568
  53.5 0.3 collective-permute-done.14.refs_3_
  53.8 3.2 %collective-permute-done.13.refs_2_ = f32[8,128]{1,0:T(8,128)S(1)} collective-permute-done((f32[8,128]{1,0:T(8,128)S(1)}, f32[8,128]{1,0:T(8,128)S(1)}, u32[]{:S(2)}, u32[]{:S(2)}) %collective-permute-start.13) | collective-permute-done | bytes 4128 | tf_op jit(solution)/shard_map/ppermute | solution.py:568
  56.9 0.9 %collective-permute-done.12.refs_1_ = f32[8,128]{1,0:T(8,128)S(1)} collective-permute-done((f32[8,128]{1,0:T(8,128)S(1)}, f32[8,128]{1,0:T(8,128)S(1)}, u32[]{:S(2)}, u32[]{:S(2)}) %collective-permute-start.12) | collective-permute-done | bytes 4128 | tf_op jit(solution)/shard_map/ppermute | solution.py:568
  57.9 1.7 %shard_map.113 = (f32[1120,256]{1,0:T(8,128)}, f32[1,2]{1,0:T(1,128)}) custom-call(f32[8,128]{1,0:T(8,128)S(1)} %shard_map.112.refs_0_, f32[8,128]{1,0:T(8,128)S(1)} %collective-permute-done.12.refs_1_, f32[8,128]{1,0:T(8,128)S(1)} %collective-permute-done.13.refs_2_, f32[8,128]{1,0:T(8,128)S(1)} %collective-permute-done.14.refs_3_, ...), custom_call_target="tpu_custom_call" | custom-call | tf_op jit(solution)/shard_map/pallas_call | solution.py:422
  (30 shorter events, 0.2 us)
Async XLA Ops:
  0.6 6.5 %copy-start = (f32[70,16,256]{2,1,0:T(8,128)S(1)}, f32[70,16,256]{2,1,0:T(8,128)}, u32[]{:S(2)}) copy-start(f32[70,16,256]{2,1,0:T(8,128)} %inc_hbm.3) | copy-start | bytes 3440644
  0.6 6.5 %copy-start.1 = (bf16[2,70,16,256]{3,2,1,0:T(8,128)(2,1)S(1)}, bf16[2,70,16,256]{3,2,1,0:T(8,128)(2,1)}, u32[]{:S(2)}) copy-start(bf16[2,70,16,256]{3,2,1,0:T(8,128)(2,1)} %members_hbm.3) | copy-start | bytes 3440644
  0.6 6.5 %copy-start.2 = (bf16[256,256]{1,0:T(8,128)(2,1)S(1)}, bf16[256,256]{1,0:T(8,128)(2,1)}, u32[]{:S(2)}) copy-start(bf16[256,256]{1,0:T(8,128)(2,1)} %constant.7.clone.s_low_hbm.s_low_ref) | copy-start | bytes 393220
  0.7 6.5 %copy-start.3 = (bf16[256,256]{1,0:T(8,128)(2,1)S(1)}, bf16[256,256]{1,0:T(8,128)(2,1)}, u32[]{:S(2)}) copy-start(bf16[256,256]{1,0:T(8,128)(2,1)} %constant.6.clone.s_high_hbm.s_high_ref) | copy-start | bytes 393220
  0.7 6.5 %copy-start.7 = (s32[70]{0:T(128)S(1)}, s32[70]{0:T(128)}, u32[]{:S(2)}) copy-start(s32[70]{0:T(128)} %param.13) | copy-start | bytes 844
  4.1 5.1 %copy-start.5 = (f32[8,256]{1,0:T(8,128)S(1)}, f32[8,256]{1,0:T(8,128)}, u32[]{:S(2)}) copy-start(f32[8,256]{1,0:T(8,128)} %constant.8.clone.waves_ref) | copy-start | bytes 24580
  4.1 5.1 %copy-start.6 = (s32[8]{0:T(128)S(1)}, s32[8]{0:T(128)}, u32[]{:S(2)}) copy-start(s32[8]{0:T(128)} %steps_ref.5) | copy-start | bytes 100
  4.1 16.2 %collective-permute-start.3 = (f32[2,2,280,128]{3,2,1,0:T(8,128)}, f32[2,2,280,128]{3,2,1,0:T(8,128)S(1)}, u32[]{:S(2)}, u32[]{:S(2)}) collective-permute-start(f32[2,2,280,128]{3,2,1,0:T(8,128)} %shard_map.106), channel_id=1, source_target_pairs={{0,1},{1,0},{2,3},{3,2},{4,5},{5,4},{6,7},{7,6},{8,9},{9,8},{10,11... | collective-permute-start | bytes 1720328 | tf_op jit(solution)/shard_map/ppermute | solution.py:501
  17.0 12.8 %collective-permute-start.7 = (f32[2,2,280,128]{3,2,1,0:T(8,128)S(1)}, f32[2,2,280,128]{3,2,1,0:T(8,128)S(1)}, u32[]{:S(2)}, u32[]{:S(2)}) collective-permute-start(f32[2,2,280,128]{3,2,1,0:T(8,128)S(1)} %shard_map.104), channel_id=1, source_target_pairs={{1,2},{2,1},{3,4},{4,3},{5,6},{6,5},{9,10},{10,9},{11,12},{12,11},... | collective-permute-start | bytes 1720328 | tf_op jit(solution)/shard_map/ppermute | solution.py:525
  17.7 7.1 %collective-permute-start = (f32[4,72,256]{2,1,0:T(8,128)S(1)}, f32[4,72,256]{2,1,0:T(8,128)S(1)}, u32[]{:S(2)}, u32[]{:S(2)}) collective-permute-start(f32[4,72,256]{2,1,0:T(8,128)S(1)} %get-tuple-element.32), channel_id=1, source_target_pairs={{0,8},{8,0},{16,24},{24,16},{1,9},{9,1},{17,25},{25,17},{2,10},{10... | collective-permute-start | bytes 884744 | tf_op jit(solution)/shard_map/ppermute | solution.py:527
  20.4 4.9 %copy-start.4 = (f32[70,16,256]{2,1,0:T(8,128)S(1)}, f32[70,16,256]{2,1,0:T(8,128)}, u32[]{:S(2)}) copy-start(f32[70,16,256]{2,1,0:T(8,128)} %param.10) | copy-start | bytes 3440644
  21.6 1.4 %collective-permute-start.4 = (f32[2,72,256]{2,1,0:T(8,128)S(1)}, f32[2,72,256]{2,1,0:T(8,128)S(1)}, u32[]{:S(2)}, u32[]{:S(2)}) collective-permute-start(f32[2,72,256]{2,1,0:T(8,128)S(1)} %get-tuple-element.37), channel_id=1, source_target_pairs={{0,8},{8,0},{16,24},{24,16},{1,9},{9,1},{17,25},{25,17},{2,10},{10... | collective-permute-start | bytes 442376 | tf_op jit(solution)/shard_map/ppermute | solution.py:543
  23.0 6.8 %collective-permute-start.5 = (f32[2,72,256]{2,1,0:T(8,128)S(1)}, f32[2,72,256]{2,1,0:T(8,128)S(1)}, u32[]{:S(2)}, u32[]{:S(2)}) collective-permute-start(f32[2,72,256]{2,1,0:T(8,128)S(1)} %add.20), channel_id=1, source_target_pairs={{0,16},{8,24},{16,0},{24,8},{1,17},{9,25},{17,1},{25,9},{2,18},{10... | collective-permute-start | bytes 442376 | tf_op jit(solution)/shard_map/ppermute | solution.py:545
  24.8 10.5 %collective-permute-start.1 = (f32[4,72,256]{2,1,0:T(8,128)S(1)}, f32[4,72,256]{2,1,0:T(8,128)S(1)}, u32[]{:S(2)}, u32[]{:S(2)}) collective-permute-start(f32[4,72,256]{2,1,0:T(8,128)S(1)} %add.18), channel_id=1, source_target_pairs={{0,16},{8,24},{16,0},{24,8},{1,17},{9,25},{17,1},{25,9},{2,18},{10... | collective-permute-start | bytes 884744 | tf_op jit(solution)/shard_map/ppermute | solution.py:529
  31.0 4.4 %collective-permute-start.8 = (f32[2,72,256]{2,1,0:T(8,128)S(1)}, f32[2,72,256]{2,1,0:T(8,128)S(1)}, u32[]{:S(2)}, u32[]{:S(2)}) collective-permute-start(f32[2,72,256]{2,1,0:T(8,128)S(1)} %get-tuple-element.48), channel_id=1, source_target_pairs={{0,8},{8,0},{16,24},{24,16},{1,9},{9,1},{17,25},{25,17},{2,10},{10... | collective-permute-start | bytes 442376 | tf_op jit(solution)/shard_map/ppermute | solution.py:556
  35.3 7.2 %collective-permute-start.2 = (f32[4,72,256]{2,1,0:T(8,128)S(1)}, f32[4,72,256]{2,1,0:T(8,128)S(1)}, u32[]{:S(2)}, u32[]{:S(2)}) collective-permute-start(f32[4,72,256]{2,1,0:T(8,128)S(1)} %add.19.mine_ref), channel_id=1, source_target_pairs={{0,8},{8,0},{16,24},{24,16},{1,9},{9,1},{17,25},{25,17},{2,10},{10... | collective-permute-start | bytes 884744 | tf_op jit(solution)/shard_map/ppermute | solution.py:530
  35.5 6.3 %collective-permute-start.9 = (f32[2,72,256]{2,1,0:T(8,128)S(1)}, f32[2,72,256]{2,1,0:T(8,128)S(1)}, u32[]{:S(2)}, u32[]{:S(2)}) collective-permute-start(f32[2,72,256]{2,1,0:T(8,128)S(1)} %add.22), channel_id=1, source_target_pairs={{0,16},{8,24},{16,0},{24,8},{1,17},{9,25},{17,1},{25,9},{2,18},{10... | collective-permute-start | bytes 442376 | tf_op jit(solution)/shard_map/ppermute | solution.py:558
  37.2 5.3 %collective-permute-start.6 = (f32[2,72,256]{2,1,0:T(8,128)S(1)}, f32[2,72,256]{2,1,0:T(8,128)S(1)}, u32[]{:S(2)}, u32[]{:S(2)}) collective-permute-start(f32[2,72,256]{2,1,0:T(8,128)S(1)} %add.21.near_mine_ref), channel_id=1, source_target_pairs={{0,8},{8,0},{16,24},{24,16},{1,9},{9,1},{17,25},{25,17},{2,10},{10... | collective-permute-start | bytes 442376 | tf_op jit(solution)/shard_map/ppermute | solution.py:546
  41.8 1.9 %collective-permute-start.10 = (f32[2,72,256]{2,1,0:T(8,128)S(1)}, f32[2,72,256]{2,1,0:T(8,128)S(1)}, u32[]{:S(2)}, u32[]{:S(2)}) collective-permute-start(f32[2,72,256]{2,1,0:T(8,128)S(1)} %add.23.mine_ref), channel_id=1, source_target_pairs={{0,8},{8,0},{16,24},{24,16},{1,9},{9,1},{17,25},{25,17},{2,10},{10... | collective-permute-start | bytes 442376 | tf_op jit(solution)/shard_map/ppermute | solution.py:559
  44.0 3.7 %collective-permute-start.11 = (f32[8,128]{1,0:T(8,128)S(1)}, f32[8,128]{1,0:T(8,128)S(1)}, u32[]{:S(2)}, u32[]{:S(2)}) collective-permute-start(f32[8,128]{1,0:T(8,128)S(1)} %get-tuple-element.49.refs_0_), channel_id=1, source_target_pairs={{0,1},{1,0},{2,3},{3,2},{4,5},{5,4},{6,7},{7,6},{8,9},{9,8},{10,11... | collective-permute-start | bytes 12296 | tf_op jit(solution)/shard_map/ppermute | solution.py:568
  47.7 6.1 %collective-permute-start.14 = (f32[8,128]{1,0:T(8,128)S(1)}, f32[8,128]{1,0:T(8,128)S(1)}, u32[]{:S(2)}, u32[]{:S(2)}) collective-permute-start(f32[8,128]{1,0:T(8,128)S(1)} %shard_map.112.refs_0_), channel_id=1, source_target_pairs={{0,6},{1,7},{2,0},{3,1},{4,2},{5,3},{6,4},{7,5},{8,14},{9,15},{10,... | collective-permute-start | bytes 12296 | tf_op jit(solution)/shard_map/ppermute | solution.py:568
  52.4 4.5 %collective-permute-start.13 = (f32[8,128]{1,0:T(8,128)S(1)}, f32[8,128]{1,0:T(8,128)S(1)}, u32[]{:S(2)}, u32[]{:S(2)}) collective-permute-start(f32[8,128]{1,0:T(8,128)S(1)} %shard_map.112.refs_0_), channel_id=1, source_target_pairs={{0,4},{1,5},{2,6},{3,7},{4,0},{5,1},{6,2},{7,3},{8,12},{9,13},{10,... | collective-permute-start | bytes 12296 | tf_op jit(solution)/shard_map/ppermute | solution.py:568
  52.4 5.4 %collective-permute-start.12 = (f32[8,128]{1,0:T(8,128)S(1)}, f32[8,128]{1,0:T(8,128)S(1)}, u32[]{:S(2)}, u32[]{:S(2)}) collective-permute-start(f32[8,128]{1,0:T(8,128)S(1)} %shard_map.112.refs_0_), channel_id=1, source_target_pairs={{0,2},{1,3},{2,4},{3,5},{4,6},{5,7},{6,0},{7,1},{8,10},{9,11},{10,... | collective-permute-start | bytes 12296 | tf_op jit(solution)/shard_map/ppermute | solution.py:568

commit v6 on v5

--- a/solution.py
+++ b/solution.py
@@ -32,6 +32,12 @@
 def strided(ref, start, count, stride):
     pieces = [ref[piece, pl.ds(start, count, stride=stride), :] for piece in range(ref.shape[0])]
     return jnp.concatenate(pieces, axis=1)
+
+
+def put_row(ref, row, rows, value):
+    for piece in range(ref.shape[0]):
+        part = value[:, piece * 128 : (piece + 1) * 128]
+        ref[piece, pl.ds(row, value.shape[0], stride=rows), :] = part
 
 
 def sweep_counts(steps_ref, tile, tiles):
@@ -112,44 +118,41 @@
     return (1.0 - 4.0 * rate) + rate * waves
 
 
-def edge_kernel(
-    near, rows, levels,
-    bands_hbm, members_hbm, inc_hbm, s_high_hbm, s_low_hbm, out_ref,
-    bands_ref, mem_ref, inc_ref, s_high_ref, s_low_ref, prod_ref, pad_ref, sems,
-):
-    tile = lax.axis_index("tile")
-    high_end = (tile % 2 == 0) == near
-    start = pl.multiple_of(jnp.where(high_end, rows - 8, 0), 8)
-    owned = members_hbm.shape[0]
-    pairs = [(bands_hbm, bands_ref), (inc_hbm.at[:, pl.ds(start, 8), :], inc_ref)]
+def product_kernel(rows, levels, members_hbm, inc_hbm, out_ref, mem_ref, inc_ref, prod_ref, sems):
+    even = lax.axis_index("tile") % 2 == 0
+    start = pl.multiple_of(jnp.where(even, rows - 8, 0), 8)
+    owned, width = members_hbm.shape[0], inc_ref.shape[-1]
+    pairs = [(inc_hbm.at[:, pl.ds(start, 8), :], inc_ref)]
     pairs += [(members_hbm.at[m, :, pl.ds(start, 8), :], mem_ref.at[m]) for m in range(owned)]
-    pairs += [(s_high_hbm, s_high_ref), (s_low_hbm, s_low_ref)]
     copies = [pltpu.make_async_copy(source, target, sems.at[k]) for k, (source, target) in enumerate(pairs)]
     for copy in copies:
         copy.start()
-    width = inc_ref.shape[-1]
+    copies[0].wait()
+    for m in range(owned):
+        copies[1 + m].wait()
+        put_flat(prod_ref, (mem_ref[m].astype(F32) * inc_ref[...]).reshape(levels * 8, width))
+        for q in range(DIFF):
+            put_row(out_ref.at[m], q, DIFF, strided(prod_ref, jnp.where(even, 7 - q, q), levels, 8))
+
+
+def edge_kernel(
+    rows, levels,
+    bands_ref, members_ref, inc_ref, s_high_ref, s_low_ref, out_ref, prod_ref, pad_ref,
+):
+    tile = lax.axis_index("tile")
     deep, tall = up_to(levels, 16), up_to(levels, 8)
-    for piece in range(width // 128):
-        prod_ref[piece, levels * 8 :, :] = jnp.zeros((prod_ref.shape[1] - levels * 8, 128), F32)
-    copies[0].wait()
+    total = rows * levels
     vertical = build_vertical(bands_ref, pad_ref, levels)
-    copies[1].wait()
-    for m in range(owned):
-        copies[2 + m].wait()
-        product = mem_ref[m].astype(F32) * inc_ref[...]
-        put_flat(prod_ref, product.reshape(levels * 8, width))
-        local = []
-        for q in range(DIFF):
-            row = jnp.where(high_end, 7 - q, q)
-            local.append(apply_vertical(vertical, strided(prod_ref, row, deep, 8)))
-        if m == 0:
-            copies[2 + owned].wait()
-            copies[3 + owned].wait()
+    for piece in range(prod_ref.shape[0]):
+        prod_ref[piece, total:, :] = jnp.zeros((prod_ref.shape[1] - total, 128), F32)
+    for m in range(members_ref.shape[0]):
+        put_flat(prod_ref, members_ref[m].astype(F32) * inc_ref[...])
+        local = [
+            apply_vertical(vertical, strided(prod_ref, grid_row(tile, q, rows), deep, rows)) for q in range(DIFF)
+        ]
         waves = transform(jnp.concatenate(local, axis=0), s_high_ref[...], s_low_ref[...])
         for q in range(DIFF):
-            for piece in range(width // 128):
-                part = waves[q * tall : q * tall + levels, piece * 128 : (piece + 1) * 128]
-                out_ref[m, piece, pl.ds(q, levels, stride=DIFF), :] = part
+            put_row(out_ref.at[m], q, DIFF, waves[q * tall : q * tall + levels])
 
 
 def turn_kernel(rows, levels, inc_ref, prev_ref, inc_t_ref, prev_t_ref, flat_ref):
@@ -234,20 +237,34 @@
 
 def halo_kernel(
     near, levels, tiles,
-    steps_ref, halo_ref, mem_ref, cov_ref, s_high_ref, s_low_ref, waves_ref, *refs,
+    bands_ref, steps_ref, halo_ref, mem_ref, cov_ref, s_high_ref, s_low_ref, waves_ref, mine_ref, theirs_ref,
+    spec_ref, base_ref, halo_row_ref, pad_ref,
 ):
-    out_refs, (spec_ref, base_ref) = refs[:-2], refs[-2:]
     counts = sweep_counts(steps_ref, lax.axis_index("tile"), tiles)
     owned, tall, width = halo_ref.shape[0], cov_ref.shape[1], cov_ref.shape[2]
     rate = [[coefficient(k, counts[0]), coefficient(k, counts[1 if near else 2])] for k in range(DIFF)]
     for k in range(DIFF):
         for side in range(2):
             base_ref[k, side] = base_of(rate[k][side], waves_ref[...])
+    if near:
+        vertical = build_vertical(bands_ref, pad_ref, levels)
+        halo_row_ref[levels:, :] = jnp.zeros((halo_row_ref.shape[0] - levels, width), F32)
     sums = [cov_ref[q] for q in range(DIFF)]
     for m in range(owned):
+        if near:
+            local = []
+            for q in range(DIFF):
+                halo_row_ref[:levels, :] = strided(halo_ref.at[m], q, levels, DIFF)
+                local.append(apply_vertical(vertical, halo_row_ref[...]))
+            waves = transform(jnp.concatenate(local, axis=0), s_high_ref[...], s_low_ref[...])
+            for q in range(DIFF):
+                spec_ref[q] = waves[q * tall : (q + 1) * tall]
         for at in range(0, levels, 8):
             size = min(8, levels - at)
-            field = {q: strided(halo_ref.at[m], q + DIFF * at, size, DIFF) for q in range(DIFF)}
+            if near:
+                field = {q: spec_ref[q, at : at + size, :] for q in range(DIFF)}
+            else:
+                field = {q: strided(halo_ref.at[m], q + DIFF * at, size, DIFF) for q in range(DIFF)}
             for k in range(DIFF):
                 kept = range(-1 - k, DIFF - 1 - k)
                 bases = {p: base_ref[k, 0 if p < 0 else 1][:size] for p in kept}
@@ -267,11 +284,11 @@
 
         @pl.when(half == q // part)
         def _(q=q):
-            out_refs[0][q % part] = sums[q]
+            mine_ref[q % part] = sums[q]
 
         @pl.when(half != q // part)
         def _(q=q):
-            out_refs[1][q % part] = sums[q]
+            theirs_ref[q % part] = sums[q]
 
 
 def reduced(value):
@@ -285,12 +302,6 @@
 def ratio(top, bottom):
     some = bottom != 0.0
     return jnp.where(some, top / jnp.where(some, bottom, F32(1.0)), F32(0.0))
-
-
-def put_row(ref, row, rows, value):
-    for piece in range(ref.shape[0]):
-        part = value[:, piece * 128 : (piece + 1) * 128]
-        ref[piece, pl.ds(row, value.shape[0], stride=rows), :] = part
 
 
 def bulk_kernel(
@@ -343,7 +354,8 @@
     return [ref[index : index + 1, :] for index in range(5)]
 
 
-def last_kernel(inverse, beta_ref, sums_ref, mine_ref, other_ref, inc_ref, prev_ref, w_ref, out_ref):
+def last_kernel(inverse, beta_ref, sums_ref, *refs):
+    mine_refs, other_refs, (inc_ref, prev_ref, w_ref, out_ref) = refs[:2], refs[2:4], refs[4:]
     own_half = lax.axis_index("mem") % 2
     part = DIFF // 2
     beta = beta_ref[0]
@@ -353,7 +365,8 @@
     for q in range(DIFF):
         inc = inc_ref[q]
         which, index = divmod(q, part)
-        scaled = inverse * jnp.where(own_half == which, mine_ref[index], other_ref[index])
+        mine, other = (refs[0][index] + refs[1][index] for refs in (mine_refs, other_refs))
+        scaled = inverse * jnp.where(own_half == which, mine, other)
         value = scaled - beta * prev_ref[q]
         w_ref[q] = value
         apart = value - pivot0 * inc
@@ -478,28 +491,27 @@
     far_pairs = [pair for i in range(1, tiles - 1, 2) for pair in ((i, i + 1), (i + 1, i))]
     pad = pltpu.VMEM((8, 128), F32)
 
-    def edges(near):
-        (value,) = call(
-            functools.partial(edge_kernel, near, rows, levels),
-            [("h", bands), ("h", members), ("h", increment), ("h", s_high), ("h", s_low)],
-            [(owned, lanes, DIFF * levels, 128)],
-            [
-                pltpu.VMEM((1, levels), jnp.int32),
-                pltpu.VMEM((owned, levels, 8, width), jnp.bfloat16),
-                pltpu.VMEM((levels, 8, width), F32),
-                pltpu.VMEM((width, width), jnp.bfloat16),
-                pltpu.VMEM((width, width), jnp.bfloat16),
-                pltpu.VMEM((lanes, deep * 8, 128), F32),
-                pad,
-                pltpu.SemaphoreType.DMA((owned + 4,)),
-            ],
-            limit=EDGE_LIMIT if near else VMEM_LIMIT,
-        )
-        return value
-
-    near_edge = edges(True)
+    packed = (owned, lanes, DIFF * levels, 128)
+    (near_edge,) = call(
+        functools.partial(product_kernel, rows, levels),
+        [("h", members), ("h", increment)],
+        [packed],
+        [
+            pltpu.VMEM((owned, levels, 8, width), jnp.bfloat16),
+            pltpu.VMEM((levels, 8, width), F32),
+            pltpu.VMEM((lanes, levels * 8, 128), F32),
+            pltpu.SemaphoreType.DMA((owned + 1,)),
+        ],
+        limit=EDGE_LIMIT,
+    )
     near_halo = lax.ppermute(near_edge, "tile", near_pairs)
-    far_edge = edges(False)
+    mem = members.reshape(owned, levels * rows, width)
+    (far_edge,) = call(
+        functools.partial(edge_kernel, rows, levels),
+        [("v", bands), ("v", mem), ("v", inc), ("v", s_high), ("v", s_low)],
+        [packed],
+        [pltpu.VMEM((lanes, deep * rows, 128), F32), pad],
+    )
     members, far_edge = lax.optimization_barrier((members, far_edge))
     mem = members.reshape(owned, levels * rows, width)
 
@@ -521,7 +533,7 @@
         [(rows, tall, width), (rows, tall, width)],
         [pltpu.VMEM((lanes, tall * rows, 128), F32)],
     )
-    theirs, far_edge = lax.optimization_barrier((theirs, far_edge))
+    theirs, far_edge, inc_t = lax.optimization_barrier((theirs, far_edge, inc_t))
     far_halo = lax.ppermute(far_edge, "tile", far_pairs)
     bits = [1 << k for k in range(1, mems.bit_length() - 1)]
     mine = mine + lax.ppermute(theirs, "mem", flipped("mem", 1))
@@ -532,10 +544,10 @@
     def edge_sum(near, halo, mem_rows, cov, outs):
         return call(
             functools.partial(halo_kernel, near, levels, tiles),
-            [("s", diffusion_steps), ("v", halo), ("v", mem_rows), ("v", cov)]
+            [("v", bands), ("s", diffusion_steps), ("v", halo), ("v", mem_rows), ("v", cov)]
             + [("v", s_high), ("v", s_low), ("v", waves)],
             outs,
-            [pltpu.VMEM(four, F32), pltpu.VMEM((DIFF, 2, 8, width), F32)],
+            [pltpu.VMEM(four, F32), pltpu.VMEM((DIFF, 2, 8, width), F32), pltpu.VMEM((deep, width), F32), pad],
         )
 
     two = (DIFF // 2, tall, width)
@@ -554,12 +566,14 @@
     )
     far_mine, far_theirs = edge_sum(False, far_halo, mem_far, cov_far, [two, two])
     far_mine = far_mine + lax.ppermute(far_theirs, "mem", flipped("mem", 1))
-    for bit in bits:
+    for bit in bits[:-1]:
         far_mine = far_mine + lax.ppermute(far_mine, "mem", flipped("mem", bit))
-    far_other = lax.ppermute(far_mine, "mem", flipped("mem", 1))
+    far_sums = [far_mine, lax.ppermute(far_mine, "mem", flipped("mem", bits[-1]))]
+    far_others = [lax.ppermute(value, "mem", flipped("mem", 1)) for value in far_sums]
     w_far, sums = call(
         functools.partial(last_kernel, inverse),
-        [("s", beta_prev), ("v", sums), ("v", far_mine), ("v", far_other), ("v", inc_t), ("v", prev_t)],
+        [("s", beta_prev), ("v", sums)]
+        + [("v", value) for value in far_sums + far_others + [inc_t, prev_t]],
         [four, (8, 128)],
     )
     digit = 1

time: 59.7 us -> 58 us (0.972)
  waiting for transfers between devices: 21.6 us -> 19.8 us
  Pallas kernels: 20.1 us -> 19.5 us
  starting transfers between devices: 16.1 us -> 16.7 us
    ppermute x4, waiting for transfers between devices: 5.98 us -> 3.72 us  [per_device(): lax.ppermute(sums, 'tile', rotated('tile', digit, radix, by))]
    ppermute x1, waiting for transfers between devices: 3.18 us -> 4.56 us  [per_device(): near_mine = near_mine + lax.ppermute(near_mine, 'mem', flipped('mem', bit))]
    ppermute x2 -> x3, waiting for transfers between devices: 4.33 us -> 4.02 us  [the longest x1 4.02 us: per_device(): lax.ppermute(far_mine, 'mem', flipped('mem', bits[-1]))]
    ppermute x2 -> x3, starting transfers between devices: 1.84 us -> 2.08 us  [the longest x1 1.77 us: per_device(): lax.ppermute(far_mine, 'mem', flipped('mem', bits[-1]))]
  transfers between devices with their start and end apart: 15 -> 16, of which waited for: 9 -> 8; matrix products, arithmetic and copies ran while one was open for 0% -> 0% of each run, Pallas kernels for 25% -> 26%
where the time goes in v6:
time: 58 us; the launch traced here: 57.8 us
  waiting for transfers between devices  19.8 us (34%)
  Pallas kernels  19.5 us (34%)
  starting transfers between devices  16.7 us (29%)
  between operations  1.56 us (3%)
    pallas_call x10, Pallas kernels, call(): pl.pallas_call(kernel, out_shape=tuple((jax.ShapeDtypeStruct(shape, F32)...  19.5 us
    ppermute x4, starting transfers between devices, per_device(): lax.ppermute(sums, 'tile', rotated('tile', digit, radix, by))  8.26 us
    ppermute x1, waiting for transfers between devices, per_device(): near_mine = near_mine + lax.ppermute(near_mine, 'mem', flipped('mem', bit))  4.56 us
    ppermute x1, waiting for transfers between devices, per_device(): mine = mine + lax.ppermute(mine, 'mem', flipped('mem', bit))  4.21 us
    ppermute x1, waiting for transfers between devices, per_device(): lax.ppermute(far_mine, 'mem', flipped('mem', bits[-1]))  4.02 us
    ppermute x4, waiting for transfers between devices, per_device(): lax.ppermute(sums, 'tile', rotated('tile', digit, radix, by))  3.72 us
    ppermute x1, starting transfers between devices, per_device(): near_halo = lax.ppermute(near_edge, 'tile', near_pairs)  3.03 us
    ppermute x1, waiting for transfers between devices, per_device(): near_halo = lax.ppermute(near_edge, 'tile', near_pairs)  1.96 us
  transfers between devices with their start and end apart: 16, of which 8 were waited for; matrix products, arithmetic and copies ran while one was open for 0% of the time, Pallas kernels for 26%

profile of v6, /device:TPU:0, one launch (start us, length us, event | category | flops | bytes accessed | tf_op | source)
XLA Modules:
  0.0 57.8 jit_solution(13755535023930072988)
XLA Ops:
  0.7 2.4 %shard_map.107 = f32[2,2,280,128]{3,2,1,0:T(8,128)} custom-call(bf16[2,70,16,256]{3,2,1,0:T(8,128)(2,1)} %members_hbm.1, f32[70,16,256]{2,1,0:T(8,128)} %inc_hbm.1), custom_call_target="tpu_custom_call" | custom-call | tf_op jit(solution)/shard_map/pallas_call | solution.py:435
  3.1 3.0 %collective-permute-start.3 = (f32[2,2,280,128]{3,2,1,0:T(8,128)}, f32[2,2,280,128]{3,2,1,0:T(8,128)S(1)}, u32[]{:S(2)}, u32[]{:S(2)}) collective-permute-start(f32[2,2,280,128]{3,2,1,0:T(8,128)} %shard_map.107), channel_id=1, source_target_pairs={{0,1},{1,0},{2,3},{3,2},{4,5},{5,4},{6,7},{7,6},{8,9},{9,8},{10,11... | collective-permute-start | bytes 1720328 | tf_op jit(solution)/shard_map/ppermute | solution.py:507
  6.2 1.2 %shard_map.104 = f32[2,2,280,128]{3,2,1,0:T(8,128)S(1)} custom-call(s32[1,70]{1,0:T(1,128)S(1)} %bitcast.14, bf16[2,1120,256]{2,1,0:T(8,128)(2,1)S(1)} %bitcast.11, f32[1120,256]{1,0:T(8,128)S(1)} %bitcast.7, bf16[256,256]{1,0:T(8,128)(2,1)S(1)} %copy-done.2, bf16[256,256]{1,0:T(8,128)(2,1)S(1)} %copy-done.3), custom_call_target="tpu_custom_call" | custom-call | tf_op jit(solution)/shard_map/pallas_call | solution.py:435
  7.4 7.8 %shard_map.105 = (f32[4,72,256]{2,1,0:T(8,128)S(1)}, f32[4,72,256]{2,1,0:T(8,128)S(1)}, f32[4,72,256]{2,1,0:T(8,128)S(1)}, f32[4,72,256]{2,1,0:T(8,128)S(1)}, f3...) custom-call(s32[1,70]{1,0:T(1,128)S(1)} %bitcast.15, s32[8]{0:T(128)S(1)} %copy-done.7, ...), custom_call_target="tpu_custom_call" | custom-call | flops 200000000 | bytes 10000000 | tf_op jit(solution)/shard_map/pallas_call | solution.py:435
  15.2 1.4 %shard_map.106 = (f32[16,72,256]{2,1,0:T(8,128)S(1)}, f32[16,72,256]{2,1,0:T(8,128)S(1)}) custom-call(f32[1120,256]{1,0:T(8,128)S(1)} %bitcast.9, f32[1120,256]{1,0:T(8,128)S(1)} %bitcast.13), custom_call_target="tpu_custom_call" | custom-call | tf_op jit(solution)/shard_map/pallas_call | solution.py:435
  16.6 0.7 %collective-permute-start.7 = (f32[2,2,280,128]{3,2,1,0:T(8,128)S(1)}, f32[2,2,280,128]{3,2,1,0:T(8,128)S(1)}, u32[]{:S(2)}, u32[]{:S(2)}) collective-permute-start(f32[2,2,280,128]{3,2,1,0:T(8,128)S(1)} %shard_map.104), channel_id=1, source_target_pairs={{1,2},{2,1},{3,4},{4,3},{5,6},{6,5},{9,10},{10,9},{11,12},{12,11},... | collective-permute-start | bytes 1720328 | tf_op jit(solution)/shard_map/ppermute | solution.py:537
  17.3 0.1 collective-permute-start
  17.4 2.0 %collective-permute-done.3.halo_ref = f32[2,2,280,128]{3,2,1,0:T(8,128)S(1)} collective-permute-done((f32[2,2,280,128]{3,2,1,0:T(8,128)}, f32[2,2,280,128]{3,2,1,0:T(8,128)S(1)}, u32[]{:S(2)}, u32[]{:S(2)}) %collective-permute-start.3) | collective-permute-done | bytes 573472 | tf_op jit(solution)/shard_map/ppermute | solution.py:507
  19.4 2.4 %shard_map.108 = (f32[2,72,256]{2,1,0:T(8,128)S(1)}, f32[2,72,256]{2,1,0:T(8,128)S(1)}) custom-call(s32[1,70]{1,0:T(1,128)S(1)} %bitcast.16, s32[8]{0:T(128)S(1)} %copy-done.7, f32[2,2,280,128]{3,2,1,0:T(8,128)S(1)} %collective-permute-done.3.halo_ref, f32[2,4,72,256]{3,2,1,0:T(8,128)S(1)} %get-tuple-element.37.mem_ref, ...), custom_call_target="tpu_custom_call" | custom-call | tf_op jit(solution)/shard_map/pallas_call | solution.py:435
  21.8 0.1 collective-permute-start.4
  21.8 1.4 %collective-permute-done.4 = f32[2,72,256]{2,1,0:T(8,128)S(1)} collective-permute-done((f32[2,72,256]{2,1,0:T(8,128)S(1)}, f32[2,72,256]{2,1,0:T(8,128)S(1)}, u32[]{:S(2)}, u32[]{:S(2)}) %collective-permute-start.4) | collective-permute-done | bytes 147488 | tf_op jit(solution)/shard_map/ppermute | solution.py:555
  23.2 1.8 %collective-permute-start.5 = (f32[2,72,256]{2,1,0:T(8,128)S(1)}, f32[2,72,256]{2,1,0:T(8,128)S(1)}, u32[]{:S(2)}, u32[]{:S(2)}) collective-permute-start(f32[2,72,256]{2,1,0:T(8,128)S(1)} %add.17), channel_id=1, source_target_pairs={{0,16},{8,24},{16,0},{24,8},{1,17},{9,25},{17,1},{25,9},{2,18},{10... | collective-permute-start | bytes 442376 | tf_op jit(solution)/shard_map/ppermute | solution.py:557
  25.0 0.4 collective-permute-start.1
  25.4 4.6 %collective-permute-done.5 = f32[2,72,256]{2,1,0:T(8,128)S(1)} collective-permute-done((f32[2,72,256]{2,1,0:T(8,128)S(1)}, f32[2,72,256]{2,1,0:T(8,128)S(1)}, u32[]{:S(2)}, u32[]{:S(2)}) %collective-permute-start.5) | collective-permute-done | bytes 147488 | tf_op jit(solution)/shard_map/ppermute | solution.py:557
  30.0 1.2 %shard_map.110 = (f32[2,72,256]{2,1,0:T(8,128)S(1)}, f32[2,72,256]{2,1,0:T(8,128)S(1)}) custom-call(s32[1,70]{1,0:T(1,128)S(1)} %bitcast.17, s32[8]{0:T(128)S(1)} %copy-done.7, f32[2,2,280,128]{3,2,1,0:T(8,128)S(1)} %collective-permute-done.7.halo_ref, f32[2,4,72,256]{3,2,1,0:T(8,128)S(1)} %get-tuple-element.47.mem_ref, ...), custom_call_target="tpu_custom_call" | custom-call | tf_op jit(solution)/shard_map/pallas_call | solution.py:435
  31.2 0.1 collective-permute-start.8
  31.3 4.2 %collective-permute-done.1 = f32[4,72,256]{2,1,0:T(8,128)S(1)} collective-permute-done((f32[4,72,256]{2,1,0:T(8,128)S(1)}, f32[4,72,256]{2,1,0:T(8,128)S(1)}, u32[]{:S(2)}, u32[]{:S(2)}) %collective-permute-start.1) | collective-permute-done | bytes 294944 | tf_op jit(solution)/shard_map/ppermute | solution.py:541
  35.6 0.1 collective-permute-start.2
  35.7 1.8 %collective-permute-start.9 = (f32[2,72,256]{2,1,0:T(8,128)S(1)}, f32[2,72,256]{2,1,0:T(8,128)S(1)}, u32[]{:S(2)}, u32[]{:S(2)}) collective-permute-start(f32[2,72,256]{2,1,0:T(8,128)S(1)} %add.19.refs_0_), channel_id=1, source_target_pairs={{0,16},{8,24},{16,0},{24,8},{1,17},{9,25},{17,1},{25,9},{2,18},{10... | collective-permute-start | bytes 442376 | tf_op jit(solution)/shard_map/ppermute | solution.py:571
  37.4 0.2 collective-permute-start.6
  37.6 0.3 collective-permute-start.10
  38.0 4.0 %collective-permute-done.9.refs_1_ = f32[2,72,256]{2,1,0:T(8,128)S(1)} collective-permute-done((f32[2,72,256]{2,1,0:T(8,128)S(1)}, f32[2,72,256]{2,1,0:T(8,128)S(1)}, u32[]{:S(2)}, u32[]{:S(2)}) %collective-permute-start.9) | collective-permute-done | bytes 147488 | tf_op jit(solution)/shard_map/ppermute | solution.py:571
  42.6 1.1 %shard_map.109 = (f32[2,1120,128]{2,1,0:T(8,128)S(1)}, f32[8,128]{1,0:T(8,128)S(1)}) custom-call(f32[1]{0:T(128)S(6)} %copy.11.beta_ref, f32[4,72,256]{2,1,0:T(8,128)S(1)} %add.16.mine_ref, f32[4,72,256]{2,1,0:T(8,128)S(1)} %collective-permute-done.2.other_ref, f32[2,72,256]{2,1,0:T(8,128)S(1)} %add.18.near_mine_ref, ...), custom_call_target="tpu_custom_call" | custom-call | tf_op jit(solution)/shard_map/pallas_call | solution.py:435
  43.8 0.4 shard_map.111
  44.1 2.7 %collective-permute-start.12 = (f32[8,128]{1,0:T(8,128)S(1)}, f32[8,128]{1,0:T(8,128)S(1)}, u32[]{:S(2)}, u32[]{:S(2)}) collective-permute-start(f32[8,128]{1,0:T(8,128)S(1)} %get-tuple-element.51.refs_0_), channel_id=1, source_target_pairs={{0,1},{1,0},{2,3},{3,2},{4,5},{5,4},{6,7},{7,6},{8,9},{9,8},{10,11... | collective-permute-start | bytes 12296 | tf_op jit(solution)/shard_map/ppermute | solution.py:582
  46.8 1.6 %collective-permute-done.12.refs_1_ = f32[8,128]{1,0:T(8,128)S(1)} collective-permute-done((f32[8,128]{1,0:T(8,128)S(1)}, f32[8,128]{1,0:T(8,128)S(1)}, u32[]{:S(2)}, u32[]{:S(2)}) %collective-permute-start.12) | collective-permute-done | bytes 4128 | tf_op jit(solution)/shard_map/ppermute | solution.py:582
  48.4 1.6 %collective-permute-start.13 = (f32[8,128]{1,0:T(8,128)S(1)}, f32[8,128]{1,0:T(8,128)S(1)}, u32[]{:S(2)}, u32[]{:S(2)}) collective-permute-start(f32[8,128]{1,0:T(8,128)S(1)} %shard_map.112.refs_0_), channel_id=1, source_target_pairs={{0,2},{1,3},{2,4},{3,5},{4,6},{5,7},{6,0},{7,1},{8,10},{9,11},{10,... | collective-permute-start | bytes 12296 | tf_op jit(solution)/shard_map/ppermute | solution.py:582
  50.1 2.5 %collective-permute-start.14 = (f32[8,128]{1,0:T(8,128)S(1)}, f32[8,128]{1,0:T(8,128)S(1)}, u32[]{:S(2)}, u32[]{:S(2)}) collective-permute-start(f32[8,128]{1,0:T(8,128)S(1)} %shard_map.112.refs_0_), channel_id=1, source_target_pairs={{0,4},{1,5},{2,6},{3,7},{4,0},{5,1},{6,2},{7,3},{8,12},{9,13},{10,... | collective-permute-start | bytes 12296 | tf_op jit(solution)/shard_map/ppermute | solution.py:582
  52.5 1.5 %collective-permute-start.15 = (f32[8,128]{1,0:T(8,128)S(1)}, f32[8,128]{1,0:T(8,128)S(1)}, u32[]{:S(2)}, u32[]{:S(2)}) collective-permute-start(f32[8,128]{1,0:T(8,128)S(1)} %shard_map.112.refs_0_), channel_id=1, source_target_pairs={{0,6},{1,7},{2,0},{3,1},{4,2},{5,3},{6,4},{7,5},{8,14},{9,15},{10,... | collective-permute-start | bytes 12296 | tf_op jit(solution)/shard_map/ppermute | solution.py:582
  54.0 0.6 collective-permute-done.14.refs_2_
  54.6 1.6 %collective-permute-done.15.refs_3_ = f32[8,128]{1,0:T(8,128)S(1)} collective-permute-done((f32[8,128]{1,0:T(8,128)S(1)}, f32[8,128]{1,0:T(8,128)S(1)}, u32[]{:S(2)}, u32[]{:S(2)}) %collective-permute-start.15) | collective-permute-done | bytes 4128 | tf_op jit(solution)/shard_map/ppermute | solution.py:582
  56.1 1.7 %shard_map.113 = (f32[1120,256]{1,0:T(8,128)}, f32[1,2]{1,0:T(1,128)}) custom-call(f32[8,128]{1,0:T(8,128)S(1)} %shard_map.112.refs_0_, f32[8,128]{1,0:T(8,128)S(1)} %collective-permute-done.13.refs_1_, f32[8,128]{1,0:T(8,128)S(1)} %collective-permute-done.14.refs_2_, f32[8,128]{1,0:T(8,128)S(1)} %collective-permute-done.15.refs_3_, ...), custom_call_target="tpu_custom_call" | custom-call | tf_op jit(solution)/shard_map/pallas_call | solution.py:435
  (31 shorter events, 0.2 us)
Async XLA Ops:
  0.6 5.5 %copy-start.2 = (bf16[256,256]{1,0:T(8,128)(2,1)S(1)}, bf16[256,256]{1,0:T(8,128)(2,1)}, u32[]{:S(2)}) copy-start(bf16[256,256]{1,0:T(8,128)(2,1)} %constant.6.clone.s_high_ref) | copy-start | bytes 393220
  0.6 5.5 %copy-start.3 = (bf16[256,256]{1,0:T(8,128)(2,1)S(1)}, bf16[256,256]{1,0:T(8,128)(2,1)}, u32[]{:S(2)}) copy-start(bf16[256,256]{1,0:T(8,128)(2,1)} %constant.7.clone.s_low_ref) | copy-start | bytes 393220
  0.7 5.5 %copy-start = (f32[70,16,256]{2,1,0:T(8,128)S(1)}, f32[70,16,256]{2,1,0:T(8,128)}, u32[]{:S(2)}) copy-start(f32[70,16,256]{2,1,0:T(8,128)} %inc_hbm.1) | copy-start | bytes 3440644
  0.7 5.5 %copy-start.1 = (bf16[2,70,16,256]{3,2,1,0:T(8,128)(2,1)S(1)}, bf16[2,70,16,256]{3,2,1,0:T(8,128)(2,1)}, u32[]{:S(2)}) copy-start(bf16[2,70,16,256]{3,2,1,0:T(8,128)(2,1)} %members_hbm.1) | copy-start | bytes 3440644
  0.7 5.5 %copy-start.6 = (s32[70]{0:T(128)S(1)}, s32[70]{0:T(128)}, u32[]{:S(2)}) copy-start(s32[70]{0:T(128)} %param.13) | copy-start | bytes 844
  3.1 16.2 %collective-permute-start.3 = (f32[2,2,280,128]{3,2,1,0:T(8,128)}, f32[2,2,280,128]{3,2,1,0:T(8,128)S(1)}, u32[]{:S(2)}, u32[]{:S(2)}) collective-permute-start(f32[2,2,280,128]{3,2,1,0:T(8,128)} %shard_map.107), channel_id=1, source_target_pairs={{0,1},{1,0},{2,3},{3,2},{4,5},{5,4},{6,7},{7,6},{8,9},{9,8},{10,11... | collective-permute-start | bytes 1720328 | tf_op jit(solution)/shard_map/ppermute | solution.py:507
  6.2 1.2 %copy-start.5 = (f32[8,256]{1,0:T(8,128)S(1)}, f32[8,256]{1,0:T(8,128)}, u32[]{:S(2)}) copy-start(f32[8,256]{1,0:T(8,128)} %constant.8.clone.waves_ref) | copy-start | bytes 24580
  6.2 1.2 %copy-start.7 = (s32[8]{0:T(128)S(1)}, s32[8]{0:T(128)}, u32[]{:S(2)}) copy-start(s32[8]{0:T(128)} %steps_ref.5) | copy-start | bytes 100
  7.4 7.8 %copy-start.4 = (f32[70,16,256]{2,1,0:T(8,128)S(1)}, f32[70,16,256]{2,1,0:T(8,128)}, u32[]{:S(2)}) copy-start(f32[70,16,256]{2,1,0:T(8,128)} %param.10) | copy-start | bytes 3440644
  16.6 13.4 %collective-permute-start.7 = (f32[2,2,280,128]{3,2,1,0:T(8,128)S(1)}, f32[2,2,280,128]{3,2,1,0:T(8,128)S(1)}, u32[]{:S(2)}, u32[]{:S(2)}) collective-permute-start(f32[2,2,280,128]{3,2,1,0:T(8,128)S(1)} %shard_map.104), channel_id=1, source_target_pairs={{1,2},{2,1},{3,4},{4,3},{5,6},{6,5},{9,10},{10,9},{11,12},{12,11},... | collective-permute-start | bytes 1720328 | tf_op jit(solution)/shard_map/ppermute | solution.py:537
  17.3 7.7 %collective-permute-start = (f32[4,72,256]{2,1,0:T(8,128)S(1)}, f32[4,72,256]{2,1,0:T(8,128)S(1)}, u32[]{:S(2)}, u32[]{:S(2)}) collective-permute-start(f32[4,72,256]{2,1,0:T(8,128)S(1)} %get-tuple-element.35), channel_id=1, source_target_pairs={{0,8},{8,0},{16,24},{24,16},{1,9},{9,1},{17,25},{25,17},{2,10},{10... | collective-permute-start | bytes 884744 | tf_op jit(solution)/shard_map/ppermute | solution.py:539
  21.8 1.4 %collective-permute-start.4 = (f32[2,72,256]{2,1,0:T(8,128)S(1)}, f32[2,72,256]{2,1,0:T(8,128)S(1)}, u32[]{:S(2)}, u32[]{:S(2)}) collective-permute-start(f32[2,72,256]{2,1,0:T(8,128)S(1)} %get-tuple-element.40), channel_id=1, source_target_pairs={{0,8},{8,0},{16,24},{24,16},{1,9},{9,1},{17,25},{25,17},{2,10},{10... | collective-permute-start | bytes 442376 | tf_op jit(solution)/shard_map/ppermute | solution.py:555
  23.2 6.8 %collective-permute-start.5 = (f32[2,72,256]{2,1,0:T(8,128)S(1)}, f32[2,72,256]{2,1,0:T(8,128)S(1)}, u32[]{:S(2)}, u32[]{:S(2)}) collective-permute-start(f32[2,72,256]{2,1,0:T(8,128)S(1)} %add.17), channel_id=1, source_target_pairs={{0,16},{8,24},{16,0},{24,8},{1,17},{9,25},{17,1},{25,9},{2,18},{10... | collective-permute-start | bytes 442376 | tf_op jit(solution)/shard_map/ppermute | solution.py:557
  25.0 10.5 %collective-permute-start.1 = (f32[4,72,256]{2,1,0:T(8,128)S(1)}, f32[4,72,256]{2,1,0:T(8,128)S(1)}, u32[]{:S(2)}, u32[]{:S(2)}) collective-permute-start(f32[4,72,256]{2,1,0:T(8,128)S(1)} %add.15), channel_id=1, source_target_pairs={{0,16},{8,24},{16,0},{24,8},{1,17},{9,25},{17,1},{25,9},{2,18},{10... | collective-permute-start | bytes 884744 | tf_op jit(solution)/shard_map/ppermute | solution.py:541
  31.2 4.4 %collective-permute-start.8 = (f32[2,72,256]{2,1,0:T(8,128)S(1)}, f32[2,72,256]{2,1,0:T(8,128)S(1)}, u32[]{:S(2)}, u32[]{:S(2)}) collective-permute-start(f32[2,72,256]{2,1,0:T(8,128)S(1)} %get-tuple-element.50), channel_id=1, source_target_pairs={{0,8},{8,0},{16,24},{24,16},{1,9},{9,1},{17,25},{25,17},{2,10},{10... | collective-permute-start | bytes 442376 | tf_op jit(solution)/shard_map/ppermute | solution.py:568
  35.6 7.1 %collective-permute-start.2 = (f32[4,72,256]{2,1,0:T(8,128)S(1)}, f32[4,72,256]{2,1,0:T(8,128)S(1)}, u32[]{:S(2)}, u32[]{:S(2)}) collective-permute-start(f32[4,72,256]{2,1,0:T(8,128)S(1)} %add.16.mine_ref), channel_id=1, source_target_pairs={{0,8},{8,0},{16,24},{24,16},{1,9},{9,1},{17,25},{25,17},{2,10},{10... | collective-permute-start | bytes 884744 | tf_op jit(solution)/shard_map/ppermute | solution.py:542
  35.7 6.3 %collective-permute-start.9 = (f32[2,72,256]{2,1,0:T(8,128)S(1)}, f32[2,72,256]{2,1,0:T(8,128)S(1)}, u32[]{:S(2)}, u32[]{:S(2)}) collective-permute-start(f32[2,72,256]{2,1,0:T(8,128)S(1)} %add.19.refs_0_), channel_id=1, source_target_pairs={{0,16},{8,24},{16,0},{24,8},{1,17},{9,25},{17,1},{25,9},{2,18},{10... | collective-permute-start | bytes 442376 | tf_op jit(solution)/shard_map/ppermute | solution.py:571
  37.4 5.2 %collective-permute-start.6 = (f32[2,72,256]{2,1,0:T(8,128)S(1)}, f32[2,72,256]{2,1,0:T(8,128)S(1)}, u32[]{:S(2)}, u32[]{:S(2)}) collective-permute-start(f32[2,72,256]{2,1,0:T(8,128)S(1)} %add.18.near_mine_ref), channel_id=1, source_target_pairs={{0,8},{8,0},{16,24},{24,16},{1,9},{9,1},{17,25},{25,17},{2,10},{10... | collective-permute-start | bytes 442376 | tf_op jit(solution)/shard_map/ppermute | solution.py:558
  37.6 6.1 %collective-permute-start.10 = (f32[2,72,256]{2,1,0:T(8,128)S(1)}, f32[2,72,256]{2,1,0:T(8,128)S(1)}, u32[]{:S(2)}, u32[]{:S(2)}) collective-permute-start(f32[2,72,256]{2,1,0:T(8,128)S(1)} %add.19.refs_0_), channel_id=1, source_target_pairs={{0,8},{8,0},{16,24},{24,16},{1,9},{9,1},{17,25},{25,17},{2,10},{10... | collective-permute-start | bytes 442376 | tf_op jit(solution)/shard_map/ppermute | solution.py:572
  42.0 1.8 %collective-permute-start.11 = (f32[2,72,256]{2,1,0:T(8,128)S(1)}, f32[2,72,256]{2,1,0:T(8,128)S(1)}, u32[]{:S(2)}, u32[]{:S(2)}) collective-permute-start(f32[2,72,256]{2,1,0:T(8,128)S(1)} %collective-permute-done.9.refs_1_), channel_id=1, source_target_pairs={{0,8},{8,0},{16,24},{24,16},{1,9},{9,1},{17,25},{25,17},{2,10},{10... | collective-permute-start | bytes 442376 | tf_op jit(solution)/shard_map/ppermute | solution.py:572
  44.1 4.3 %collective-permute-start.12 = (f32[8,128]{1,0:T(8,128)S(1)}, f32[8,128]{1,0:T(8,128)S(1)}, u32[]{:S(2)}, u32[]{:S(2)}) collective-permute-start(f32[8,128]{1,0:T(8,128)S(1)} %get-tuple-element.51.refs_0_), channel_id=1, source_target_pairs={{0,1},{1,0},{2,3},{3,2},{4,5},{5,4},{6,7},{7,6},{8,9},{9,8},{10,11... | collective-permute-start | bytes 12296 | tf_op jit(solution)/shard_map/ppermute | solution.py:582
  48.4 5.6 %collective-permute-start.13 = (f32[8,128]{1,0:T(8,128)S(1)}, f32[8,128]{1,0:T(8,128)S(1)}, u32[]{:S(2)}, u32[]{:S(2)}) collective-permute-start(f32[8,128]{1,0:T(8,128)S(1)} %shard_map.112.refs_0_), channel_id=1, source_target_pairs={{0,2},{1,3},{2,4},{3,5},{4,6},{5,7},{6,0},{7,1},{8,10},{9,11},{10,... | collective-permute-start | bytes 12296 | tf_op jit(solution)/shard_map/ppermute | solution.py:582
  50.1 4.5 %collective-permute-start.14 = (f32[8,128]{1,0:T(8,128)S(1)}, f32[8,128]{1,0:T(8,128)S(1)}, u32[]{:S(2)}, u32[]{:S(2)}) collective-permute-start(f32[8,128]{1,0:T(8,128)S(1)} %shard_map.112.refs_0_), channel_id=1, source_target_pairs={{0,4},{1,5},{2,6},{3,7},{4,0},{5,1},{6,2},{7,3},{8,12},{9,13},{10,... | collective-permute-start | bytes 12296 | tf_op jit(solution)/shard_map/ppermute | solution.py:582
  52.5 3.6 %collective-permute-start.15 = (f32[8,128]{1,0:T(8,128)S(1)}, f32[8,128]{1,0:T(8,128)S(1)}, u32[]{:S(2)}, u32[]{:S(2)}) collective-permute-start(f32[8,128]{1,0:T(8,128)S(1)} %shard_map.112.refs_0_), channel_id=1, source_target_pairs={{0,6},{1,7},{2,0},{3,1},{4,2},{5,3},{6,4},{7,5},{8,14},{9,15},{10,... | collective-permute-start | bytes 12296 | tf_op jit(solution)/shard_map/ppermute | solution.py:582

commit v7 on v6

--- a/solution.py
+++ b/solution.py
@@ -135,9 +135,18 @@
             put_row(out_ref.at[m], q, DIFF, strided(prod_ref, jnp.where(even, 7 - q, q), levels, 8))
 
 
+def half_span(levels):
+    return up_to(-(-levels // 2), 2)
+
+
+def core():
+    return lax.axis_index("mem") % 2
+
+
 def edge_kernel(
     rows, levels,
-    bands_ref, members_ref, inc_ref, s_high_ref, s_low_ref, out_ref, prod_ref, pad_ref,
+    bands_ref, members_ref, inc_ref, s_high_ref, s_low_ref,
+    far_own_ref, far_other_ref, mem_own_ref, mem_other_ref, prod_ref, pad_ref, wave_ref, pack_ref,
 ):
     tile = lax.axis_index("tile")
     deep, tall = up_to(levels, 16), up_to(levels, 8)
@@ -146,13 +155,21 @@
     for piece in range(prod_ref.shape[0]):
         prod_ref[piece, total:, :] = jnp.zeros((prod_ref.shape[1] - total, 128), F32)
     for m in range(members_ref.shape[0]):
-        put_flat(prod_ref, members_ref[m].astype(F32) * inc_ref[...])
+        member = members_ref[m].astype(F32)
+        put_flat(prod_ref, member * inc_ref[...])
         local = [
             apply_vertical(vertical, strided(prod_ref, grid_row(tile, q, rows), deep, rows)) for q in range(DIFF)
         ]
         waves = transform(jnp.concatenate(local, axis=0), s_high_ref[...], s_low_ref[...])
+        put_flat(prod_ref, member)
         for q in range(DIFF):
-            put_row(out_ref.at[m], q, DIFF, waves[q * tall : q * tall + levels])
+            put_row(wave_ref.at[m], q, DIFF, waves[q * tall : q * tall + levels])
+            put_row(pack_ref.at[m], q, DIFF, strided(prod_ref, grid_row(tile, q, rows), levels, rows))
+    size = half_span(levels)
+    for pack, own_ref, other_ref in ((wave_ref, far_own_ref, far_other_ref), (pack_ref, mem_own_ref, mem_other_ref)):
+        for part, ref in ((core(), own_ref), (1 - core(), other_ref)):
+            low = pl.multiple_of(part * (levels - size) * DIFF, 8)
+            ref[...] = pack[:, :, pl.ds(low, size * DIFF), :]
 
 
 def turn_kernel(rows, levels, inc_ref, prev_ref, inc_t_ref, prev_t_ref, flat_ref):
@@ -168,7 +185,7 @@
 def own_kernel(
     rows, levels, tiles,
     bands_ref, steps_ref, members_ref, inc_ref, s_high_ref, s_low_ref, waves_ref,
-    mine_ref, theirs_ref, cov_near_ref, cov_far_ref, mem_near_ref, mem_far_ref,
+    mine_ref, theirs_ref, cov_near_ref, cov_far_ref, cov_other_ref, mem_near_ref,
     prod_ref, memf_ref, spec_ref, acc_ref, base_ref, pad_ref,
 ):
     tile = lax.axis_index("tile")
@@ -220,75 +237,107 @@
             for k in range(group):
                 row = first + k
                 member = row_of(memf_ref, row, tall)
-                if row < DIFF:
-                    mem_far_ref[m, row] = member
                 if row >= rows - DIFF:
                     mem_near_ref[m, rows - 1 - row] = member
                 value = member * block[k * tall : (k + 1) * tall]
                 acc_ref[row] = value if m == 0 else acc_ref[row] + value
     part = (rows - 2 * DIFF) // 2
+    size = half_span(levels)
+    blank = jnp.zeros((cov_far_ref.shape[1] - size, width), F32)
     for q in range(DIFF):
-        cov_far_ref[q] = acc_ref[q]
         cov_near_ref[q] = acc_ref[rows - 1 - q]
+        halves = (acc_ref[q, :size], acc_ref[q, levels - size : levels])
+        for ref, first in ((cov_far_ref, half == 0), (cov_other_ref, half == 1)):
+            ref[q, :size] = jnp.where(first, halves[0], halves[1])
+            ref[q, size:] = blank
     for q in range(part):
         mine_ref[q] = acc_ref[DIFF + half * part + q]
         theirs_ref[q] = acc_ref[DIFF + (1 - half) * part + q]
 
 
-def halo_kernel(
-    near, levels, tiles,
+def settle(field, rates, base_ref, size):
+    for k in range(DIFF):
+        kept = range(-1 - k, DIFF - 1 - k)
+        bases = {p: base_ref[k, 0 if p < 0 else 1][:size] for p in kept}
+        field = advance(field, {p: rates[k][0 if p < 0 else 1] for p in kept}, bases)
+    return [field[-1 - q] for q in range(DIFF)]
+
+
+def side_rates(near, tiles, steps_ref, waves_ref, base_ref):
+    counts = sweep_counts(steps_ref, lax.axis_index("tile"), tiles)
+    rates = [[coefficient(k, counts[0]), coefficient(k, counts[1 if near else 2])] for k in range(DIFF)]
+    for k in range(DIFF):
+        for side in range(2):
+            base_ref[k, side] = base_of(rates[k][side], waves_ref[...])
+    return rates
+
+
+def near_kernel(
+    levels, tiles,
     bands_ref, steps_ref, halo_ref, mem_ref, cov_ref, s_high_ref, s_low_ref, waves_ref, mine_ref, theirs_ref,
     spec_ref, base_ref, halo_row_ref, pad_ref,
 ):
-    counts = sweep_counts(steps_ref, lax.axis_index("tile"), tiles)
-    owned, tall, width = halo_ref.shape[0], cov_ref.shape[1], cov_ref.shape[2]
-    rate = [[coefficient(k, counts[0]), coefficient(k, counts[1 if near else 2])] for k in range(DIFF)]
-    for k in range(DIFF):
-        for side in range(2):
-            base_ref[k, side] = base_of(rate[k][side], waves_ref[...])
-    if near:
-        vertical = build_vertical(bands_ref, pad_ref, levels)
-        halo_row_ref[levels:, :] = jnp.zeros((halo_row_ref.shape[0] - levels, width), F32)
+    rates = side_rates(True, tiles, steps_ref, waves_ref, base_ref)
+    tall, width = spec_ref.shape[1:]
+    vertical = build_vertical(bands_ref, pad_ref, levels)
+    halo_row_ref[levels:, :] = jnp.zeros((halo_row_ref.shape[0] - levels, width), F32)
     sums = [cov_ref[q] for q in range(DIFF)]
-    for m in range(owned):
-        if near:
-            local = []
-            for q in range(DIFF):
-                halo_row_ref[:levels, :] = strided(halo_ref.at[m], q, levels, DIFF)
-                local.append(apply_vertical(vertical, halo_row_ref[...]))
-            waves = transform(jnp.concatenate(local, axis=0), s_high_ref[...], s_low_ref[...])
-            for q in range(DIFF):
-                spec_ref[q] = waves[q * tall : (q + 1) * tall]
-        for at in range(0, levels, 8):
-            size = min(8, levels - at)
-            if near:
-                field = {q: spec_ref[q, at : at + size, :] for q in range(DIFF)}
-            else:
-                field = {q: strided(halo_ref.at[m], q + DIFF * at, size, DIFF) for q in range(DIFF)}
-            for k in range(DIFF):
-                kept = range(-1 - k, DIFF - 1 - k)
-                bases = {p: base_ref[k, 0 if p < 0 else 1][:size] for p in kept}
-                field = advance(field, {p: rate[k][0 if p < 0 else 1] for p in kept}, bases)
-            for q in range(DIFF):
-                spec_ref[q, at : at + size, :] = field[-1 - q]
-        if levels < tall:
-            for q in range(DIFF):
-                spec_ref[q, levels:, :] = jnp.zeros((tall - levels, width), F32)
+    for m in range(halo_ref.shape[0]):
+        local = []
+        for q in range(DIFF):
+            halo_row_ref[:levels, :] = strided(halo_ref.at[m], q, levels, DIFF)
+            local.append(apply_vertical(vertical, halo_row_ref[...]))
+        waves = transform(jnp.concatenate(local, axis=0), s_high_ref[...], s_low_ref[...])
+        for q in range(DIFF):
+            spec_ref[q] = waves[q * tall : (q + 1) * tall]
+        for at in range(0, tall, 8):
+            field = {q: spec_ref[q, at : at + 8, :] for q in range(DIFF)}
+            for q, value in enumerate(settle(field, rates, base_ref, 8)):
+                spec_ref[q, at : at + 8, :] = value
         block = spec_ref[...].reshape(DIFF * tall, width)
         block = transform(block, s_high_ref[...], s_low_ref[...])
         for q in range(DIFF):
             sums[q] = sums[q] + mem_ref[m, q] * block[q * tall : (q + 1) * tall]
     part = DIFF // 2
-    half = lax.axis_index("mem") % 2
     for q in range(DIFF):
 
-        @pl.when(half == q // part)
+        @pl.when(core() == q // part)
         def _(q=q):
             mine_ref[q % part] = sums[q]
 
-        @pl.when(half != q // part)
+        @pl.when(core() != q // part)
         def _(q=q):
             theirs_ref[q % part] = sums[q]
+
+
+def far_kernel(
+    levels, tiles,
+    steps_ref, halo_ref, mem_ref, mem_other_ref, cov_ref, cov_other_ref, s_high_ref, s_low_ref, waves_ref,
+    out_ref, spec_ref, base_ref,
+):
+    rates = side_rates(False, tiles, steps_ref, waves_ref, base_ref)
+    tall, width = spec_ref.shape[2:]
+    size = half_span(levels)
+    owned = mem_ref.shape[0]
+    for m in range(2 * owned):
+        for q in range(DIFF):
+            spec_ref[m, q, size:, :] = jnp.zeros((tall - size, width), F32)
+        for at in range(0, size, 8):
+            count = min(8, size - at)
+            field = {q: strided(halo_ref.at[m], q + DIFF * at, count, DIFF) for q in range(DIFF)}
+            for q, value in enumerate(settle(field, rates, base_ref, count)):
+                spec_ref[m, q, at : at + count, :] = value
+    block = spec_ref[...].reshape(2 * owned * DIFF * tall, width)
+    spec_ref[...] = transform(block, s_high_ref[...], s_low_ref[...]).reshape(spec_ref.shape)
+    for q in range(DIFF):
+        out_ref[q, size:] = jnp.zeros((tall - size, width), F32)
+        for at in range(0, size, 8):
+            span = slice(at, min(at + 8, size))
+            total = cov_ref[q, span] + cov_other_ref[q, span]
+            for m in range(2 * owned):
+                member_ref = (mem_ref if m < owned else mem_other_ref).at[m % owned]
+                total = total + strided(member_ref, q + DIFF * at, span.stop - at, DIFF) * spec_ref[m, q, span]
+            out_ref[q, span] = total
 
 
 def reduced(value):
@@ -354,19 +403,20 @@
     return [ref[index : index + 1, :] for index in range(5)]
 
 
-def last_kernel(inverse, beta_ref, sums_ref, *refs):
-    mine_refs, other_refs, (inc_ref, prev_ref, w_ref, out_ref) = refs[:2], refs[2:4], refs[4:]
-    own_half = lax.axis_index("mem") % 2
-    part = DIFF // 2
+def last_kernel(inverse, levels, beta_ref, sums_ref, *refs):
+    mine_refs, other_refs, (inc_ref, prev_ref, w_ref, out_ref, cov_ref) = refs[:2], refs[2:4], refs[4:]
     beta = beta_ref[0]
     square0, cross0, mixed0, rest0, pivot0 = [value[:, 0:1] for value in load_sums(sums_ref)]
     zero = jnp.zeros((8, inc_ref.shape[-1]), F32)
     square, cross, mixed, rest = zero, zero, zero, zero
+    size = half_span(levels)
     for q in range(DIFF):
+        mine, other = (first[q, :size] + second[q, :size] for first, second in (mine_refs, other_refs))
+        cov_ref[levels:, :] = jnp.zeros((cov_ref.shape[0] - levels, cov_ref.shape[1]), F32)
+        cov_ref[levels - size : levels, :] = jnp.where(core() == 1, mine, other)
+        cov_ref[:size, :] = jnp.where(core() == 0, mine, other)
         inc = inc_ref[q]
-        which, index = divmod(q, part)
-        mine, other = (refs[0][index] + refs[1][index] for refs in (mine_refs, other_refs))
-        scaled = inverse * jnp.where(own_half == which, mine, other)
+        scaled = inverse * cov_ref[...]
         value = scaled - beta * prev_ref[q]
         w_ref[q] = value
         apart = value - pivot0 * inc
@@ -453,7 +503,8 @@
 
     def target(i):
         value = i // digit % radix
-        return i + ((value + by) % radix - value) * digit
+        other = value ^ by if radix & (radix - 1) == 0 else (value + by) % radix
+        return i + (other - value) * digit
 
     return [(i, target(i)) for i in range(count)]
 
@@ -504,27 +555,34 @@
         ],
         limit=EDGE_LIMIT,
     )
+    mem = members.reshape(owned, levels * rows, width)
+    bands, near_edge = lax.optimization_barrier((bands, near_edge))
     near_halo = lax.ppermute(near_edge, "tile", near_pairs)
-    mem = members.reshape(owned, levels * rows, width)
-    (far_edge,) = call(
+    size = half_span(levels)
+    half_packed = (owned, lanes, DIFF * size, 128)
+    pair = flipped("mem", 1)
+    far_edge, far_edge_other, mem_far, mem_far_other = call(
         functools.partial(edge_kernel, rows, levels),
         [("v", bands), ("v", mem), ("v", inc), ("v", s_high), ("v", s_low)],
-        [packed],
-        [pltpu.VMEM((lanes, deep * rows, 128), F32), pad],
-    )
+        [half_packed] * 4,
+        [pltpu.VMEM((lanes, deep * rows, 128), F32), pad, pltpu.VMEM(packed, F32), pltpu.VMEM(packed, F32)],
+    )
+    far_edge_other = lax.ppermute(far_edge_other, "mem", pair)
+    mem_far_other = lax.ppermute(mem_far_other, "mem", pair)
     members, far_edge = lax.optimization_barrier((members, far_edge))
     mem = members.reshape(owned, levels * rows, width)
 
     piece, four = (part, tall, width), (DIFF, tall, width)
-    mine, theirs, cov_near, cov_far, mem_near, mem_far = call(
+    short = (DIFF, up_to(size, 8), width)
+    mine, theirs, cov_near, cov_far, cov_far_other, mem_near = call(
         functools.partial(own_kernel, rows, levels, tiles),
         [("v", bands), ("s", diffusion_steps), ("v", mem), ("v", inc)]
         + [("v", s_high), ("v", s_low), ("v", waves)],
-        [piece, piece, four, four, edge, edge],
+        [piece, piece, four, short, short, edge],
         [pltpu.VMEM((lanes, deep * rows, 128), F32)] * 2
         + [pltpu.VMEM((rows, tall, width), F32)] * 2
         + [pltpu.VMEM((DIFF, 3, 8, width), F32), pad],
-        (200_000_000, 10_000_000),
+        (20_000_000, 1_000_000),
     )
     prev, _ = lax.optimization_barrier((prev, theirs))
     inc_t, prev_t = call(
@@ -533,7 +591,8 @@
         [(rows, tall, width), (rows, tall, width)],
         [pltpu.VMEM((lanes, tall * rows, 128), F32)],
     )
-    theirs, far_edge, inc_t = lax.optimization_barrier((theirs, far_edge, inc_t))
+    theirs, far_edge_other = lax.optimization_barrier((theirs, far_edge_other))
+    far_edge = jnp.concatenate([far_edge, far_edge_other])
     far_halo = lax.ppermute(far_edge, "tile", far_pairs)
     bits = [1 << k for k in range(1, mems.bit_length() - 1)]
     mine = mine + lax.ppermute(theirs, "mem", flipped("mem", 1))
@@ -541,22 +600,20 @@
         mine = mine + lax.ppermute(mine, "mem", flipped("mem", bit))
     other = lax.ppermute(mine, "mem", flipped("mem", 1))
 
-    def edge_sum(near, halo, mem_rows, cov, outs):
-        return call(
-            functools.partial(halo_kernel, near, levels, tiles),
-            [("v", bands), ("s", diffusion_steps), ("v", halo), ("v", mem_rows), ("v", cov)]
-            + [("v", s_high), ("v", s_low), ("v", waves)],
-            outs,
-            [pltpu.VMEM(four, F32), pltpu.VMEM((DIFF, 2, 8, width), F32), pltpu.VMEM((deep, width), F32), pad],
-        )
-
+    cov_far_other = lax.ppermute(cov_far_other, "mem", pair)
     two = (DIFF // 2, tall, width)
-    near_mine, near_theirs = edge_sum(True, near_halo, mem_near, cov_near, [two, two])
+    near_mine, near_theirs = call(
+        functools.partial(near_kernel, levels, tiles),
+        [("v", bands), ("s", diffusion_steps), ("v", near_halo), ("v", mem_near), ("v", cov_near)]
+        + [("v", s_high), ("v", s_low), ("v", waves)],
+        [two, two],
+        [pltpu.VMEM(four, F32), pltpu.VMEM((DIFF, 2, 8, width), F32), pltpu.VMEM((deep, width), F32), pad],
+    )
     near_mine = near_mine + lax.ppermute(near_theirs, "mem", flipped("mem", 1))
     for bit in bits:
         near_mine = near_mine + lax.ppermute(near_mine, "mem", flipped("mem", bit))
     near_other = lax.ppermute(near_mine, "mem", flipped("mem", 1))
-    cov_far, near_mine, inc_t = lax.optimization_barrier((cov_far, near_mine, inc_t))
+    cov_far, near_other, inc_t = lax.optimization_barrier((cov_far, near_other, inc_t))
     w_rest, sums = call(
         functools.partial(bulk_kernel, rows, levels, inverse),
         [("s", beta_prev), ("v", mine), ("v", other), ("v", near_mine), ("v", near_other)]
@@ -564,17 +621,23 @@
         [(lanes, levels * rows, 128), (8, 128)],
         [pltpu.VMEM((rows - DIFF, tall, width), F32)],
     )
-    far_mine, far_theirs = edge_sum(False, far_halo, mem_far, cov_far, [two, two])
-    far_mine = far_mine + lax.ppermute(far_theirs, "mem", flipped("mem", 1))
+    (cov,) = call(
+        functools.partial(far_kernel, levels, tiles),
+        [("s", diffusion_steps), ("v", far_halo), ("v", mem_far), ("v", mem_far_other)]
+        + [("v", cov_far), ("v", cov_far_other), ("v", s_high), ("v", s_low), ("v", waves)],
+        [short],
+        [pltpu.VMEM((2 * owned, *short), F32), pltpu.VMEM((DIFF, 2, 8, width), F32)],
+    )
     for bit in bits[:-1]:
-        far_mine = far_mine + lax.ppermute(far_mine, "mem", flipped("mem", bit))
-    far_sums = [far_mine, lax.ppermute(far_mine, "mem", flipped("mem", bits[-1]))]
-    far_others = [lax.ppermute(value, "mem", flipped("mem", 1)) for value in far_sums]
+        cov = cov + lax.ppermute(cov, "mem", flipped("mem", bit))
+    far_sums = [cov, lax.ppermute(cov, "mem", flipped("mem", bits[-1]))]
+    far_others = [lax.ppermute(value, "mem", pair) for value in far_sums]
     w_far, sums = call(
-        functools.partial(last_kernel, inverse),
+        functools.partial(last_kernel, inverse, levels),
         [("s", beta_prev), ("v", sums)]
         + [("v", value) for value in far_sums + far_others + [inc_t, prev_t]],
         [four, (8, 128)],
+        [pltpu.VMEM((tall, width), F32)],
     )
     digit = 1
     stages = radices(tiles)

time: 58 us -> 57.6 us (level)
  waiting for transfers between devices: 19.8 us -> 17.4 us
  starting transfers between devices: 16.7 us -> 17.7 us
  Pallas kernels: 19.5 us -> 20.3 us
    ppermute x1, waiting for transfers between devices: 4.21 us -> 1.01 us  [per_device(): mine = mine + lax.ppermute(mine, 'mem', flipped('mem', bit))]
    ppermute x4, waiting for transfers between devices: 3.72 us -> 5.45 us  [per_device(): lax.ppermute(sums, 'tile', rotated('tile', digit, radix, by))]
    pallas_call x10, Pallas kernels: 19.5 us -> 20.3 us  [call(): pl.pallas_call(kernel, out_shape=tuple((jax.ShapeDtypeStruct(shape, F32)...]
    ppermute x4 -> x6, waiting for transfers between devices: 4.02 us -> 3.26 us  [the longest x1 3.25 us: per_device(): far_sums = [cov, lax.ppermute(cov, 'mem', flipped('mem', bits[-1]))]]
    ppermute x4 -> x6, starting transfers between devices: 2.15 us -> 2.63 us  [the longest x1 1.78 us: per_device(): far_sums = [cov, lax.ppermute(cov, 'mem', flipped('mem', bits[-1]))]]
  transfers between devices with their start and end apart: 16 -> 18, of which waited for: 8 -> 8; matrix products, arithmetic and copies ran while one was open for 0% -> 0% of each run, Pallas kernels for 26% -> 27%
where the time goes in v7:
time: 57.6 us; the launch traced here: 57.5 us
  Pallas kernels  20.3 us (35%)
  starting transfers between devices  17.7 us (31%)
  waiting for transfers between devices  17.4 us (30%)
  between operations  1.73 us (3%)
    pallas_call x10, Pallas kernels, call(): pl.pallas_call(kernel, out_shape=tuple((jax.ShapeDtypeStruct(shape, F32)...  20.3 us
    ppermute x4, starting transfers between devices, per_device(): lax.ppermute(sums, 'tile', rotated('tile', digit, radix, by))  8.48 us
    ppermute x4, waiting for transfers between devices, per_device(): lax.ppermute(sums, 'tile', rotated('tile', digit, radix, by))  5.45 us
    ppermute x1, waiting for transfers between devices, per_device(): near_mine = near_mine + lax.ppermute(near_mine, 'mem', flipped('mem', bit))  4.28 us
    ppermute x1, waiting for transfers between devices, per_device(): far_sums = [cov, lax.ppermute(cov, 'mem', flipped('mem', bits[-1]))]  3.25 us
    ppermute x1, starting transfers between devices, per_device(): near_halo = lax.ppermute(near_edge, 'tile', near_pairs)  3.03 us
    ppermute x1, waiting for transfers between devices, per_device(): near_halo = lax.ppermute(near_edge, 'tile', near_pairs)  2.08 us
    ppermute x1, starting transfers between devices, per_device(): far_sums = [cov, lax.ppermute(cov, 'mem', flipped('mem', bits[-1]))]  1.78 us
  transfers between devices with their start and end apart: 18, of which 8 were waited for; matrix products, arithmetic and copies ran while one was open for 0% of the time, Pallas kernels for 27%

profile of v7, /device:TPU:0, one launch (start us, length us, event | category | flops | bytes accessed | tf_op | source)
XLA Modules:
  0.0 57.5 jit_solution(8401368495316941842)
XLA Ops:
  0.7 2.4 %shard_map.104 = f32[2,2,280,128]{3,2,1,0:T(8,128)} custom-call(bf16[2,70,16,256]{3,2,1,0:T(8,128)(2,1)} %members_hbm.1, f32[70,16,256]{2,1,0:T(8,128)} %inc_hbm.1), custom_call_target="tpu_custom_call" | custom-call | tf_op jit(solution)/shard_map/pallas_call | solution.py:485
  3.1 3.0 %collective-permute-start.4 = (f32[2,2,280,128]{3,2,1,0:T(8,128)}, f32[2,2,280,128]{3,2,1,0:T(8,128)S(1)}, u32[]{:S(2)}, u32[]{:S(2)}) collective-permute-start(f32[2,2,280,128]{3,2,1,0:T(8,128)} %shard_map.104), channel_id=1, source_target_pairs={{0,1},{1,0},{2,3},{3,2},{4,5},{5,4},{6,7},{7,6},{8,9},{9,8},{10,11... | collective-permute-start | bytes 1720328 | tf_op jit(solution)/shard_map/ppermute | solution.py:560
  6.2 1.8 %shard_map.105 = (f32[2,2,144,128]{3,2,1,0:T(8,128)S(1)}, f32[2,2,144,128]{3,2,1,0:T(8,128)S(1)}, f32[2,2,144,128]{3,2,1,0:T(8,128)S(1)}, f32[2,2,144,128]{3,2,1,0:T(8,128)S(1)}) custom-call(s32[1,70]{1,0:T(1,128)S(1)} %bitcast.14, bf16[2,1120,256]{2,1,0:T(8,128)(2,1)S(1)} %bitcast.11, f32[1120,256]{1,0:T(8,128)S(1)} %bitcast.7, ...), custom_call_target="tpu_custom_call" | custom-call | tf_op jit(solution)/shard_map/pallas_call | solution.py:485
  8.0 0.1 collective-permute-start
  8.1 7.9 %shard_map.106 = (f32[4,72,256]{2,1,0:T(8,128)S(1)}, f32[4,72,256]{2,1,0:T(8,128)S(1)}, f32[4,72,256]{2,1,0:T(8,128)S(1)}, f32[4,40,256]{2,1,0:T(8,128)S(1)}, f3...) custom-call(s32[1,70]{1,0:T(1,128)S(1)} %bitcast.15, s32[8]{0:T(128)S(1)} %copy-done.6, ...), custom_call_target="tpu_custom_call" | custom-call | flops 20000000 | bytes 1000000 | tf_op jit(solution)/shard_map/pallas_call | solution.py:485
  16.0 0.7 %collective-permute-start.8 = (f32[4,2,144,128]{3,2,1,0:T(8,128)S(1)}, f32[4,2,144,128]{3,2,1,0:T(8,128)S(1)}, u32[]{:S(2)}, u32[]{:S(2)}) collective-permute-start(f32[4,2,144,128]{3,2,1,0:T(8,128)S(1)} %pad_maximum_fusion), channel_id=1, source_target_pairs={{1,2},{2,1},{3,4},{4,3},{5,6},{6,5},{9,10},{10,9},{11,12},{12,11},... | collective-permute-start | bytes 1769480 | tf_op jit(solution)/shard_map/ppermute | solution.py:596
  16.7 0.5 collective-permute-start.1
  17.3 2.1 %collective-permute-done.4.halo_ref = f32[2,2,280,128]{3,2,1,0:T(8,128)S(1)} collective-permute-done((f32[2,2,280,128]{3,2,1,0:T(8,128)}, f32[2,2,280,128]{3,2,1,0:T(8,128)S(1)}, u32[]{:S(2)}, u32[]{:S(2)}) %collective-permute-start.4) | collective-permute-done | bytes 573472 | tf_op jit(solution)/shard_map/ppermute | solution.py:560
  19.4 2.5 %shard_map.107 = (f32[2,72,256]{2,1,0:T(8,128)S(1)}, f32[2,72,256]{2,1,0:T(8,128)S(1)}) custom-call(s32[1,70]{1,0:T(1,128)S(1)} %bitcast.16, s32[8]{0:T(128)S(1)} %copy-done.6, f32[2,2,280,128]{3,2,1,0:T(8,128)S(1)} %collective-permute-done.4.halo_ref, f32[2,4,72,256]{3,2,1,0:T(8,128)S(1)} %get-tuple-element.40.mem_ref, ...), custom_call_target="tpu_custom_call" | custom-call | tf_op jit(solution)/shard_map/pallas_call | solution.py:485
  21.9 0.1 collective-permute-start.5
  22.0 1.4 %collective-permute-done.5 = f32[2,72,256]{2,1,0:T(8,128)S(1)} collective-permute-done((f32[2,72,256]{2,1,0:T(8,128)S(1)}, f32[2,72,256]{2,1,0:T(8,128)S(1)}, u32[]{:S(2)}, u32[]{:S(2)}) %collective-permute-start.5) | collective-permute-done | bytes 147488 | tf_op jit(solution)/shard_map/ppermute | solution.py:612
  23.3 1.8 %collective-permute-start.6 = (f32[2,72,256]{2,1,0:T(8,128)S(1)}, f32[2,72,256]{2,1,0:T(8,128)S(1)}, u32[]{:S(2)}, u32[]{:S(2)}) collective-permute-start(f32[2,72,256]{2,1,0:T(8,128)S(1)} %add.14), channel_id=1, source_target_pairs={{0,16},{8,24},{16,0},{24,8},{1,17},{9,25},{17,1},{25,9},{2,18},{10... | collective-permute-start | bytes 442376 | tf_op jit(solution)/shard_map/ppermute | solution.py:614
  25.2 0.4 collective-permute-start.2
  25.5 0.3 collective-permute-start.10
  25.8 4.3 %collective-permute-done.6 = f32[2,72,256]{2,1,0:T(8,128)S(1)} collective-permute-done((f32[2,72,256]{2,1,0:T(8,128)S(1)}, f32[2,72,256]{2,1,0:T(8,128)S(1)}, u32[]{:S(2)}, u32[]{:S(2)}) %collective-permute-start.6) | collective-permute-done | bytes 147488 | tf_op jit(solution)/shard_map/ppermute | solution.py:614
  30.1 0.1 collective-permute-start.7
  30.2 1.4 %shard_map.108 = (f32[16,72,256]{2,1,0:T(8,128)S(1)}, f32[16,72,256]{2,1,0:T(8,128)S(1)}) custom-call(f32[1120,256]{1,0:T(8,128)S(1)} %bitcast.9, f32[1120,256]{1,0:T(8,128)S(1)} %bitcast.13), custom_call_target="tpu_custom_call" | custom-call | tf_op jit(solution)/shard_map/pallas_call | solution.py:485
  31.6 1.2 %shard_map.110.refs_0_ = f32[4,40,256]{2,1,0:T(8,128)S(1)} custom-call(s32[8]{0:T(128)S(1)} %copy-done.6, f32[4,2,144,128]{3,2,1,0:T(8,128)S(1)} %collective-permute-done.8.halo_ref, f32[2,2,144,128]{3,2,1,0:T(8,128)S(1)} %get-tuple-element.53.mem_ref, f32[2,2,144,128]{3,2,1,0:T(8,128)S(1)} %collective-permute-done.9.mem_other_ref, ...), custom_call_target="tpu_custom_call" | custom-call | tf_op jit(solution)/shard_map/pallas_call | solution.py:485
  32.8 1.8 %collective-permute-start.11 = (f32[4,40,256]{2,1,0:T(8,128)S(1)}, f32[4,40,256]{2,1,0:T(8,128)S(1)}, u32[]{:S(2)}, u32[]{:S(2)}) collective-permute-start(f32[4,40,256]{2,1,0:T(8,128)S(1)} %shard_map.110.refs_0_), channel_id=1, source_target_pairs={{0,16},{8,24},{16,0},{24,8},{1,17},{9,25},{17,1},{25,9},{2,18},{10... | collective-permute-start | bytes 491528 | tf_op jit(solution)/shard_map/ppermute | solution.py:633
  34.6 1.0 %collective-permute-done.2 = f32[4,72,256]{2,1,0:T(8,128)S(1)} collective-permute-done((f32[4,72,256]{2,1,0:T(8,128)S(1)}, f32[4,72,256]{2,1,0:T(8,128)S(1)}, u32[]{:S(2)}, u32[]{:S(2)}) %collective-permute-start.2) | collective-permute-done | bytes 294944 | tf_op jit(solution)/shard_map/ppermute | solution.py:600
  35.7 0.1 collective-permute-start.3
  35.7 0.5 collective-permute-start.12
  36.2 3.2 %collective-permute-done.11.refs_1_ = f32[4,40,256]{2,1,0:T(8,128)S(1)} collective-permute-done((f32[4,40,256]{2,1,0:T(8,128)S(1)}, f32[4,40,256]{2,1,0:T(8,128)S(1)}, u32[]{:S(2)}, u32[]{:S(2)}) %collective-permute-start.11) | collective-permute-done | bytes 163872 | tf_op jit(solution)/shard_map/ppermute | solution.py:633
  40.2 1.1 %shard_map.109 = (f32[2,1120,128]{2,1,0:T(8,128)S(1)}, f32[8,128]{1,0:T(8,128)S(1)}) custom-call(f32[1]{0:T(128)S(6)} %copy.11.beta_ref, f32[4,72,256]{2,1,0:T(8,128)S(1)} %add.13.mine_ref, f32[4,72,256]{2,1,0:T(8,128)S(1)} %collective-permute-done.3.other_ref, f32[2,72,256]{2,1,0:T(8,128)S(1)} %add.15.near_mine_ref, ...), custom_call_target="tpu_custom_call" | custom-call | tf_op jit(solution)/shard_map/pallas_call | solution.py:485
  41.3 0.4 shard_map.111
  41.6 2.7 %collective-permute-start.14 = (f32[8,128]{1,0:T(8,128)S(1)}, f32[8,128]{1,0:T(8,128)S(1)}, u32[]{:S(2)}, u32[]{:S(2)}) collective-permute-start(f32[8,128]{1,0:T(8,128)S(1)} %get-tuple-element.57.refs_0_), channel_id=1, source_target_pairs={{0,1},{1,0},{2,3},{3,2},{4,5},{5,4},{6,7},{7,6},{8,9},{9,8},{10,11... | collective-permute-start | bytes 12296 | tf_op jit(solution)/shard_map/ppermute | solution.py:645
  44.4 1.6 %collective-permute-done.14.refs_1_ = f32[8,128]{1,0:T(8,128)S(1)} collective-permute-done((f32[8,128]{1,0:T(8,128)S(1)}, f32[8,128]{1,0:T(8,128)S(1)}, u32[]{:S(2)}, u32[]{:S(2)}) %collective-permute-start.14) | collective-permute-done | bytes 4128 | tf_op jit(solution)/shard_map/ppermute | solution.py:645
  46.0 5.1 %collective-permute-start.17 = (f32[8,128]{1,0:T(8,128)S(1)}, f32[8,128]{1,0:T(8,128)S(1)}, u32[]{:S(2)}, u32[]{:S(2)}) collective-permute-start(f32[8,128]{1,0:T(8,128)S(1)} %shard_map.112.refs_0_), channel_id=1, source_target_pairs={{0,6},{1,7},{2,4},{3,5},{4,2},{5,3},{6,0},{7,1},{8,14},{9,15},{10,... | collective-permute-start | bytes 12296 | tf_op jit(solution)/shard_map/ppermute | solution.py:645
  51.1 0.6 %collective-permute-start.15 = (f32[8,128]{1,0:T(8,128)S(1)}, f32[8,128]{1,0:T(8,128)S(1)}, u32[]{:S(2)}, u32[]{:S(2)}) collective-permute-start(f32[8,128]{1,0:T(8,128)S(1)} %shard_map.112.refs_0_), channel_id=1, source_target_pairs={{0,2},{1,3},{2,0},{3,1},{4,6},{5,7},{6,4},{7,5},{8,10},{9,11},{10,... | collective-permute-start | bytes 12296 | tf_op jit(solution)/shard_map/ppermute | solution.py:645
  51.7 1.0 %collective-permute-done.17.refs_3_ = f32[8,128]{1,0:T(8,128)S(1)} collective-permute-done((f32[8,128]{1,0:T(8,128)S(1)}, f32[8,128]{1,0:T(8,128)S(1)}, u32[]{:S(2)}, u32[]{:S(2)}) %collective-permute-start.17) | collective-permute-done | bytes 4128 | tf_op jit(solution)/shard_map/ppermute | solution.py:645
  52.7 2.9 %collective-permute-done.16.refs_2_ = f32[8,128]{1,0:T(8,128)S(1)} collective-permute-done((f32[8,128]{1,0:T(8,128)S(1)}, f32[8,128]{1,0:T(8,128)S(1)}, u32[]{:S(2)}, u32[]{:S(2)}) %collective-permute-start.16) | collective-permute-done | bytes 4128 | tf_op jit(solution)/shard_map/ppermute | solution.py:645
  55.6 1.7 %shard_map.113 = (f32[1120,256]{1,0:T(8,128)}, f32[1,2]{1,0:T(1,128)}) custom-call(f32[8,128]{1,0:T(8,128)S(1)} %shard_map.112.refs_0_, f32[8,128]{1,0:T(8,128)S(1)} %collective-permute-done.15.refs_1_, f32[8,128]{1,0:T(8,128)S(1)} %collective-permute-done.16.refs_2_, f32[8,128]{1,0:T(8,128)S(1)} %collective-permute-done.17.refs_3_, ...), custom_call_target="tpu_custom_call" | custom-call | tf_op jit(solution)/shard_map/pallas_call | solution.py:485
  (35 shorter events, 0.3 us)
Async XLA Ops:
  0.6 5.5 %copy-start.2 = (bf16[256,256]{1,0:T(8,128)(2,1)S(1)}, bf16[256,256]{1,0:T(8,128)(2,1)}, u32[]{:S(2)}) copy-start(bf16[256,256]{1,0:T(8,128)(2,1)} %constant.7.clone.s_low_ref) | copy-start | bytes 393220
  0.6 5.5 %copy-start.3 = (bf16[256,256]{1,0:T(8,128)(2,1)S(1)}, bf16[256,256]{1,0:T(8,128)(2,1)}, u32[]{:S(2)}) copy-start(bf16[256,256]{1,0:T(8,128)(2,1)} %constant.6.clone.s_high_ref) | copy-start | bytes 393220
  0.7 5.5 %copy-start.1 = (bf16[2,70,16,256]{3,2,1,0:T(8,128)(2,1)S(1)}, bf16[2,70,16,256]{3,2,1,0:T(8,128)(2,1)}, u32[]{:S(2)}) copy-start(bf16[2,70,16,256]{3,2,1,0:T(8,128)(2,1)} %members_hbm.1) | copy-start | bytes 3440644
  0.7 5.5 %copy-start = (f32[70,16,256]{2,1,0:T(8,128)S(1)}, f32[70,16,256]{2,1,0:T(8,128)}, u32[]{:S(2)}) copy-start(f32[70,16,256]{2,1,0:T(8,128)} %inc_hbm.1) | copy-start | bytes 3440644
  0.7 5.5 %copy-start.7 = (s32[70]{0:T(128)S(1)}, s32[70]{0:T(128)}, u32[]{:S(2)}) copy-start(s32[70]{0:T(128)} %param.13) | copy-start | bytes 844
  3.1 16.2 %collective-permute-start.4 = (f32[2,2,280,128]{3,2,1,0:T(8,128)}, f32[2,2,280,128]{3,2,1,0:T(8,128)S(1)}, u32[]{:S(2)}, u32[]{:S(2)}) collective-permute-start(f32[2,2,280,128]{3,2,1,0:T(8,128)} %shard_map.104), channel_id=1, source_target_pairs={{0,1},{1,0},{2,3},{3,2},{4,5},{5,4},{6,7},{7,6},{8,9},{9,8},{10,11... | collective-permute-start | bytes 1720328 | tf_op jit(solution)/shard_map/ppermute | solution.py:560
  6.2 1.9 %copy-start.5 = (f32[8,256]{1,0:T(8,128)S(1)}, f32[8,256]{1,0:T(8,128)}, u32[]{:S(2)}) copy-start(f32[8,256]{1,0:T(8,128)} %constant.8.clone.waves_ref) | copy-start | bytes 24580
  6.2 1.9 %copy-start.6 = (s32[8]{0:T(128)S(1)}, s32[8]{0:T(128)}, u32[]{:S(2)}) copy-start(s32[8]{0:T(128)} %steps_ref.5) | copy-start | bytes 100
  8.0 8.0 %collective-permute-start = (f32[2,2,144,128]{3,2,1,0:T(8,128)S(1)}, f32[2,2,144,128]{3,2,1,0:T(8,128)S(1)}, u32[]{:S(2)}, u32[]{:S(2)}) collective-permute-start(f32[2,2,144,128]{3,2,1,0:T(8,128)S(1)} %get-tuple-element.37), channel_id=1, source_target_pairs={{0,8},{8,0},{16,24},{24,16},{1,9},{9,1},{17,25},{25,17},{2,10},{10... | collective-permute-start | bytes 884744 | tf_op jit(solution)/shard_map/ppermute | solution.py:570
  16.0 15.6 %collective-permute-start.8 = (f32[4,2,144,128]{3,2,1,0:T(8,128)S(1)}, f32[4,2,144,128]{3,2,1,0:T(8,128)S(1)}, u32[]{:S(2)}, u32[]{:S(2)}) collective-permute-start(f32[4,2,144,128]{3,2,1,0:T(8,128)S(1)} %pad_maximum_fusion), channel_id=1, source_target_pairs={{1,2},{2,1},{3,4},{4,3},{5,6},{6,5},{9,10},{10,9},{11,12},{12,11},... | collective-permute-start | bytes 1769480 | tf_op jit(solution)/shard_map/ppermute | solution.py:596
  16.7 8.4 %collective-permute-start.1 = (f32[4,72,256]{2,1,0:T(8,128)S(1)}, f32[4,72,256]{2,1,0:T(8,128)S(1)}, u32[]{:S(2)}, u32[]{:S(2)}) collective-permute-start(f32[4,72,256]{2,1,0:T(8,128)S(1)} %get-tuple-element.38), channel_id=1, source_target_pairs={{0,8},{8,0},{16,24},{24,16},{1,9},{9,1},{17,25},{25,17},{2,10},{10... | collective-permute-start | bytes 884744 | tf_op jit(solution)/shard_map/ppermute | solution.py:598
  21.9 8.3 %copy-start.4 = (f32[70,16,256]{2,1,0:T(8,128)S(1)}, f32[70,16,256]{2,1,0:T(8,128)}, u32[]{:S(2)}) copy-start(f32[70,16,256]{2,1,0:T(8,128)} %param.10) | copy-start | bytes 3440644
  21.9 1.4 %collective-permute-start.5 = (f32[2,72,256]{2,1,0:T(8,128)S(1)}, f32[2,72,256]{2,1,0:T(8,128)S(1)}, u32[]{:S(2)}, u32[]{:S(2)}) collective-permute-start(f32[2,72,256]{2,1,0:T(8,128)S(1)} %get-tuple-element.43), channel_id=1, source_target_pairs={{0,8},{8,0},{16,24},{24,16},{1,9},{9,1},{17,25},{25,17},{2,10},{10... | collective-permute-start | bytes 442376 | tf_op jit(solution)/shard_map/ppermute | solution.py:612
  23.3 6.8 %collective-permute-start.6 = (f32[2,72,256]{2,1,0:T(8,128)S(1)}, f32[2,72,256]{2,1,0:T(8,128)S(1)}, u32[]{:S(2)}, u32[]{:S(2)}) collective-permute-start(f32[2,72,256]{2,1,0:T(8,128)S(1)} %add.14), channel_id=1, source_target_pairs={{0,16},{8,24},{16,0},{24,8},{1,17},{9,25},{17,1},{25,9},{2,18},{10... | collective-permute-start | bytes 442376 | tf_op jit(solution)/shard_map/ppermute | solution.py:614
  25.1 6.5 %collective-permute-start.9 = (f32[2,2,144,128]{3,2,1,0:T(8,128)S(1)}, f32[2,2,144,128]{3,2,1,0:T(8,128)S(1)}, u32[]{:S(2)}, u32[]{:S(2)}) collective-permute-start(f32[2,2,144,128]{3,2,1,0:T(8,128)S(1)} %get-tuple-element.54), channel_id=1, source_target_pairs={{0,8},{8,0},{16,24},{24,16},{1,9},{9,1},{17,25},{25,17},{2,10},{10... | collective-permute-start | bytes 884744 | tf_op jit(solution)/shard_map/ppermute | solution.py:571
  25.2 10.5 %collective-permute-start.2 = (f32[4,72,256]{2,1,0:T(8,128)S(1)}, f32[4,72,256]{2,1,0:T(8,128)S(1)}, u32[]{:S(2)}, u32[]{:S(2)}) collective-permute-start(f32[4,72,256]{2,1,0:T(8,128)S(1)} %add.12), channel_id=1, source_target_pairs={{0,16},{8,24},{16,0},{24,8},{1,17},{9,25},{17,1},{25,9},{2,18},{10... | collective-permute-start | bytes 884744 | tf_op jit(solution)/shard_map/ppermute | solution.py:600
  25.5 6.1 %collective-permute-start.10 = (f32[4,40,256]{2,1,0:T(8,128)S(1)}, f32[4,40,256]{2,1,0:T(8,128)S(1)}, u32[]{:S(2)}, u32[]{:S(2)}) collective-permute-start(f32[4,40,256]{2,1,0:T(8,128)S(1)} %get-tuple-element.56), channel_id=1, source_target_pairs={{0,8},{8,0},{16,24},{24,16},{1,9},{9,1},{17,25},{25,17},{2,10},{10... | collective-permute-start | bytes 491528 | tf_op jit(solution)/shard_map/ppermute | solution.py:603
  30.1 1.5 %collective-permute-start.7 = (f32[2,72,256]{2,1,0:T(8,128)S(1)}, f32[2,72,256]{2,1,0:T(8,128)S(1)}, u32[]{:S(2)}, u32[]{:S(2)}) collective-permute-start(f32[2,72,256]{2,1,0:T(8,128)S(1)} %add.15.near_mine_ref), channel_id=1, source_target_pairs={{0,8},{8,0},{16,24},{24,16},{1,9},{9,1},{17,25},{25,17},{2,10},{10... | collective-permute-start | bytes 442376 | tf_op jit(solution)/shard_map/ppermute | solution.py:615
  32.8 6.7 %collective-permute-start.11 = (f32[4,40,256]{2,1,0:T(8,128)S(1)}, f32[4,40,256]{2,1,0:T(8,128)S(1)}, u32[]{:S(2)}, u32[]{:S(2)}) collective-permute-start(f32[4,40,256]{2,1,0:T(8,128)S(1)} %shard_map.110.refs_0_), channel_id=1, source_target_pairs={{0,16},{8,24},{16,0},{24,8},{1,17},{9,25},{17,1},{25,9},{2,18},{10... | collective-permute-start | bytes 491528 | tf_op jit(solution)/shard_map/ppermute | solution.py:633
  35.7 4.5 %collective-permute-start.3 = (f32[4,72,256]{2,1,0:T(8,128)S(1)}, f32[4,72,256]{2,1,0:T(8,128)S(1)}, u32[]{:S(2)}, u32[]{:S(2)}) collective-permute-start(f32[4,72,256]{2,1,0:T(8,128)S(1)} %add.13.mine_ref), channel_id=1, source_target_pairs={{0,8},{8,0},{16,24},{24,16},{1,9},{9,1},{17,25},{25,17},{2,10},{10... | collective-permute-start | bytes 884744 | tf_op jit(solution)/shard_map/ppermute | solution.py:601
  35.7 5.5 %collective-permute-start.12 = (f32[4,40,256]{2,1,0:T(8,128)S(1)}, f32[4,40,256]{2,1,0:T(8,128)S(1)}, u32[]{:S(2)}, u32[]{:S(2)}) collective-permute-start(f32[4,40,256]{2,1,0:T(8,128)S(1)} %shard_map.110.refs_0_), channel_id=1, source_target_pairs={{0,8},{8,0},{16,24},{24,16},{1,9},{9,1},{17,25},{25,17},{2,10},{10... | collective-permute-start | bytes 491528 | tf_op jit(solution)/shard_map/ppermute | solution.py:634
  39.5 1.8 %collective-permute-start.13 = (f32[4,40,256]{2,1,0:T(8,128)S(1)}, f32[4,40,256]{2,1,0:T(8,128)S(1)}, u32[]{:S(2)}, u32[]{:S(2)}) collective-permute-start(f32[4,40,256]{2,1,0:T(8,128)S(1)} %collective-permute-done.11.refs_1_), channel_id=1, source_target_pairs={{0,8},{8,0},{16,24},{24,16},{1,9},{9,1},{17,25},{25,17},{2,10},{10... | collective-permute-start | bytes 491528 | tf_op jit(solution)/shard_map/ppermute | solution.py:634
  41.6 4.3 %collective-permute-start.14 = (f32[8,128]{1,0:T(8,128)S(1)}, f32[8,128]{1,0:T(8,128)S(1)}, u32[]{:S(2)}, u32[]{:S(2)}) collective-permute-start(f32[8,128]{1,0:T(8,128)S(1)} %get-tuple-element.57.refs_0_), channel_id=1, source_target_pairs={{0,1},{1,0},{2,3},{3,2},{4,5},{5,4},{6,7},{7,6},{8,9},{9,8},{10,11... | collective-permute-start | bytes 12296 | tf_op jit(solution)/shard_map/ppermute | solution.py:645
  46.0 6.7 %collective-permute-start.17 = (f32[8,128]{1,0:T(8,128)S(1)}, f32[8,128]{1,0:T(8,128)S(1)}, u32[]{:S(2)}, u32[]{:S(2)}) collective-permute-start(f32[8,128]{1,0:T(8,128)S(1)} %shard_map.112.refs_0_), channel_id=1, source_target_pairs={{0,6},{1,7},{2,4},{3,5},{4,2},{5,3},{6,0},{7,1},{8,14},{9,15},{10,... | collective-permute-start | bytes 12296 | tf_op jit(solution)/shard_map/ppermute | solution.py:645
  51.1 4.5 %collective-permute-start.16 = (f32[8,128]{1,0:T(8,128)S(1)}, f32[8,128]{1,0:T(8,128)S(1)}, u32[]{:S(2)}, u32[]{:S(2)}) collective-permute-start(f32[8,128]{1,0:T(8,128)S(1)} %shard_map.112.refs_0_), channel_id=1, source_target_pairs={{0,4},{1,5},{2,6},{3,7},{4,0},{5,1},{6,2},{7,3},{8,12},{9,13},{10,... | collective-permute-start | bytes 12296 | tf_op jit(solution)/shard_map/ppermute | solution.py:645
  51.1 4.5 %collective-permute-start.15 = (f32[8,128]{1,0:T(8,128)S(1)}, f32[8,128]{1,0:T(8,128)S(1)}, u32[]{:S(2)}, u32[]{:S(2)}) collective-permute-start(f32[8,128]{1,0:T(8,128)S(1)} %shard_map.112.refs_0_), channel_id=1, source_target_pairs={{0,2},{1,3},{2,0},{3,1},{4,6},{5,7},{6,4},{7,5},{8,10},{9,11},{10,... | collective-permute-start | bytes 12296 | tf_op jit(solution)/shard_map/ppermute | solution.py:645

commit v8 on v7

--- a/solution.py
+++ b/solution.py
@@ -143,10 +143,17 @@
     return lax.axis_index("mem") % 2
 
 
+def put_parts(ref, own_ref, other_ref, levels):
+    size = half_span(levels)
+    for part, target in ((core(), own_ref), (1 - core(), other_ref)):
+        low = pl.multiple_of(part * (levels - size) * DIFF, 8)
+        target[...] = ref[:, :, pl.ds(low, size * DIFF), :]
+
+
 def edge_kernel(
     rows, levels,
     bands_ref, members_ref, inc_ref, s_high_ref, s_low_ref,
-    far_own_ref, far_other_ref, mem_own_ref, mem_other_ref, prod_ref, pad_ref, wave_ref, pack_ref,
+    far_own_ref, far_other_ref, prod_ref, pad_ref, wave_ref,
 ):
     tile = lax.axis_index("tile")
     deep, tall = up_to(levels, 16), up_to(levels, 8)
@@ -155,27 +162,28 @@
     for piece in range(prod_ref.shape[0]):
         prod_ref[piece, total:, :] = jnp.zeros((prod_ref.shape[1] - total, 128), F32)
     for m in range(members_ref.shape[0]):
-        member = members_ref[m].astype(F32)
-        put_flat(prod_ref, member * inc_ref[...])
+        put_flat(prod_ref, members_ref[m].astype(F32) * inc_ref[...])
         local = [
             apply_vertical(vertical, strided(prod_ref, grid_row(tile, q, rows), deep, rows)) for q in range(DIFF)
         ]
         waves = transform(jnp.concatenate(local, axis=0), s_high_ref[...], s_low_ref[...])
-        put_flat(prod_ref, member)
         for q in range(DIFF):
             put_row(wave_ref.at[m], q, DIFF, waves[q * tall : q * tall + levels])
-            put_row(pack_ref.at[m], q, DIFF, strided(prod_ref, grid_row(tile, q, rows), levels, rows))
-    size = half_span(levels)
-    for pack, own_ref, other_ref in ((wave_ref, far_own_ref, far_other_ref), (pack_ref, mem_own_ref, mem_other_ref)):
-        for part, ref in ((core(), own_ref), (1 - core(), other_ref)):
-            low = pl.multiple_of(part * (levels - size) * DIFF, 8)
-            ref[...] = pack[:, :, pl.ds(low, size * DIFF), :]
-
-
-def turn_kernel(rows, levels, inc_ref, prev_ref, inc_t_ref, prev_t_ref, flat_ref):
+    put_parts(wave_ref, far_own_ref, far_other_ref, levels)
+
+
+def turn_kernel(
+    rows, levels,
+    inc_ref, prev_ref, members_ref, inc_t_ref, prev_t_ref, mem_own_ref, mem_other_ref, flat_ref, pack_ref,
+):
     tile = lax.axis_index("tile")
     for piece in range(flat_ref.shape[0]):
         flat_ref[piece, rows * levels :, :] = jnp.zeros((flat_ref.shape[1] - rows * levels, 128), F32)
+    for m in range(members_ref.shape[0]):
+        put_flat(flat_ref, members_ref[m].astype(F32))
+        for q in range(DIFF):
+            put_row(pack_ref.at[m], q, DIFF, strided(flat_ref, grid_row(tile, q, rows), levels, rows))
+    put_parts(pack_ref, mem_own_ref, mem_other_ref, levels)
     for source, target in ((inc_ref, inc_t_ref), (prev_ref, prev_t_ref)):
         put_flat(flat_ref, source[...])
         for row in range(rows):
@@ -509,6 +517,10 @@
     return [(i, target(i)) for i in range(count)]
 
 
+def partners(radix):
+    return [2, 3, 1] if radix == 4 else range(radix - 1, 0, -1)
+
+
 def radices(count):
     out = [] if count % 2 else [2]
     rest = count // 2 if out else count
@@ -561,14 +573,13 @@
     size = half_span(levels)
     half_packed = (owned, lanes, DIFF * size, 128)
     pair = flipped("mem", 1)
-    far_edge, far_edge_other, mem_far, mem_far_other = call(
+    far_edge, far_edge_other = call(
         functools.partial(edge_kernel, rows, levels),
         [("v", bands), ("v", mem), ("v", inc), ("v", s_high), ("v", s_low)],
-        [half_packed] * 4,
-        [pltpu.VMEM((lanes, deep * rows, 128), F32), pad, pltpu.VMEM(packed, F32), pltpu.VMEM(packed, F32)],
+        [half_packed] * 2,
+        [pltpu.VMEM((lanes, deep * rows, 128), F32), pad, pltpu.VMEM(packed, F32)],
     )
     far_edge_other = lax.ppermute(far_edge_other, "mem", pair)
-    mem_far_other = lax.ppermute(mem_far_other, "mem", pair)
     members, far_edge = lax.optimization_barrier((members, far_edge))
     mem = members.reshape(owned, levels * rows, width)
 
@@ -585,12 +596,13 @@
         (20_000_000, 1_000_000),
     )
     prev, _ = lax.optimization_barrier((prev, theirs))
-    inc_t, prev_t = call(
+    inc_t, prev_t, mem_far, mem_far_other = call(
         functools.partial(turn_kernel, rows, levels),
-        [("v", inc), ("v", prev)],
-        [(rows, tall, width), (rows, tall, width)],
-        [pltpu.VMEM((lanes, tall * rows, 128), F32)],
-    )
+        [("v", inc), ("v", prev), ("v", mem)],
+        [(rows, tall, width)] * 2 + [half_packed] * 2,
+        [pltpu.VMEM((lanes, tall * rows, 128), F32), pltpu.VMEM(packed, F32)],
+    )
+    mem_far_other = lax.ppermute(mem_far_other, "mem", pair)
     theirs, far_edge_other = lax.optimization_barrier((theirs, far_edge_other))
     far_edge = jnp.concatenate([far_edge, far_edge_other])
     far_halo = lax.ppermute(far_edge, "tile", far_pairs)
@@ -642,7 +654,7 @@
     digit = 1
     stages = radices(tiles)
     for index, radix in enumerate(stages):
-        parts = [sums] + [lax.ppermute(sums, "tile", rotated("tile", digit, radix, by)) for by in range(1, radix)]
+        parts = [sums] + [lax.ppermute(sums, "tile", rotated("tile", digit, radix, by)) for by in partners(radix)]
         if index < len(stages) - 1:
             (sums,) = call(merge_kernel, [("v", value) for value in parts], [(8, 128)])
         digit *= radix

time: 57.6 us -> 57.1 us (level)
  starting transfers between devices: 17.7 us -> 16.9 us
    ppermute x1, waiting for transfers between devices: 4.28 us -> 1.55 us  [per_device(): near_mine = near_mine + lax.ppermute(near_mine, 'mem', flipped('mem', bit))]
    ppermute x1, waiting for transfers between devices: 1.01 us -> 2.87 us  [per_device(): mine = mine + lax.ppermute(mine, 'mem', flipped('mem', bit))]
    ppermute x4, starting transfers between devices: 8.48 us -> 7.08 us  [per_device(): lax.ppermute(sums, 'tile', rotated('tile', digit, radix, by))]
    ppermute x1, waiting for transfers between devices: 0.01 us -> 1.36 us  [per_device(): near_other = lax.ppermute(near_mine, 'mem', flipped('mem', 1))]
    ppermute x1, waiting for transfers between devices: 3.25 us -> 2.48 us  [per_device(): far_sums = [cov, lax.ppermute(cov, 'mem', flipped('mem', bits[-1]))]]
  transfers between devices with their start and end apart: 18 -> 18, of which waited for: 8 -> 8; matrix products, arithmetic and copies ran while one was open for 0% -> 0% of each run, Pallas kernels for 27% -> 28%
where the time goes in v8:
time: 57.1 us; the launch traced here: 57 us
  Pallas kernels  20.3 us (36%)
  waiting for transfers between devices  17.9 us (31%)
  starting transfers between devices  16.9 us (30%)
  between operations  1.72 us (3%)
    pallas_call x10, Pallas kernels, call(): pl.pallas_call(kernel, out_shape=tuple((jax.ShapeDtypeStruct(shape, F32)...  20.3 us
    ppermute x4, starting transfers between devices, per_device(): lax.ppermute(sums, 'tile', rotated('tile', digit, radix, by))  7.08 us
    ppermute x4, waiting for transfers between devices, per_device(): lax.ppermute(sums, 'tile', rotated('tile', digit, radix, by))  5.74 us
    ppermute x1, starting transfers between devices, per_device(): near_halo = lax.ppermute(near_edge, 'tile', near_pairs)  3.03 us
    ppermute x1, waiting for transfers between devices, per_device(): mine = mine + lax.ppermute(mine, 'mem', flipped('mem', bit))  2.87 us
    ppermute x1, waiting for transfers between devices, per_device(): near_halo = lax.ppermute(near_edge, 'tile', near_pairs)  2.49 us
    ppermute x1, waiting for transfers between devices, per_device(): far_sums = [cov, lax.ppermute(cov, 'mem', flipped('mem', bits[-1]))]  2.48 us
    ppermute x1, starting transfers between devices, per_device(): far_sums = [cov, lax.ppermute(cov, 'mem', flipped('mem', bits[-1]))]  2.15 us
  transfers between devices with their start and end apart: 18, of which 8 were waited for; matrix products, arithmetic and copies ran while one was open for 0% of the time, Pallas kernels for 28%

profile of v8, /device:TPU:0, one launch (start us, length us, event | category | flops | bytes accessed | tf_op | source)
XLA Modules:
  0.0 57.0 jit_solution(14113975703117395960)
XLA Ops:
  0.7 2.4 %shard_map.104 = f32[2,2,280,128]{3,2,1,0:T(8,128)} custom-call(bf16[2,70,16,256]{3,2,1,0:T(8,128)(2,1)} %members_hbm.1, f32[70,16,256]{2,1,0:T(8,128)} %inc_hbm.1), custom_call_target="tpu_custom_call" | custom-call | tf_op jit(solution)/shard_map/pallas_call | solution.py:493
  3.1 3.0 %collective-permute-start.4 = (f32[2,2,280,128]{3,2,1,0:T(8,128)}, f32[2,2,280,128]{3,2,1,0:T(8,128)S(1)}, u32[]{:S(2)}, u32[]{:S(2)}) collective-permute-start(f32[2,2,280,128]{3,2,1,0:T(8,128)} %shard_map.104), channel_id=1, source_target_pairs={{0,1},{1,0},{2,3},{3,2},{4,5},{5,4},{6,7},{7,6},{8,9},{9,8},{10,11... | collective-permute-start | bytes 1720328 | tf_op jit(solution)/shard_map/ppermute | solution.py:572
  6.2 1.2 %shard_map.105 = (f32[2,2,144,128]{3,2,1,0:T(8,128)S(1)}, f32[2,2,144,128]{3,2,1,0:T(8,128)S(1)}) custom-call(s32[1,70]{1,0:T(1,128)S(1)} %bitcast.15, bf16[2,1120,256]{2,1,0:T(8,128)(2,1)S(1)} %bitcast.11, f32[1120,256]{1,0:T(8,128)S(1)} %bitcast.7, bf16[256,256]{1,0:T(8,128)(2,1)S(1)} %copy-done.2, bf16[256,256]{1,0:T(8,128)(2,1)S(1)} %copy-done.3), custom_call_target="tpu_custom_call" | custom-call | tf_op jit(solution)/shard_map/pallas_call | solution.py:493
  7.5 7.9 %shard_map.106 = (f32[4,72,256]{2,1,0:T(8,128)S(1)}, f32[4,72,256]{2,1,0:T(8,128)S(1)}, f32[4,72,256]{2,1,0:T(8,128)S(1)}, f32[4,40,256]{2,1,0:T(8,128)S(1)}, f3...) custom-call(s32[1,70]{1,0:T(1,128)S(1)} %bitcast.16, s32[8]{0:T(128)S(1)} %copy-done.6, ...), custom_call_target="tpu_custom_call" | custom-call | flops 20000000 | bytes 1000000 | tf_op jit(solution)/shard_map/pallas_call | solution.py:493
  15.5 0.8 %collective-permute-start.8 = (f32[4,2,144,128]{3,2,1,0:T(8,128)S(1)}, f32[4,2,144,128]{3,2,1,0:T(8,128)S(1)}, u32[]{:S(2)}, u32[]{:S(2)}) collective-permute-start(f32[4,2,144,128]{3,2,1,0:T(8,128)S(1)} %pad_maximum_fusion), channel_id=1, source_target_pairs={{1,2},{2,1},{3,4},{4,3},{5,6},{6,5},{9,10},{10,9},{11,12},{12,11},... | collective-permute-start | bytes 1769480 | tf_op jit(solution)/shard_map/ppermute | solution.py:608
  16.3 0.5 collective-permute-start.1
  16.9 2.5 %collective-permute-done.4.halo_ref = f32[2,2,280,128]{3,2,1,0:T(8,128)S(1)} collective-permute-done((f32[2,2,280,128]{3,2,1,0:T(8,128)}, f32[2,2,280,128]{3,2,1,0:T(8,128)S(1)}, u32[]{:S(2)}, u32[]{:S(2)}) %collective-permute-start.4) | collective-permute-done | bytes 573472 | tf_op jit(solution)/shard_map/ppermute | solution.py:572
  19.4 2.5 %shard_map.107 = (f32[2,72,256]{2,1,0:T(8,128)S(1)}, f32[2,72,256]{2,1,0:T(8,128)S(1)}) custom-call(s32[1,70]{1,0:T(1,128)S(1)} %bitcast.17, s32[8]{0:T(128)S(1)} %copy-done.6, f32[2,2,280,128]{3,2,1,0:T(8,128)S(1)} %collective-permute-done.4.halo_ref, f32[2,4,72,256]{3,2,1,0:T(8,128)S(1)} %get-tuple-element.40.mem_ref, ...), custom_call_target="tpu_custom_call" | custom-call | tf_op jit(solution)/shard_map/pallas_call | solution.py:493
  21.9 0.1 collective-permute-start.5
  21.9 1.4 %collective-permute-done.5 = f32[2,72,256]{2,1,0:T(8,128)S(1)} collective-permute-done((f32[2,72,256]{2,1,0:T(8,128)S(1)}, f32[2,72,256]{2,1,0:T(8,128)S(1)}, u32[]{:S(2)}, u32[]{:S(2)}) %collective-permute-start.5) | collective-permute-done | bytes 147488 | tf_op jit(solution)/shard_map/ppermute | solution.py:624
  23.3 1.8 %collective-permute-start.6 = (f32[2,72,256]{2,1,0:T(8,128)S(1)}, f32[2,72,256]{2,1,0:T(8,128)S(1)}, u32[]{:S(2)}, u32[]{:S(2)}) collective-permute-start(f32[2,72,256]{2,1,0:T(8,128)S(1)} %add.14), channel_id=1, source_target_pairs={{0,16},{8,24},{16,0},{24,8},{1,17},{9,25},{17,1},{25,9},{2,18},{10... | collective-permute-start | bytes 442376 | tf_op jit(solution)/shard_map/ppermute | solution.py:626
  25.1 1.9 %shard_map.108 = (f32[16,72,256]{2,1,0:T(8,128)S(1)}, f32[16,72,256]{2,1,0:T(8,128)S(1)}, f32[2,2,144,128]{3,2,1,0:T(8,128)S(1)}, f32[2,2,144,128]{3,2,1,0:T(8,128)S(1)}) custom-call(f32[1120,256]{1,0:T(8,128)S(1)} %bitcast.9, f32[1120,256]{1,0:T(8,128)S(1)} %bitcast.14, bf16[2,1120,256]{2,1,0:T(8,128)(2,1)S(1)} %bitcast.13), custom_call_target="tpu_custom_call" | custom-call | tf_op jit(solution)/shard_map/pallas_call | solution.py:493
  27.1 0.4 collective-permute-start.2
  27.5 0.3 collective-permute-start.10
  27.7 1.5 %collective-permute-done.6 = f32[2,72,256]{2,1,0:T(8,128)S(1)} collective-permute-done((f32[2,72,256]{2,1,0:T(8,128)S(1)}, f32[2,72,256]{2,1,0:T(8,128)S(1)}, u32[]{:S(2)}, u32[]{:S(2)}) %collective-permute-start.6) | collective-permute-done | bytes 147488 | tf_op jit(solution)/shard_map/ppermute | solution.py:626
  29.3 0.1 collective-permute-start.7
  29.4 1.4 %collective-permute-done.7.near_other_ref = f32[2,72,256]{2,1,0:T(8,128)S(1)} collective-permute-done((f32[2,72,256]{2,1,0:T(8,128)S(1)}, f32[2,72,256]{2,1,0:T(8,128)S(1)}, u32[]{:S(2)}, u32[]{:S(2)}) %collective-permute-start.7) | collective-permute-done | bytes 147488 | tf_op jit(solution)/shard_map/ppermute | solution.py:627
  30.8 1.2 %shard_map.110.refs_0_ = f32[4,40,256]{2,1,0:T(8,128)S(1)} custom-call(s32[8]{0:T(128)S(1)} %copy-done.6, f32[4,2,144,128]{3,2,1,0:T(8,128)S(1)} %collective-permute-done.8.halo_ref, f32[2,2,144,128]{3,2,1,0:T(8,128)S(1)} %get-tuple-element.53.mem_ref, f32[2,2,144,128]{3,2,1,0:T(8,128)S(1)} %collective-permute-done.9.mem_other_ref, ...), custom_call_target="tpu_custom_call" | custom-call | tf_op jit(solution)/shard_map/pallas_call | solution.py:493
  32.0 2.1 %collective-permute-start.11 = (f32[4,40,256]{2,1,0:T(8,128)S(1)}, f32[4,40,256]{2,1,0:T(8,128)S(1)}, u32[]{:S(2)}, u32[]{:S(2)}) collective-permute-start(f32[4,40,256]{2,1,0:T(8,128)S(1)} %shard_map.110.refs_0_), channel_id=1, source_target_pairs={{0,16},{8,24},{16,0},{24,8},{1,17},{9,25},{17,1},{25,9},{2,18},{10... | collective-permute-start | bytes 491528 | tf_op jit(solution)/shard_map/ppermute | solution.py:645
  34.1 2.9 %collective-permute-done.2 = f32[4,72,256]{2,1,0:T(8,128)S(1)} collective-permute-done((f32[4,72,256]{2,1,0:T(8,128)S(1)}, f32[4,72,256]{2,1,0:T(8,128)S(1)}, u32[]{:S(2)}, u32[]{:S(2)}) %collective-permute-start.2) | collective-permute-done | bytes 294944 | tf_op jit(solution)/shard_map/ppermute | solution.py:612
  37.0 0.1 collective-permute-start.3
  37.1 0.5 collective-permute-start.12
  37.6 2.5 %collective-permute-done.11.refs_1_ = f32[4,40,256]{2,1,0:T(8,128)S(1)} collective-permute-done((f32[4,40,256]{2,1,0:T(8,128)S(1)}, f32[4,40,256]{2,1,0:T(8,128)S(1)}, u32[]{:S(2)}, u32[]{:S(2)}) %collective-permute-start.11) | collective-permute-done | bytes 163872 | tf_op jit(solution)/shard_map/ppermute | solution.py:645
  40.8 1.1 %shard_map.109 = (f32[2,1120,128]{2,1,0:T(8,128)S(1)}, f32[8,128]{1,0:T(8,128)S(1)}) custom-call(f32[1]{0:T(128)S(6)} %copy.11.beta_ref, f32[4,72,256]{2,1,0:T(8,128)S(1)} %add.13.mine_ref, f32[4,72,256]{2,1,0:T(8,128)S(1)} %collective-permute-done.3.other_ref, f32[2,72,256]{2,1,0:T(8,128)S(1)} %add.15.near_mine_ref, ...), custom_call_target="tpu_custom_call" | custom-call | tf_op jit(solution)/shard_map/pallas_call | solution.py:493
  41.9 0.4 shard_map.111
  42.3 1.8 %collective-permute-start.14 = (f32[8,128]{1,0:T(8,128)S(1)}, f32[8,128]{1,0:T(8,128)S(1)}, u32[]{:S(2)}, u32[]{:S(2)}) collective-permute-start(f32[8,128]{1,0:T(8,128)S(1)} %get-tuple-element.57.refs_0_), channel_id=1, source_target_pairs={{0,1},{1,0},{2,3},{3,2},{4,5},{5,4},{6,7},{7,6},{8,9},{9,8},{10,11... | collective-permute-start | bytes 12296 | tf_op jit(solution)/shard_map/ppermute | solution.py:657
  44.0 1.9 %collective-permute-done.14.refs_1_ = f32[8,128]{1,0:T(8,128)S(1)} collective-permute-done((f32[8,128]{1,0:T(8,128)S(1)}, f32[8,128]{1,0:T(8,128)S(1)}, u32[]{:S(2)}, u32[]{:S(2)}) %collective-permute-start.14) | collective-permute-done | bytes 4128 | tf_op jit(solution)/shard_map/ppermute | solution.py:657
  45.9 3.8 %collective-permute-start.15 = (f32[8,128]{1,0:T(8,128)S(1)}, f32[8,128]{1,0:T(8,128)S(1)}, u32[]{:S(2)}, u32[]{:S(2)}) collective-permute-start(f32[8,128]{1,0:T(8,128)S(1)} %shard_map.112.refs_0_), channel_id=1, source_target_pairs={{0,4},{1,5},{2,6},{3,7},{4,0},{5,1},{6,2},{7,3},{8,12},{9,13},{10,... | collective-permute-start | bytes 12296 | tf_op jit(solution)/shard_map/ppermute | solution.py:657
  49.7 1.3 %collective-permute-start.16 = (f32[8,128]{1,0:T(8,128)S(1)}, f32[8,128]{1,0:T(8,128)S(1)}, u32[]{:S(2)}, u32[]{:S(2)}) collective-permute-start(f32[8,128]{1,0:T(8,128)S(1)} %shard_map.112.refs_0_), channel_id=1, source_target_pairs={{0,6},{1,7},{2,4},{3,5},{4,2},{5,3},{6,0},{7,1},{8,14},{9,15},{10,... | collective-permute-start | bytes 12296 | tf_op jit(solution)/shard_map/ppermute | solution.py:657
  51.0 0.2 collective-permute-start.17
  51.3 3.8 %collective-permute-done.16.refs_2_ = f32[8,128]{1,0:T(8,128)S(1)} collective-permute-done((f32[8,128]{1,0:T(8,128)S(1)}, f32[8,128]{1,0:T(8,128)S(1)}, u32[]{:S(2)}, u32[]{:S(2)}) %collective-permute-start.16) | collective-permute-done | bytes 4128 | tf_op jit(solution)/shard_map/ppermute | solution.py:657
  55.1 1.7 %shard_map.113 = (f32[1120,256]{1,0:T(8,128)}, f32[1,2]{1,0:T(1,128)}) custom-call(f32[8,128]{1,0:T(8,128)S(1)} %shard_map.112.refs_0_, f32[8,128]{1,0:T(8,128)S(1)} %collective-permute-done.15.refs_1_, f32[8,128]{1,0:T(8,128)S(1)} %collective-permute-done.16.refs_2_, f32[8,128]{1,0:T(8,128)S(1)} %collective-permute-done.17.refs_3_, ...), custom_call_target="tpu_custom_call" | custom-call | tf_op jit(solution)/shard_map/pallas_call | solution.py:493
  (35 shorter events, 0.4 us)
Async XLA Ops:
  0.6 5.5 %copy-start.2 = (bf16[256,256]{1,0:T(8,128)(2,1)S(1)}, bf16[256,256]{1,0:T(8,128)(2,1)}, u32[]{:S(2)}) copy-start(bf16[256,256]{1,0:T(8,128)(2,1)} %constant.6.clone.s_high_ref) | copy-start | bytes 393220
  0.6 5.5 %copy-start.3 = (bf16[256,256]{1,0:T(8,128)(2,1)S(1)}, bf16[256,256]{1,0:T(8,128)(2,1)}, u32[]{:S(2)}) copy-start(bf16[256,256]{1,0:T(8,128)(2,1)} %constant.7.clone.s_low_ref) | copy-start | bytes 393220
  0.7 5.5 %copy-start.1 = (bf16[2,70,16,256]{3,2,1,0:T(8,128)(2,1)S(1)}, bf16[2,70,16,256]{3,2,1,0:T(8,128)(2,1)}, u32[]{:S(2)}) copy-start(bf16[2,70,16,256]{3,2,1,0:T(8,128)(2,1)} %members_hbm.1) | copy-start | bytes 3440644
  0.7 5.5 %copy-start = (f32[70,16,256]{2,1,0:T(8,128)S(1)}, f32[70,16,256]{2,1,0:T(8,128)}, u32[]{:S(2)}) copy-start(f32[70,16,256]{2,1,0:T(8,128)} %inc_hbm.1) | copy-start | bytes 3440644
  0.7 5.5 %copy-start.7 = (s32[70]{0:T(128)S(1)}, s32[70]{0:T(128)}, u32[]{:S(2)}) copy-start(s32[70]{0:T(128)} %param.13) | copy-start | bytes 844
  3.1 16.2 %collective-permute-start.4 = (f32[2,2,280,128]{3,2,1,0:T(8,128)}, f32[2,2,280,128]{3,2,1,0:T(8,128)S(1)}, u32[]{:S(2)}, u32[]{:S(2)}) collective-permute-start(f32[2,2,280,128]{3,2,1,0:T(8,128)} %shard_map.104), channel_id=1, source_target_pairs={{0,1},{1,0},{2,3},{3,2},{4,5},{5,4},{6,7},{7,6},{8,9},{9,8},{10,11... | collective-permute-start | bytes 1720328 | tf_op jit(solution)/shard_map/ppermute | solution.py:572
  6.2 1.3 %copy-start.5 = (f32[8,256]{1,0:T(8,128)S(1)}, f32[8,256]{1,0:T(8,128)}, u32[]{:S(2)}) copy-start(f32[8,256]{1,0:T(8,128)} %constant.8.clone.waves_ref) | copy-start | bytes 24580
  6.2 1.3 %copy-start.6 = (s32[8]{0:T(128)S(1)}, s32[8]{0:T(128)}, u32[]{:S(2)}) copy-start(s32[8]{0:T(128)} %steps_ref.5) | copy-start | bytes 100
  7.4 8.0 %collective-permute-start = (f32[2,2,144,128]{3,2,1,0:T(8,128)S(1)}, f32[2,2,144,128]{3,2,1,0:T(8,128)S(1)}, u32[]{:S(2)}, u32[]{:S(2)}) collective-permute-start(f32[2,2,144,128]{3,2,1,0:T(8,128)S(1)} %get-tuple-element.37), channel_id=1, source_target_pairs={{0,8},{8,0},{16,24},{24,16},{1,9},{9,1},{17,25},{25,17},{2,10},{10... | collective-permute-start | bytes 884744 | tf_op jit(solution)/shard_map/ppermute | solution.py:582
  15.5 9.6 %copy-start.4 = (f32[70,16,256]{2,1,0:T(8,128)S(1)}, f32[70,16,256]{2,1,0:T(8,128)}, u32[]{:S(2)}) copy-start(f32[70,16,256]{2,1,0:T(8,128)} %param.10) | copy-start | bytes 3440644
  15.5 15.3 %collective-permute-start.8 = (f32[4,2,144,128]{3,2,1,0:T(8,128)S(1)}, f32[4,2,144,128]{3,2,1,0:T(8,128)S(1)}, u32[]{:S(2)}, u32[]{:S(2)}) collective-permute-start(f32[4,2,144,128]{3,2,1,0:T(8,128)S(1)} %pad_maximum_fusion), channel_id=1, source_target_pairs={{1,2},{2,1},{3,4},{4,3},{5,6},{6,5},{9,10},{10,9},{11,12},{12,11},... | collective-permute-start | bytes 1769480 | tf_op jit(solution)/shard_map/ppermute | solution.py:608
  16.3 10.7 %collective-permute-start.1 = (f32[4,72,256]{2,1,0:T(8,128)S(1)}, f32[4,72,256]{2,1,0:T(8,128)S(1)}, u32[]{:S(2)}, u32[]{:S(2)}) collective-permute-start(f32[4,72,256]{2,1,0:T(8,128)S(1)} %get-tuple-element.38), channel_id=1, source_target_pairs={{0,8},{8,0},{16,24},{24,16},{1,9},{9,1},{17,25},{25,17},{2,10},{10... | collective-permute-start | bytes 884744 | tf_op jit(solution)/shard_map/ppermute | solution.py:610
  21.9 1.4 %collective-permute-start.5 = (f32[2,72,256]{2,1,0:T(8,128)S(1)}, f32[2,72,256]{2,1,0:T(8,128)S(1)}, u32[]{:S(2)}, u32[]{:S(2)}) collective-permute-start(f32[2,72,256]{2,1,0:T(8,128)S(1)} %get-tuple-element.43), channel_id=1, source_target_pairs={{0,8},{8,0},{16,24},{24,16},{1,9},{9,1},{17,25},{25,17},{2,10},{10... | collective-permute-start | bytes 442376 | tf_op jit(solution)/shard_map/ppermute | solution.py:624
  23.3 6.0 %collective-permute-start.6 = (f32[2,72,256]{2,1,0:T(8,128)S(1)}, f32[2,72,256]{2,1,0:T(8,128)S(1)}, u32[]{:S(2)}, u32[]{:S(2)}) collective-permute-start(f32[2,72,256]{2,1,0:T(8,128)S(1)} %add.14), channel_id=1, source_target_pairs={{0,16},{8,24},{16,0},{24,8},{1,17},{9,25},{17,1},{25,9},{2,18},{10... | collective-permute-start | bytes 442376 | tf_op jit(solution)/shard_map/ppermute | solution.py:626
  27.0 3.8 %collective-permute-start.9 = (f32[2,2,144,128]{3,2,1,0:T(8,128)S(1)}, f32[2,2,144,128]{3,2,1,0:T(8,128)S(1)}, u32[]{:S(2)}, u32[]{:S(2)}) collective-permute-start(f32[2,2,144,128]{3,2,1,0:T(8,128)S(1)} %get-tuple-element.54), channel_id=1, source_target_pairs={{0,8},{8,0},{16,24},{24,16},{1,9},{9,1},{17,25},{25,17},{2,10},{10... | collective-permute-start | bytes 884744 | tf_op jit(solution)/shard_map/ppermute | solution.py:605
  27.1 9.9 %collective-permute-start.2 = (f32[4,72,256]{2,1,0:T(8,128)S(1)}, f32[4,72,256]{2,1,0:T(8,128)S(1)}, u32[]{:S(2)}, u32[]{:S(2)}) collective-permute-start(f32[4,72,256]{2,1,0:T(8,128)S(1)} %add.12), channel_id=1, source_target_pairs={{0,16},{8,24},{16,0},{24,8},{1,17},{9,25},{17,1},{25,9},{2,18},{10... | collective-permute-start | bytes 884744 | tf_op jit(solution)/shard_map/ppermute | solution.py:612
  27.5 3.3 %collective-permute-start.10 = (f32[4,40,256]{2,1,0:T(8,128)S(1)}, f32[4,40,256]{2,1,0:T(8,128)S(1)}, u32[]{:S(2)}, u32[]{:S(2)}) collective-permute-start(f32[4,40,256]{2,1,0:T(8,128)S(1)} %get-tuple-element.56), channel_id=1, source_target_pairs={{0,8},{8,0},{16,24},{24,16},{1,9},{9,1},{17,25},{25,17},{2,10},{10... | collective-permute-start | bytes 491528 | tf_op jit(solution)/shard_map/ppermute | solution.py:615
  29.3 1.4 %collective-permute-start.7 = (f32[2,72,256]{2,1,0:T(8,128)S(1)}, f32[2,72,256]{2,1,0:T(8,128)S(1)}, u32[]{:S(2)}, u32[]{:S(2)}) collective-permute-start(f32[2,72,256]{2,1,0:T(8,128)S(1)} %add.15.near_mine_ref), channel_id=1, source_target_pairs={{0,8},{8,0},{16,24},{24,16},{1,9},{9,1},{17,25},{25,17},{2,10},{10... | collective-permute-start | bytes 442376 | tf_op jit(solution)/shard_map/ppermute | solution.py:627
  32.0 8.1 %collective-permute-start.11 = (f32[4,40,256]{2,1,0:T(8,128)S(1)}, f32[4,40,256]{2,1,0:T(8,128)S(1)}, u32[]{:S(2)}, u32[]{:S(2)}) collective-permute-start(f32[4,40,256]{2,1,0:T(8,128)S(1)} %shard_map.110.refs_0_), channel_id=1, source_target_pairs={{0,16},{8,24},{16,0},{24,8},{1,17},{9,25},{17,1},{25,9},{2,18},{10... | collective-permute-start | bytes 491528 | tf_op jit(solution)/shard_map/ppermute | solution.py:645
  37.0 3.7 %collective-permute-start.3 = (f32[4,72,256]{2,1,0:T(8,128)S(1)}, f32[4,72,256]{2,1,0:T(8,128)S(1)}, u32[]{:S(2)}, u32[]{:S(2)}) collective-permute-start(f32[4,72,256]{2,1,0:T(8,128)S(1)} %add.13.mine_ref), channel_id=1, source_target_pairs={{0,8},{8,0},{16,24},{24,16},{1,9},{9,1},{17,25},{25,17},{2,10},{10... | collective-permute-start | bytes 884744 | tf_op jit(solution)/shard_map/ppermute | solution.py:613
  37.1 4.8 %collective-permute-start.12 = (f32[4,40,256]{2,1,0:T(8,128)S(1)}, f32[4,40,256]{2,1,0:T(8,128)S(1)}, u32[]{:S(2)}, u32[]{:S(2)}) collective-permute-start(f32[4,40,256]{2,1,0:T(8,128)S(1)} %shard_map.110.refs_0_), channel_id=1, source_target_pairs={{0,8},{8,0},{16,24},{24,16},{1,9},{9,1},{17,25},{25,17},{2,10},{10... | collective-permute-start | bytes 491528 | tf_op jit(solution)/shard_map/ppermute | solution.py:646
  40.1 1.8 %collective-permute-start.13 = (f32[4,40,256]{2,1,0:T(8,128)S(1)}, f32[4,40,256]{2,1,0:T(8,128)S(1)}, u32[]{:S(2)}, u32[]{:S(2)}) collective-permute-start(f32[4,40,256]{2,1,0:T(8,128)S(1)} %collective-permute-done.11.refs_1_), channel_id=1, source_target_pairs={{0,8},{8,0},{16,24},{24,16},{1,9},{9,1},{17,25},{25,17},{2,10},{10... | collective-permute-start | bytes 491528 | tf_op jit(solution)/shard_map/ppermute | solution.py:646
  42.3 3.7 %collective-permute-start.14 = (f32[8,128]{1,0:T(8,128)S(1)}, f32[8,128]{1,0:T(8,128)S(1)}, u32[]{:S(2)}, u32[]{:S(2)}) collective-permute-start(f32[8,128]{1,0:T(8,128)S(1)} %get-tuple-element.57.refs_0_), channel_id=1, source_target_pairs={{0,1},{1,0},{2,3},{3,2},{4,5},{5,4},{6,7},{7,6},{8,9},{9,8},{10,11... | collective-permute-start | bytes 12296 | tf_op jit(solution)/shard_map/ppermute | solution.py:657
  45.9 5.3 %collective-permute-start.15 = (f32[8,128]{1,0:T(8,128)S(1)}, f32[8,128]{1,0:T(8,128)S(1)}, u32[]{:S(2)}, u32[]{:S(2)}) collective-permute-start(f32[8,128]{1,0:T(8,128)S(1)} %shard_map.112.refs_0_), channel_id=1, source_target_pairs={{0,4},{1,5},{2,6},{3,7},{4,0},{5,1},{6,2},{7,3},{8,12},{9,13},{10,... | collective-permute-start | bytes 12296 | tf_op jit(solution)/shard_map/ppermute | solution.py:657
  49.7 5.4 %collective-permute-start.16 = (f32[8,128]{1,0:T(8,128)S(1)}, f32[8,128]{1,0:T(8,128)S(1)}, u32[]{:S(2)}, u32[]{:S(2)}) collective-permute-start(f32[8,128]{1,0:T(8,128)S(1)} %shard_map.112.refs_0_), channel_id=1, source_target_pairs={{0,6},{1,7},{2,4},{3,5},{4,2},{5,3},{6,0},{7,1},{8,14},{9,15},{10,... | collective-permute-start | bytes 12296 | tf_op jit(solution)/shard_map/ppermute | solution.py:657
  51.0 4.1 %collective-permute-start.17 = (f32[8,128]{1,0:T(8,128)S(1)}, f32[8,128]{1,0:T(8,128)S(1)}, u32[]{:S(2)}, u32[]{:S(2)}) collective-permute-start(f32[8,128]{1,0:T(8,128)S(1)} %shard_map.112.refs_0_), channel_id=1, source_target_pairs={{0,2},{1,3},{2,0},{3,1},{4,6},{5,7},{6,4},{7,5},{8,10},{9,11},{10,... | collective-permute-start | bytes 12296 | tf_op jit(solution)/shard_map/ppermute | solution.py:657

commit v9 on v8

--- a/solution.py
+++ b/solution.py
@@ -13,7 +13,7 @@
 RATE = 0.24
 F32 = jnp.float32
 VMEM_LIMIT = 32 * 1024 * 1024
-EDGE_LIMIT = 60 * 1024 * 1024
+EDGE_LIMIT = 53 * 1024 * 1024
 
 
 def up_to(value, unit):

time: 57.1 us -> 56.3 us (0.986)
  Pallas kernels: 20.3 us -> 19.5 us
    pallas_call x10, Pallas kernels: 20.3 us -> 19.5 us  [call(): pl.pallas_call(kernel, out_shape=tuple((jax.ShapeDtypeStruct(shape, F32)...]
where the time goes in v9:
time: 56.3 us; the launch traced here: 56.2 us
  Pallas kernels  19.5 us (35%)
  waiting for transfers between devices  17.6 us (31%)
  starting transfers between devices  17.1 us (30%)
  between operations  1.72 us (3%)
    pallas_call x10, Pallas kernels, call(): pl.pallas_call(kernel, out_shape=tuple((jax.ShapeDtypeStruct(shape, F32)...  19.5 us
    ppermute x4, starting transfers between devices, per_device(): lax.ppermute(sums, 'tile', rotated('tile', digit, radix, by))  7.34 us
    ppermute x4, waiting for transfers between devices, per_device(): lax.ppermute(sums, 'tile', rotated('tile', digit, radix, by))  5.69 us
    ppermute x1, starting transfers between devices, per_device(): near_halo = lax.ppermute(near_edge, 'tile', near_pairs)  3.03 us
    ppermute x1, waiting for transfers between devices, per_device(): mine = mine + lax.ppermute(mine, 'mem', flipped('mem', bit))  2.88 us
    ppermute x1, waiting for transfers between devices, per_device(): far_sums = [cov, lax.ppermute(cov, 'mem', flipped('mem', bits[-1]))]  2.48 us
    ppermute x1, waiting for transfers between devices, per_device(): near_halo = lax.ppermute(near_edge, 'tile', near_pairs)  2.28 us
    ppermute x1, starting transfers between devices, per_device(): far_sums = [cov, lax.ppermute(cov, 'mem', flipped('mem', bits[-1]))]  2.14 us
  transfers between devices with their start and end apart: 18, of which 8 were waited for; matrix products, arithmetic and copies ran while one was open for 0% of the time, Pallas kernels for 28%

profile of v9, /device:TPU:0, one launch (start us, length us, event | category | flops | bytes accessed | tf_op | source)
XLA Modules:
  0.0 56.2 jit_solution(1213310674588508336)
XLA Ops:
  0.7 1.6 %shard_map.104 = f32[2,2,280,128]{3,2,1,0:T(8,128)S(1)} custom-call(bf16[2,70,16,256]{3,2,1,0:T(8,128)(2,1)} %members_hbm.1, f32[70,16,256]{2,1,0:T(8,128)} %inc_hbm.1), custom_call_target="tpu_custom_call" | custom-call | tf_op jit(solution)/shard_map/pallas_call | solution.py:493
  2.3 3.0 %collective-permute-start.4 = (f32[2,2,280,128]{3,2,1,0:T(8,128)S(1)}, f32[2,2,280,128]{3,2,1,0:T(8,128)S(1)}, u32[]{:S(2)}, u32[]{:S(2)}) collective-permute-start(f32[2,2,280,128]{3,2,1,0:T(8,128)S(1)} %shard_map.104), channel_id=1, source_target_pairs={{0,1},{1,0},{2,3},{3,2},{4,5},{5,4},{6,7},{7,6},{8,9},{9,8},{10,11... | collective-permute-start | bytes 1720328 | tf_op jit(solution)/shard_map/ppermute | solution.py:572
  5.4 1.2 %shard_map.105 = (f32[2,2,144,128]{3,2,1,0:T(8,128)S(1)}, f32[2,2,144,128]{3,2,1,0:T(8,128)S(1)}) custom-call(s32[1,70]{1,0:T(1,128)S(1)} %bitcast.15, bf16[2,1120,256]{2,1,0:T(8,128)(2,1)S(1)} %bitcast.11, f32[1120,256]{1,0:T(8,128)S(1)} %bitcast.7, bf16[256,256]{1,0:T(8,128)(2,1)S(1)} %copy-done.2, bf16[256,256]{1,0:T(8,128)(2,1)S(1)} %copy-done.3), custom_call_target="tpu_custom_call" | custom-call | tf_op jit(solution)/shard_map/pallas_call | solution.py:493
  6.6 0.1 collective-permute-start
  6.7 7.9 %shard_map.106 = (f32[4,72,256]{2,1,0:T(8,128)S(1)}, f32[4,72,256]{2,1,0:T(8,128)S(1)}, f32[4,72,256]{2,1,0:T(8,128)S(1)}, f32[4,40,256]{2,1,0:T(8,128)S(1)}, f3...) custom-call(s32[1,70]{1,0:T(1,128)S(1)} %bitcast.16, s32[8]{0:T(128)S(1)} %copy-done.6, ...), custom_call_target="tpu_custom_call" | custom-call | flops 20000000 | bytes 1000000 | tf_op jit(solution)/shard_map/pallas_call | solution.py:493
  14.7 0.8 %collective-permute-start.8 = (f32[4,2,144,128]{3,2,1,0:T(8,128)S(1)}, f32[4,2,144,128]{3,2,1,0:T(8,128)S(1)}, u32[]{:S(2)}, u32[]{:S(2)}) collective-permute-start(f32[4,2,144,128]{3,2,1,0:T(8,128)S(1)} %pad_maximum_fusion), channel_id=1, source_target_pairs={{1,2},{2,1},{3,4},{4,3},{5,6},{6,5},{9,10},{10,9},{11,12},{12,11},... | collective-permute-start | bytes 1769480 | tf_op jit(solution)/shard_map/ppermute | solution.py:608
  15.5 0.5 collective-permute-start.1
  16.1 2.3 %collective-permute-done.4.halo_ref = f32[2,2,280,128]{3,2,1,0:T(8,128)S(1)} collective-permute-done((f32[2,2,280,128]{3,2,1,0:T(8,128)S(1)}, f32[2,2,280,128]{3,2,1,0:T(8,128)S(1)}, u32[]{:S(2)}, u32[]{:S(2)}) %collective-permute-start.4) | collective-permute-done | bytes 573472 | tf_op jit(solution)/shard_map/ppermute | solution.py:572
  18.3 2.5 %shard_map.107 = (f32[2,72,256]{2,1,0:T(8,128)S(1)}, f32[2,72,256]{2,1,0:T(8,128)S(1)}) custom-call(s32[1,70]{1,0:T(1,128)S(1)} %bitcast.17, s32[8]{0:T(128)S(1)} %copy-done.6, f32[2,2,280,128]{3,2,1,0:T(8,128)S(1)} %collective-permute-done.4.halo_ref, f32[2,4,72,256]{3,2,1,0:T(8,128)S(1)} %get-tuple-element.40.mem_ref, ...), custom_call_target="tpu_custom_call" | custom-call | tf_op jit(solution)/shard_map/pallas_call | solution.py:493
  20.9 0.1 collective-permute-start.5
  20.9 1.4 %collective-permute-done.5 = f32[2,72,256]{2,1,0:T(8,128)S(1)} collective-permute-done((f32[2,72,256]{2,1,0:T(8,128)S(1)}, f32[2,72,256]{2,1,0:T(8,128)S(1)}, u32[]{:S(2)}, u32[]{:S(2)}) %collective-permute-start.5) | collective-permute-done | bytes 147488 | tf_op jit(solution)/shard_map/ppermute | solution.py:624
  22.3 1.8 %collective-permute-start.6 = (f32[2,72,256]{2,1,0:T(8,128)S(1)}, f32[2,72,256]{2,1,0:T(8,128)S(1)}, u32[]{:S(2)}, u32[]{:S(2)}) collective-permute-start(f32[2,72,256]{2,1,0:T(8,128)S(1)} %add.14), channel_id=1, source_target_pairs={{0,16},{8,24},{16,0},{24,8},{1,17},{9,25},{17,1},{25,9},{2,18},{10... | collective-permute-start | bytes 442376 | tf_op jit(solution)/shard_map/ppermute | solution.py:626
  24.1 1.9 %shard_map.108 = (f32[16,72,256]{2,1,0:T(8,128)S(1)}, f32[16,72,256]{2,1,0:T(8,128)S(1)}, f32[2,2,144,128]{3,2,1,0:T(8,128)S(1)}, f32[2,2,144,128]{3,2,1,0:T(8,128)S(1)}) custom-call(f32[1120,256]{1,0:T(8,128)S(1)} %bitcast.9, f32[1120,256]{1,0:T(8,128)S(1)} %bitcast.14, bf16[2,1120,256]{2,1,0:T(8,128)(2,1)S(1)} %bitcast.13), custom_call_target="tpu_custom_call" | custom-call | tf_op jit(solution)/shard_map/pallas_call | solution.py:493
  26.0 0.1 collective-permute-start.9
  26.1 0.4 collective-permute-start.2
  26.5 0.2 collective-permute-start.10
  26.7 1.5 %collective-permute-done.6 = f32[2,72,256]{2,1,0:T(8,128)S(1)} collective-permute-done((f32[2,72,256]{2,1,0:T(8,128)S(1)}, f32[2,72,256]{2,1,0:T(8,128)S(1)}, u32[]{:S(2)}, u32[]{:S(2)}) %collective-permute-start.6) | collective-permute-done | bytes 147488 | tf_op jit(solution)/shard_map/ppermute | solution.py:626
  28.4 1.4 %collective-permute-done.7.near_other_ref = f32[2,72,256]{2,1,0:T(8,128)S(1)} collective-permute-done((f32[2,72,256]{2,1,0:T(8,128)S(1)}, f32[2,72,256]{2,1,0:T(8,128)S(1)}, u32[]{:S(2)}, u32[]{:S(2)}) %collective-permute-start.7) | collective-permute-done | bytes 147488 | tf_op jit(solution)/shard_map/ppermute | solution.py:627
  29.7 1.2 %shard_map.110.refs_0_ = f32[4,40,256]{2,1,0:T(8,128)S(1)} custom-call(s32[8]{0:T(128)S(1)} %copy-done.6, f32[4,2,144,128]{3,2,1,0:T(8,128)S(1)} %collective-permute-done.8.halo_ref, f32[2,2,144,128]{3,2,1,0:T(8,128)S(1)} %get-tuple-element.53.mem_ref, f32[2,2,144,128]{3,2,1,0:T(8,128)S(1)} %collective-permute-done.9.mem_other_ref, ...), custom_call_target="tpu_custom_call" | custom-call | tf_op jit(solution)/shard_map/pallas_call | solution.py:493
  30.9 2.1 %collective-permute-start.11 = (f32[4,40,256]{2,1,0:T(8,128)S(1)}, f32[4,40,256]{2,1,0:T(8,128)S(1)}, u32[]{:S(2)}, u32[]{:S(2)}) collective-permute-start(f32[4,40,256]{2,1,0:T(8,128)S(1)} %shard_map.110.refs_0_), channel_id=1, source_target_pairs={{0,16},{8,24},{16,0},{24,8},{1,17},{9,25},{17,1},{25,9},{2,18},{10... | collective-permute-start | bytes 491528 | tf_op jit(solution)/shard_map/ppermute | solution.py:645
  33.1 2.9 %collective-permute-done.2 = f32[4,72,256]{2,1,0:T(8,128)S(1)} collective-permute-done((f32[4,72,256]{2,1,0:T(8,128)S(1)}, f32[4,72,256]{2,1,0:T(8,128)S(1)}, u32[]{:S(2)}, u32[]{:S(2)}) %collective-permute-start.2) | collective-permute-done | bytes 294944 | tf_op jit(solution)/shard_map/ppermute | solution.py:612
  36.1 0.5 collective-permute-start.12
  36.6 2.5 %collective-permute-done.11.refs_1_ = f32[4,40,256]{2,1,0:T(8,128)S(1)} collective-permute-done((f32[4,40,256]{2,1,0:T(8,128)S(1)}, f32[4,40,256]{2,1,0:T(8,128)S(1)}, u32[]{:S(2)}, u32[]{:S(2)}) %collective-permute-start.11) | collective-permute-done | bytes 163872 | tf_op jit(solution)/shard_map/ppermute | solution.py:645
  39.7 1.1 %shard_map.109 = (f32[2,1120,128]{2,1,0:T(8,128)S(1)}, f32[8,128]{1,0:T(8,128)S(1)}) custom-call(f32[1]{0:T(128)S(6)} %copy.11.beta_ref, f32[4,72,256]{2,1,0:T(8,128)S(1)} %add.13.mine_ref, f32[4,72,256]{2,1,0:T(8,128)S(1)} %collective-permute-done.3.other_ref, f32[2,72,256]{2,1,0:T(8,128)S(1)} %add.15.near_mine_ref, ...), custom_call_target="tpu_custom_call" | custom-call | tf_op jit(solution)/shard_map/pallas_call | solution.py:493
  40.9 0.4 shard_map.111
  41.2 1.8 %collective-permute-start.14 = (f32[8,128]{1,0:T(8,128)S(1)}, f32[8,128]{1,0:T(8,128)S(1)}, u32[]{:S(2)}, u32[]{:S(2)}) collective-permute-start(f32[8,128]{1,0:T(8,128)S(1)} %get-tuple-element.57.refs_0_), channel_id=1, source_target_pairs={{0,1},{1,0},{2,3},{3,2},{4,5},{5,4},{6,7},{7,6},{8,9},{9,8},{10,11... | collective-permute-start | bytes 12296 | tf_op jit(solution)/shard_map/ppermute | solution.py:657
  43.0 1.9 %collective-permute-done.14.refs_1_ = f32[8,128]{1,0:T(8,128)S(1)} collective-permute-done((f32[8,128]{1,0:T(8,128)S(1)}, f32[8,128]{1,0:T(8,128)S(1)}, u32[]{:S(2)}, u32[]{:S(2)}) %collective-permute-start.14) | collective-permute-done | bytes 4128 | tf_op jit(solution)/shard_map/ppermute | solution.py:657
  44.9 4.0 %collective-permute-start.15 = (f32[8,128]{1,0:T(8,128)S(1)}, f32[8,128]{1,0:T(8,128)S(1)}, u32[]{:S(2)}, u32[]{:S(2)}) collective-permute-start(f32[8,128]{1,0:T(8,128)S(1)} %shard_map.112.refs_0_), channel_id=1, source_target_pairs={{0,4},{1,5},{2,6},{3,7},{4,0},{5,1},{6,2},{7,3},{8,12},{9,13},{10,... | collective-permute-start | bytes 12296 | tf_op jit(solution)/shard_map/ppermute | solution.py:657
  48.9 1.3 %collective-permute-start.16 = (f32[8,128]{1,0:T(8,128)S(1)}, f32[8,128]{1,0:T(8,128)S(1)}, u32[]{:S(2)}, u32[]{:S(2)}) collective-permute-start(f32[8,128]{1,0:T(8,128)S(1)} %shard_map.112.refs_0_), channel_id=1, source_target_pairs={{0,6},{1,7},{2,4},{3,5},{4,2},{5,3},{6,0},{7,1},{8,14},{9,15},{10,... | collective-permute-start | bytes 12296 | tf_op jit(solution)/shard_map/ppermute | solution.py:657
  50.2 0.2 collective-permute-start.17
  50.5 3.8 %collective-permute-done.16.refs_2_ = f32[8,128]{1,0:T(8,128)S(1)} collective-permute-done((f32[8,128]{1,0:T(8,128)S(1)}, f32[8,128]{1,0:T(8,128)S(1)}, u32[]{:S(2)}, u32[]{:S(2)}) %collective-permute-start.16) | collective-permute-done | bytes 4128 | tf_op jit(solution)/shard_map/ppermute | solution.py:657
  54.3 1.7 %shard_map.113 = (f32[1120,256]{1,0:T(8,128)}, f32[1,2]{1,0:T(1,128)}) custom-call(f32[8,128]{1,0:T(8,128)S(1)} %shard_map.112.refs_0_, f32[8,128]{1,0:T(8,128)S(1)} %collective-permute-done.15.refs_1_, f32[8,128]{1,0:T(8,128)S(1)} %collective-permute-done.16.refs_2_, f32[8,128]{1,0:T(8,128)S(1)} %collective-permute-done.17.refs_3_, ...), custom_call_target="tpu_custom_call" | custom-call | tf_op jit(solution)/shard_map/pallas_call | solution.py:493
  (35 shorter events, 0.4 us)
Async XLA Ops:
  0.6 4.7 %copy-start.2 = (bf16[256,256]{1,0:T(8,128)(2,1)S(1)}, bf16[256,256]{1,0:T(8,128)(2,1)}, u32[]{:S(2)}) copy-start(bf16[256,256]{1,0:T(8,128)(2,1)} %constant.6.clone.s_high_ref) | copy-start | bytes 393220
  0.6 4.7 %copy-start.3 = (bf16[256,256]{1,0:T(8,128)(2,1)S(1)}, bf16[256,256]{1,0:T(8,128)(2,1)}, u32[]{:S(2)}) copy-start(bf16[256,256]{1,0:T(8,128)(2,1)} %constant.7.clone.s_low_ref) | copy-start | bytes 393220
  0.7 4.7 %copy-start.1 = (bf16[2,70,16,256]{3,2,1,0:T(8,128)(2,1)S(1)}, bf16[2,70,16,256]{3,2,1,0:T(8,128)(2,1)}, u32[]{:S(2)}) copy-start(bf16[2,70,16,256]{3,2,1,0:T(8,128)(2,1)} %members_hbm.1) | copy-start | bytes 3440644
  0.7 4.7 %copy-start = (f32[70,16,256]{2,1,0:T(8,128)S(1)}, f32[70,16,256]{2,1,0:T(8,128)}, u32[]{:S(2)}) copy-start(f32[70,16,256]{2,1,0:T(8,128)} %inc_hbm.1) | copy-start | bytes 3440644
  0.7 4.7 %copy-start.7 = (s32[70]{0:T(128)S(1)}, s32[70]{0:T(128)}, u32[]{:S(2)}) copy-start(s32[70]{0:T(128)} %param.13) | copy-start | bytes 844
  2.3 16.0 %collective-permute-start.4 = (f32[2,2,280,128]{3,2,1,0:T(8,128)S(1)}, f32[2,2,280,128]{3,2,1,0:T(8,128)S(1)}, u32[]{:S(2)}, u32[]{:S(2)}) collective-permute-start(f32[2,2,280,128]{3,2,1,0:T(8,128)S(1)} %shard_map.104), channel_id=1, source_target_pairs={{0,1},{1,0},{2,3},{3,2},{4,5},{5,4},{6,7},{7,6},{8,9},{9,8},{10,11... | collective-permute-start | bytes 1720328 | tf_op jit(solution)/shard_map/ppermute | solution.py:572
  5.4 1.3 %copy-start.5 = (f32[8,256]{1,0:T(8,128)S(1)}, f32[8,256]{1,0:T(8,128)}, u32[]{:S(2)}) copy-start(f32[8,256]{1,0:T(8,128)} %constant.8.clone.waves_ref) | copy-start | bytes 24580
  5.4 1.3 %copy-start.6 = (s32[8]{0:T(128)S(1)}, s32[8]{0:T(128)}, u32[]{:S(2)}) copy-start(s32[8]{0:T(128)} %steps_ref.5) | copy-start | bytes 100
  6.6 8.0 %collective-permute-start = (f32[2,2,144,128]{3,2,1,0:T(8,128)S(1)}, f32[2,2,144,128]{3,2,1,0:T(8,128)S(1)}, u32[]{:S(2)}, u32[]{:S(2)}) collective-permute-start(f32[2,2,144,128]{3,2,1,0:T(8,128)S(1)} %get-tuple-element.37), channel_id=1, source_target_pairs={{0,8},{8,0},{16,24},{24,16},{1,9},{9,1},{17,25},{25,17},{2,10},{10... | collective-permute-start | bytes 884744 | tf_op jit(solution)/shard_map/ppermute | solution.py:582
  14.7 9.4 %copy-start.4 = (f32[70,16,256]{2,1,0:T(8,128)S(1)}, f32[70,16,256]{2,1,0:T(8,128)}, u32[]{:S(2)}) copy-start(f32[70,16,256]{2,1,0:T(8,128)} %param.10) | copy-start | bytes 3440644
  14.7 15.1 %collective-permute-start.8 = (f32[4,2,144,128]{3,2,1,0:T(8,128)S(1)}, f32[4,2,144,128]{3,2,1,0:T(8,128)S(1)}, u32[]{:S(2)}, u32[]{:S(2)}) collective-permute-start(f32[4,2,144,128]{3,2,1,0:T(8,128)S(1)} %pad_maximum_fusion), channel_id=1, source_target_pairs={{1,2},{2,1},{3,4},{4,3},{5,6},{6,5},{9,10},{10,9},{11,12},{12,11},... | collective-permute-start | bytes 1769480 | tf_op jit(solution)/shard_map/ppermute | solution.py:608
  15.5 10.5 %collective-permute-start.1 = (f32[4,72,256]{2,1,0:T(8,128)S(1)}, f32[4,72,256]{2,1,0:T(8,128)S(1)}, u32[]{:S(2)}, u32[]{:S(2)}) collective-permute-start(f32[4,72,256]{2,1,0:T(8,128)S(1)} %get-tuple-element.38), channel_id=1, source_target_pairs={{0,8},{8,0},{16,24},{24,16},{1,9},{9,1},{17,25},{25,17},{2,10},{10... | collective-permute-start | bytes 884744 | tf_op jit(solution)/shard_map/ppermute | solution.py:610
  20.9 1.4 %collective-permute-start.5 = (f32[2,72,256]{2,1,0:T(8,128)S(1)}, f32[2,72,256]{2,1,0:T(8,128)S(1)}, u32[]{:S(2)}, u32[]{:S(2)}) collective-permute-start(f32[2,72,256]{2,1,0:T(8,128)S(1)} %get-tuple-element.43), channel_id=1, source_target_pairs={{0,8},{8,0},{16,24},{24,16},{1,9},{9,1},{17,25},{25,17},{2,10},{10... | collective-permute-start | bytes 442376 | tf_op jit(solution)/shard_map/ppermute | solution.py:624
  22.3 6.0 %collective-permute-start.6 = (f32[2,72,256]{2,1,0:T(8,128)S(1)}, f32[2,72,256]{2,1,0:T(8,128)S(1)}, u32[]{:S(2)}, u32[]{:S(2)}) collective-permute-start(f32[2,72,256]{2,1,0:T(8,128)S(1)} %add.14), channel_id=1, source_target_pairs={{0,16},{8,24},{16,0},{24,8},{1,17},{9,25},{17,1},{25,9},{2,18},{10... | collective-permute-start | bytes 442376 | tf_op jit(solution)/shard_map/ppermute | solution.py:626
  26.0 3.8 %collective-permute-start.9 = (f32[2,2,144,128]{3,2,1,0:T(8,128)S(1)}, f32[2,2,144,128]{3,2,1,0:T(8,128)S(1)}, u32[]{:S(2)}, u32[]{:S(2)}) collective-permute-start(f32[2,2,144,128]{3,2,1,0:T(8,128)S(1)} %get-tuple-element.54), channel_id=1, source_target_pairs={{0,8},{8,0},{16,24},{24,16},{1,9},{9,1},{17,25},{25,17},{2,10},{10... | collective-permute-start | bytes 884744 | tf_op jit(solution)/shard_map/ppermute | solution.py:605
  26.1 9.9 %collective-permute-start.2 = (f32[4,72,256]{2,1,0:T(8,128)S(1)}, f32[4,72,256]{2,1,0:T(8,128)S(1)}, u32[]{:S(2)}, u32[]{:S(2)}) collective-permute-start(f32[4,72,256]{2,1,0:T(8,128)S(1)} %add.12), channel_id=1, source_target_pairs={{0,16},{8,24},{16,0},{24,8},{1,17},{9,25},{17,1},{25,9},{2,18},{10... | collective-permute-start | bytes 884744 | tf_op jit(solution)/shard_map/ppermute | solution.py:612
  26.5 3.3 %collective-permute-start.10 = (f32[4,40,256]{2,1,0:T(8,128)S(1)}, f32[4,40,256]{2,1,0:T(8,128)S(1)}, u32[]{:S(2)}, u32[]{:S(2)}) collective-permute-start(f32[4,40,256]{2,1,0:T(8,128)S(1)} %get-tuple-element.56), channel_id=1, source_target_pairs={{0,8},{8,0},{16,24},{24,16},{1,9},{9,1},{17,25},{25,17},{2,10},{10... | collective-permute-start | bytes 491528 | tf_op jit(solution)/shard_map/ppermute | solution.py:615
  28.3 1.4 %collective-permute-start.7 = (f32[2,72,256]{2,1,0:T(8,128)S(1)}, f32[2,72,256]{2,1,0:T(8,128)S(1)}, u32[]{:S(2)}, u32[]{:S(2)}) collective-permute-start(f32[2,72,256]{2,1,0:T(8,128)S(1)} %add.15.near_mine_ref), channel_id=1, source_target_pairs={{0,8},{8,0},{16,24},{24,16},{1,9},{9,1},{17,25},{25,17},{2,10},{10... | collective-permute-start | bytes 442376 | tf_op jit(solution)/shard_map/ppermute | solution.py:627
  30.9 8.1 %collective-permute-start.11 = (f32[4,40,256]{2,1,0:T(8,128)S(1)}, f32[4,40,256]{2,1,0:T(8,128)S(1)}, u32[]{:S(2)}, u32[]{:S(2)}) collective-permute-start(f32[4,40,256]{2,1,0:T(8,128)S(1)} %shard_map.110.refs_0_), channel_id=1, source_target_pairs={{0,16},{8,24},{16,0},{24,8},{1,17},{9,25},{17,1},{25,9},{2,18},{10... | collective-permute-start | bytes 491528 | tf_op jit(solution)/shard_map/ppermute | solution.py:645
  36.0 3.7 %collective-permute-start.3 = (f32[4,72,256]{2,1,0:T(8,128)S(1)}, f32[4,72,256]{2,1,0:T(8,128)S(1)}, u32[]{:S(2)}, u32[]{:S(2)}) collective-permute-start(f32[4,72,256]{2,1,0:T(8,128)S(1)} %add.13.mine_ref), channel_id=1, source_target_pairs={{0,8},{8,0},{16,24},{24,16},{1,9},{9,1},{17,25},{25,17},{2,10},{10... | collective-permute-start | bytes 884744 | tf_op jit(solution)/shard_map/ppermute | solution.py:613
  36.1 4.8 %collective-permute-start.12 = (f32[4,40,256]{2,1,0:T(8,128)S(1)}, f32[4,40,256]{2,1,0:T(8,128)S(1)}, u32[]{:S(2)}, u32[]{:S(2)}) collective-permute-start(f32[4,40,256]{2,1,0:T(8,128)S(1)} %shard_map.110.refs_0_), channel_id=1, source_target_pairs={{0,8},{8,0},{16,24},{24,16},{1,9},{9,1},{17,25},{25,17},{2,10},{10... | collective-permute-start | bytes 491528 | tf_op jit(solution)/shard_map/ppermute | solution.py:646
  39.1 1.8 %collective-permute-start.13 = (f32[4,40,256]{2,1,0:T(8,128)S(1)}, f32[4,40,256]{2,1,0:T(8,128)S(1)}, u32[]{:S(2)}, u32[]{:S(2)}) collective-permute-start(f32[4,40,256]{2,1,0:T(8,128)S(1)} %collective-permute-done.11.refs_1_), channel_id=1, source_target_pairs={{0,8},{8,0},{16,24},{24,16},{1,9},{9,1},{17,25},{25,17},{2,10},{10... | collective-permute-start | bytes 491528 | tf_op jit(solution)/shard_map/ppermute | solution.py:646
  41.2 3.7 %collective-permute-start.14 = (f32[8,128]{1,0:T(8,128)S(1)}, f32[8,128]{1,0:T(8,128)S(1)}, u32[]{:S(2)}, u32[]{:S(2)}) collective-permute-start(f32[8,128]{1,0:T(8,128)S(1)} %get-tuple-element.57.refs_0_), channel_id=1, source_target_pairs={{0,1},{1,0},{2,3},{3,2},{4,5},{5,4},{6,7},{7,6},{8,9},{9,8},{10,11... | collective-permute-start | bytes 12296 | tf_op jit(solution)/shard_map/ppermute | solution.py:657
  44.9 5.5 %collective-permute-start.15 = (f32[8,128]{1,0:T(8,128)S(1)}, f32[8,128]{1,0:T(8,128)S(1)}, u32[]{:S(2)}, u32[]{:S(2)}) collective-permute-start(f32[8,128]{1,0:T(8,128)S(1)} %shard_map.112.refs_0_), channel_id=1, source_target_pairs={{0,4},{1,5},{2,6},{3,7},{4,0},{5,1},{6,2},{7,3},{8,12},{9,13},{10,... | collective-permute-start | bytes 12296 | tf_op jit(solution)/shard_map/ppermute | solution.py:657
  48.9 5.4 %collective-permute-start.16 = (f32[8,128]{1,0:T(8,128)S(1)}, f32[8,128]{1,0:T(8,128)S(1)}, u32[]{:S(2)}, u32[]{:S(2)}) collective-permute-start(f32[8,128]{1,0:T(8,128)S(1)} %shard_map.112.refs_0_), channel_id=1, source_target_pairs={{0,6},{1,7},{2,4},{3,5},{4,2},{5,3},{6,0},{7,1},{8,14},{9,15},{10,... | collective-permute-start | bytes 12296 | tf_op jit(solution)/shard_map/ppermute | solution.py:657
  50.2 4.1 %collective-permute-start.17 = (f32[8,128]{1,0:T(8,128)S(1)}, f32[8,128]{1,0:T(8,128)S(1)}, u32[]{:S(2)}, u32[]{:S(2)}) collective-permute-start(f32[8,128]{1,0:T(8,128)S(1)} %shard_map.112.refs_0_), channel_id=1, source_target_pairs={{0,2},{1,3},{2,0},{3,1},{4,6},{5,7},{6,4},{7,5},{8,10},{9,11},{10,... | collective-permute-start | bytes 12296 | tf_op jit(solution)/shard_map/ppermute | solution.py:657
